TPU v7x, 512 devices: a whole 4x4x16 slice. The times are simulated.
512 devices in a mesh: ctx: 32 (over x, y, core), head: 16 (over z).
Axes of the slice: x: 4, y: 4, z: 16, core: 2. Of those that a mesh axis runs over, the one named last changes fastest.
Arguments:
- x_in: bfloat16 [49152, 8192], P(('ctx', 'head')), may hold values from -6 to 6
- dt_raw: bfloat16 [49152, 128], P(('ctx', 'head')), may hold values from -3 to 3
- bc_in: bfloat16 [49152, 256], P(('ctx', 'head')), may hold values from -6 to 6
- z_in: bfloat16 [49152, 8192], P(('ctx', 'head')), may hold values from -6 to 6
- conv_x: float32 [4, 8192], P(None, 'head'), may hold values from -3 to 3
- bias_x: float32 [8192], P('head'), may hold values from -3 to 3
- conv_bc: float32 [4, 256], replicated, may hold values from -3 to 3
- bias_bc: float32 [256], replicated, may hold values from -3 to 3
- dt_bias: float32 [128], P('head'), may hold values from -0.5 to 0.5
- a_log: float32 [128], P('head'), may hold values from -16 to -2
- d_skip: float32 [128], P('head'), may hold values from 0.5 to 1.5
- norm_gain: float32 [8192], replicated, may hold values from 0.5 to 1.5
Outputs:
- mixed: bfloat16 [49152, 8192], P(('ctx', 'head'))
All inputs are finite; a program needn't handle non-finite values.
Results may differ from a plain program's by a relative error of at most 0.0015.
The roundings to bfloat16 on the way count: a program that leaves them out, or rounds other values in their place, can miss the bound.
Values may be sent and summed in bfloat16 or wider, within the bound.
No kernel may reach another device: no remote copies, remote signals or barrier semaphores. Data moves between devices by JAX's collectives and lax.ppermute only.
A program may use at most 64 MiB of HBM per device.

v0:
```python
import jax
import jax.numpy as jnp
from jax import lax
from jax.sharding import PartitionSpec as P

BLOCK = 256


def from_behind(value, axis, by):
    count = lax.axis_size(axis)
    pairs = [(i, i + by) for i in range(count) if 0 <= i + by < count]
    return lax.ppermute(value, axis, pairs)


def entering(value, axis, combine, identity):
    count, place = (lax.axis_size(axis), lax.axis_index(axis))
    everything = jax.tree.map(lambda part: lax.all_gather(part, axis), value)
    start = jax.tree.map(
        lambda part, zero: jnp.broadcast_to(jnp.asarray(zero, part.dtype), part.shape),
        value,
        identity,
    )

    def step(k, before):
        reached = k < place
        new = combine(before, jax.tree.map(lambda part: part[k], everything))
        return jax.tree.map(lambda a, b: jnp.where(reached, a, b), new, before)

    return lax.fori_loop(0, count, step, start)


def causal_conv(values, rim_rows, taps, offset):
    padded = jnp.concatenate([rim_rows.astype(jnp.float32), values.astype(jnp.float32)], 0)
    summed = (
        offset[None, :]
        + taps[0] * padded[0:-3]
        + taps[1] * padded[1:-2]
        + taps[2] * padded[2:-1]
        + taps[3] * padded[3:]
    )
    return jax.nn.silu(summed).astype(jnp.bfloat16)


def per_device(
    x_in, dt_raw, bc_in, z_in, conv_x, bias_x, conv_bc, bias_bc, dt_bias, a_log, d_skip, norm_gain
):
    x_group, dt_group = (
        lax.all_to_all(x_in, "head", split_axis=1, concat_axis=0, tiled=True),
        lax.all_to_all(dt_raw, "head", split_axis=1, concat_axis=0, tiled=True),
    )
    bc_group = lax.all_gather(bc_in, "head", axis=0, tiled=True)
    tail_rows = jnp.concatenate([x_group[-3:], bc_group[-3:]], 1)
    rim_rows = from_behind(tail_rows, "ctx", 1)
    x_width = x_group.shape[1]
    x_conv = causal_conv(x_group, rim_rows[:, :x_width], conv_x, bias_x)
    bc_conv = causal_conv(bc_group, rim_rows[:, x_width:], conv_bc, bias_bc)
    state_size = bc_in.shape[1] // 2
    seg_rows = x_group.shape[0]
    head_count = dt_group.shape[1]
    head_width = x_width // head_count
    nblk = seg_rows // BLOCK
    x_blk = x_conv.reshape(nblk, BLOCK, head_count, head_width)
    b_blk = bc_conv[:, :state_size].reshape(nblk, BLOCK, state_size)
    c_blk = bc_conv[:, state_size:].reshape(nblk, BLOCK, state_size)
    step_size = jax.nn.softplus(dt_group.astype(jnp.float32) + dt_bias[None, :])
    log_decay = step_size * (-jnp.exp(a_log))[None, :]
    dt_blk = step_size.reshape(nblk, BLOCK, head_count)
    cum_sum = jnp.cumsum(log_decay.reshape(nblk, BLOCK, head_count), axis=1)
    scores = jnp.einsum("ctn,csn->cts", c_blk, b_blk, preferred_element_type=jnp.float32)
    cum_t = cum_sum.transpose(0, 2, 1)
    lower = jnp.arange(BLOCK)[:, None] >= jnp.arange(BLOCK)[None, :]
    spread = jnp.exp(
        jnp.where(lower[None, None], cum_t[:, :, :, None] - cum_t[:, :, None, :], -1e30)
    )
    m_mat = (scores[:, None] * spread * dt_blk.transpose(0, 2, 1)[:, :, None, :]).astype(
        jnp.bfloat16
    )
    y_diag = jnp.einsum("chts,cshp->cthp", m_mat, x_blk, preferred_element_type=jnp.float32)
    weight = jnp.exp(cum_sum[:, -1:, :] - cum_sum) * dt_blk
    b_weighted = (b_blk.astype(jnp.float32)[:, :, None, :] * weight[:, :, :, None]).astype(
        jnp.bfloat16
    )
    st_new = jnp.einsum("cqhn,cqhp->chnp", b_weighted, x_blk, preferred_element_type=jnp.float32)
    totals = cum_sum[:, -1, :]
    local_states = [jnp.zeros((head_count, state_size, head_width), jnp.float32)]
    for blk_i in range(nblk):
        local_states.append(
            local_states[-1] * jnp.exp(totals[blk_i])[:, None, None] + st_new[blk_i]
        )
    summary = local_states[nblk]
    seg_decay = jnp.sum(totals, axis=0)

    def combine_pair(earlier, later):
        return (earlier[0] + later[0], earlier[1] * jnp.exp(later[0])[:, None, None] + later[1])

    identity = (jnp.zeros_like(seg_decay), jnp.zeros_like(summary))
    _, incoming = entering((seg_decay, summary), "ctx", combine_pair, identity)
    prior = jnp.cumsum(totals, axis=0) - totals
    h_in = incoming[None] * jnp.exp(prior)[:, :, None, None] + jnp.stack(local_states[:nblk], 0)
    h_bf = h_in.astype(jnp.bfloat16)
    y_off = (
        jnp.einsum("ctn,chnp->cthp", c_blk, h_bf, preferred_element_type=jnp.float32)
        * jnp.exp(cum_sum)[:, :, :, None]
    )
    y_out = (y_diag + y_off + d_skip[None, None, :, None] * x_blk.astype(jnp.float32)).astype(
        jnp.bfloat16
    )
    y_tokens = lax.all_to_all(
        y_out.reshape(seg_rows, x_width), "head", split_axis=0, concat_axis=1, tiled=True
    )
    gated = y_tokens.astype(jnp.float32) * jax.nn.silu(z_in.astype(jnp.float32))
    mean_sq = jnp.mean(gated * gated, axis=-1, keepdims=True)
    return (gated * lax.rsqrt(mean_sq + 1e-05) * norm_gain[None, :]).astype(jnp.bfloat16)


def solution(mesh):
    in_specs = (
        P(("ctx", "head"), None),
        P(("ctx", "head"), None),
        P(("ctx", "head"), None),
        P(("ctx", "head"), None),
        P(None, "head"),
        P("head"),
        P(),
        P(),
        P("head"),
        P("head"),
        P("head"),
        P(),
    )
    out_specs = P(("ctx", "head"), None)
    return jax.shard_map(
        per_device, mesh=mesh, in_specs=in_specs, out_specs=out_specs, check_vma=False
    )
```

profile of v0, /device:TPU:64, one launch (start us, length us, event | category | flops | bytes accessed | tf_op | source)
XLA Modules:
  0.0 414.6 jit_solution(7345406918957226392)
XLA Ops:
  6.5 1.4 copy.91
  8.0 14.8 %all-to-all-start.1 = ((bf16[96,16,8]{0,2,1:T(8,128)(2,1)}), bf16[96,16,8]{0,2,1:T(8,128)(2,1)S(1)}, u32[]{:S(2)}, u32[]{:S(2)}) async-start(bf16[96,16,8]{0,2,1:T(8,128)(2,1)} %bitcast.13), calls=%async_computation.1 | async-start | bytes 65536 | tf_op jit(solution)/shard_map/all_to_all | solution.py:49
  22.7 2.7 copy.119
  25.5 7.9 %all-to-all-done.1 = bf16[96,16,8]{0,2,1:T(8,128)(2,1)S(1)} async-done(((bf16[96,16,8]{0,2,1:T(8,128)(2,1)}), bf16[96,16,8]{0,2,1:T(8,128)(2,1)S(1)}, u32[]{:S(2)}, u32[]{:S(2)}) %all-to-all-start.1) | async-done | bytes 24608 | tf_op jit(solution)/shard_map/all_to_all | solution.py:49
  33.4 5.7 %all-to-all-start = ((bf16[96,16,512]{2,0,1:T(8,128)(2,1)}), bf16[96,16,512]{2,0,1:T(8,128)(2,1)S(1)}, u32[]{:S(2)}, u32[]{:S(2)}) async-start(bf16[96,16,512]{2,0,1:T(8,128)(2,1)} %bitcast.63), calls=%async_computation | async-start | bytes 3145728 | tf_op jit(solution)/shard_map/all_to_all | solution.py:48
  39.1 95.7 %all_gather.13 = bf16[1536,256]{1,0:T(8,128)(2,1)S(1)} all-gather(bf16[96,256]{1,0:T(8,128)(2,1)S(1)} %copy-done.4), channel_id=1, replica_groups=mesh['ctx'=32,'head'=16] {'head'}, dimensions={0}, use_global_device_ids=true | all-gather | bytes 835584 | tf_op jit(solution)/shard_map/all_gather | solution.py:51
  134.8 1.3 convert_element_type.70
  137.1 3.4 reduce-window.6
  143.2 1.3 collective-permute-start
  145.3 2.9 multiply_convert_fusion.5
  148.2 3.9 reshape.196
  152.2 2.7 copy.94
  154.9 4.3 %multiply_convert_fusion.8 = bf16[1536,256]{1,0:T(8,128)(2,1)S(1)} fusion(f32[1536,256]{1,0:T(8,128)} %convert_element_type.70, f32[3,256]{1,0:T(4,128)S(1)} %slice_convert_fusion.1, f32[256]{0:T(256)S(1)} %bitcast.84, f32[256]{0:T(256)S(1)} %bitcast.85, f32[256]{0:T(256)S(1)} %bitcast.83, f32[256]{0:T(256)S(1)} %bitcast.82, f32[256]{0:T(256)S(1)} %copy-done.13), kind=kLoop, calls=%fused_computation.55 | loop fusion | flops 6291456 | bytes 2367488 | tf_op jit(solution)/shard_map/convert_element_type | solution.py:41
  159.4 3.0 fusion.20
  163.3 1.3 dynamic-slice
  165.5 68.9 %all-reduce = f32[256]{0:T(256)S(1)} all-reduce(f32[256]{0:T(256)S(1)} %dynamic-update-slice), channel_id=2, replica_groups=mesh['ctx'=32,'head'=16] {'ctx'}, use_global_device_ids=true, to_apply=%add | all-reduce | flops 256 | bytes 2048
  238.8 1.6 fusion.51
  240.4 64.9 %while.14 = (s32[]{:T(128)}, f32[8,128,64]{2,1,0:T(8,128)S(1)}, s32[]{:T(128)}, f32[32,8]{1,0:T(8,128)}, f32[32,8,128,64]{2,3,1,0:T(8,128)}, /*index=5*/s32[]{:T(128)}, s32[]{:T(128)}) while((s32[]{:T(128)}, f32[8,128,64]{2,1,0:T(8,128)S(1)}, s32[]{:T(128)}, f32[32,8]{1,0:T(8,128)}, f32[32,8,128,64]{2,3,1,0:T(8,128)}, ...), condition=%wide.region_4.5_spmd.clone, body=%wide.region_3.4_spmd.clone.sunk | while | flops 262148 | bytes 1835217 | solution.py:29
  242.5 1.0 constant_dynamic-slice_fusion.2
  244.5 1.0 constant_dynamic-slice_fusion.2
  246.5 1.0 constant_dynamic-slice_fusion.2
  248.6 1.0 constant_dynamic-slice_fusion.2
  250.6 1.0 constant_dynamic-slice_fusion.2
  252.6 1.0 constant_dynamic-slice_fusion.2
  254.7 1.0 constant_dynamic-slice_fusion.2
  256.7 1.0 constant_dynamic-slice_fusion.2
  258.7 1.0 constant_dynamic-slice_fusion.2
  260.7 1.0 constant_dynamic-slice_fusion.2
  262.8 1.0 constant_dynamic-slice_fusion.2
  264.8 1.0 constant_dynamic-slice_fusion.2
  266.8 1.0 constant_dynamic-slice_fusion.2
  268.8 1.0 constant_dynamic-slice_fusion.2
  270.8 1.0 constant_dynamic-slice_fusion.2
  272.9 1.0 constant_dynamic-slice_fusion.2
  274.9 1.0 constant_dynamic-slice_fusion.2
  276.9 1.0 constant_dynamic-slice_fusion.2
  279.0 1.0 constant_dynamic-slice_fusion.2
  281.0 1.0 constant_dynamic-slice_fusion.2
  283.0 1.0 constant_dynamic-slice_fusion.2
  285.1 1.0 constant_dynamic-slice_fusion.2
  305.6 1.8 add_convert_fusion
  308.0 5.4 %fusion.23 = bf16[6,256,8,64]{1,3,2,0:T(8,128)(2,1)} fusion(bf16[6,256,8,64]{1,3,2,0:T(8,128)(2,1)S(1)} %copy-done.2, f32[6,256,8,64]{1,3,2,0:T(8,128)S(1)} %bitcast.75, f32[6,8,256]{2,1,0:T(8,128)S(1)} %copy-done.7, f32[6,8,256]{2,1,0:T(8,128)S(1)} %copy-done.5, f32[6,256,256]{2,1,0:T(8,128)S(1)} %copy-done.3, pred[256,256]{1,0:T(8,128)(4,1)S(1)} %iota_compare_fusion, ...), kind=kOutput, calls=%fused_computation.34 | convolution fusion | flops 423100416 | bytes 8077344 | tf_op jit(solution)/shard_map/chts,cshp->cthp/dot_general | solution.py:78
  313.4 3.2 copy.102
  316.6 2.9 reshape.195
  319.5 83.1 %all_to_all.45 = bf16[16,96,512]{2,1,0:T(8,128)(2,1)S(1)} all-to-all(bf16[16,96,512]{2,1,0:T(8,128)(2,1)} %reshape.195), channel_id=1, replica_groups=mesh['ctx'=32,'head'=16] {'head'}, dimensions={0} | all-to-all | bytes 3145728 | tf_op jit(solution)/shard_map/all_to_all | solution.py:108
  403.3 1.1 copy-done
  404.4 1.1 multiply_reduce_fusion
  405.5 2.2 multiply_convert_fusion.4
  (185 shorter events, 54.2 us)
Async XLA Ops:
  8.0 25.4 %all-to-all-start.1 = ((bf16[96,16,8]{0,2,1:T(8,128)(2,1)}), bf16[96,16,8]{0,2,1:T(8,128)(2,1)S(1)}, u32[]{:S(2)}, u32[]{:S(2)}) async-start(bf16[96,16,8]{0,2,1:T(8,128)(2,1)} %bitcast.13), calls=%async_computation.1 | async-start | bytes 65536 | tf_op jit(solution)/shard_map/all_to_all | solution.py:49
  22.7 16.4 %copy-start.4 = (bf16[96,256]{1,0:T(8,128)(2,1)S(1)}, bf16[96,256]{1,0:T(8,128)(2,1)}, u32[]{:S(2)}) copy-start(bf16[96,256]{1,0:T(8,128)(2,1)} %param.16) | copy-start | bytes 147460
  33.4 103.4 %copy-start.15 = (f32[8]{0:T(128)S(1)}, f32[8]{0:T(128)}, u32[]{:S(2)}) copy-start(f32[8]{0:T(128)} %param.23) | copy-start | bytes 100
  33.4 103.4 %copy-start.10 = (f32[4,256]{1,0:T(4,128)S(1)}, f32[4,256]{1,0:T(4,128)}, u32[]{:S(2)}) copy-start(f32[4,256]{1,0:T(4,128)} %param.20) | copy-start | bytes 12292
  33.4 103.5 %copy-start.9 = (f32[4,512]{1,0:T(4,128)S(1)}, f32[4,512]{1,0:T(4,128)}, u32[]{:S(2)}) copy-start(f32[4,512]{1,0:T(4,128)} %param.18) | copy-start | bytes 24580
  33.4 103.6 %copy-start.12 = (f32[8]{0:T(128)S(1)}, f32[8]{0:T(128)}, u32[]{:S(2)}) copy-start(f32[8]{0:T(128)} %param.22) | copy-start | bytes 100
  33.4 109.8 %all-to-all-start = ((bf16[96,16,512]{2,0,1:T(8,128)(2,1)}), bf16[96,16,512]{2,0,1:T(8,128)(2,1)S(1)}, u32[]{:S(2)}, u32[]{:S(2)}) async-start(bf16[96,16,512]{2,0,1:T(8,128)(2,1)} %bitcast.63), calls=%async_computation | async-start | bytes 3145728 | tf_op jit(solution)/shard_map/all_to_all | solution.py:48
  39.1 201.4 %all-gather.3.cloned.1.call-start = ((), (), s32[]{:S(2)}) async-start(), calls=%async_computation.3 | async-start | bytes 8650752 | tf_op jit(solution)/shard_map/all_gather | solution.py:17
  136.1 9.2 %copy-start.11 = (f32[512]{0:T(512)S(1)}, f32[512]{0:T(512)}, u32[]{:S(2)}) copy-start(f32[512]{0:T(512)} %param.19) | copy-start | bytes 6148
  143.2 2.1 collective-permute-start
  152.2 2.7 copy-start.13
  154.9 4.4 %copy-start.1 = (bf16[6,256,8,64]{1,3,2,0:T(8,128)(2,1)S(1)}, bf16[6,256,8,64]{1,3,2,0:T(8,128)(2,1)}, u32[]{:S(2)}) copy-start(bf16[6,256,8,64]{1,3,2,0:T(8,128)(2,1)} %copy.94) | copy-start | bytes 4718596
  159.4 5.9 %copy-start.14 = (f32[8]{0:T(128)S(1)}, f32[8]{0:T(128)}, u32[]{:S(2)}) copy-start(f32[8]{0:T(128)} %get-tuple-element.154) | copy-start | bytes 100
  305.5 2.5 copy-start.2
  305.5 2.5 copy-start.3
  305.5 2.5 copy-start.5
  305.5 2.5 copy-start.6
  305.5 2.5 copy-start.7
  305.5 2.5 copy-start.16
  403.0 1.4 copy-start
  403.3 2.2 copy-start.8
Sparse Core Ops, SparseCore 0:
  163.4 71.9 all-gather.2
where the time goes:
time: 417 us; the launch traced here: 415 us
  blocking collectives  248 us (59%)
  local copies, waits for them, and re-layouts  82.9 us (20%)
  other arithmetic  28.1 us (7%)
  starting transfers between devices  21.7 us (5%)
  between operations  14.4 us (3%)
  matrix products  10.5 us (3%)
  waiting for transfers between devices  8.2 us (2%)
    all_gather x1, blocking collectives, per_device(): bc_group = lax.all_gather(bc_in, 'head', axis=0, tiled=True)  95.7 us
    all_to_all x1, blocking collectives, per_device(): lax.all_to_all(y_out.reshape(seg_rows, x_width), 'head', split_axis=0, co...  83.1 us
    unnamed x1, blocking collectives  68.9 us
    dynamic_slice x64, local copies, waits for them, and re-layouts, step(): new = combine(before, jax.tree.map(lambda part: part[k], everything))  37.5 us
    exp x32, local copies, waits for them, and re-layouts, combine_pair(): jnp.exp(later[0])[:, None, None]  22.1 us
    all_to_all x1, starting transfers between devices, per_device(): lax.all_to_all(dt_raw, 'head', split_axis=1, concat_axis=0, tiled=True)  14.8 us
  transfers between devices with their start and end apart: 4, of which 2 were waited for; matrix products, arithmetic and copies ran while one was open for 5% of the time, Pallas kernels for 0%

commit v1 on v0

v1 whole, which is shorter than its diff:
```python
import jax
import jax.numpy as jnp
from jax import lax
from jax.experimental import pallas as pl
from jax.experimental.pallas import tpu as pltpu
from jax.sharding import PartitionSpec as P

BLOCK = 256
STATE = 128
WIDTH = 64
HEADS = 4
LANES = HEADS * WIDTH
CHUNKS = 2
RIM = 16
F32 = jnp.float32
BF16 = jnp.bfloat16


def silu(u):
    return u / (1.0 + jnp.exp(-u))


def causal_conv(before, rows, taps, offset):
    count = rows.shape[0]
    padded = jnp.concatenate([before, rows], 0).astype(F32)
    summed = offset + taps[0:1] * padded[RIM - 3 : RIM - 3 + count]
    summed = summed + taps[1:2] * padded[RIM - 2 : RIM - 2 + count]
    summed = summed + taps[2:3] * padded[RIM - 1 : RIM - 1 + count]
    summed = summed + taps[3:4] * padded[RIM : RIM + count]
    return silu(summed).astype(BF16)


def prep_kernel(g_ref, rim_ref, taps_ref, bias_ref, pick_ref, par_ref, c_ref, bt_ref, rows_ref, cols_ref, carry):
    @pl.when(pl.program_id(0) == 0)
    def _():
        carry[...] = rim_ref[...]

    raw = g_ref[:, : 2 * STATE]
    bcc = causal_conv(carry[...], raw, taps_ref[...], bias_ref[...])
    carry[...] = raw[BLOCK - RIM :]
    c_ref[...] = bcc[:, STATE:]
    bt_ref[...] = bcc[:, :STATE].astype(F32).T.astype(BF16)
    dt_raw = lax.dot_general(
        pick_ref[...], g_ref[:, 2 * STATE :], (((1,), (1,)), ((), ())), preferred_element_type=F32
    )
    shifted = dt_raw + par_ref[0]
    dt = jnp.maximum(shifted, 0.0) + jnp.log1p(jnp.exp(-jnp.abs(shifted)))
    cs = dt * -jnp.exp(par_ref[1])
    lane = lax.broadcasted_iota(jnp.int32, cs.shape, 1)
    step = 1
    while step < BLOCK:
        cs = cs + jnp.where(lane >= step, pltpu.roll(cs, step, 1), 0.0)
        step *= 2
    tot = cs[:, BLOCK - 1 :]
    rows_ref[0:8] = cs
    rows_ref[8:16] = dt
    rows_ref[16:24] = jnp.exp(tot - cs) * dt
    cols_ref[...] = jnp.concatenate([cs, jnp.exp(cs)], 0).T


def lane_pair(first, second, shape):
    lane = lax.broadcasted_iota(jnp.int32, shape, 1)
    return jnp.where(lane < WIDTH, first, second)


def state_kernel(chunk, x_ref, rim_ref, taps_ref, bias_ref, bt_ref, rows_ref, xc_ref, local_ref, sum_ref, carry):
    @pl.when(pl.program_id(0) == 0)
    def _():
        carry[...] = rim_ref[...]
        sum_ref[...] = jnp.zeros_like(sum_ref)

    raw = x_ref[...]
    xc = causal_conv(carry[...], raw, taps_ref[...], bias_ref[...])
    carry[...] = raw[BLOCK - RIM :]
    xc_ref[...] = xc
    local_ref[0] = sum_ref[...]
    bt = bt_ref[...].astype(F32)
    for pair in range(HEADS // 2):
        cols = slice(2 * WIDTH * pair, 2 * WIDTH * (pair + 1))
        parts, tots = [], []
        for h in (HEADS * chunk + 2 * pair, HEADS * chunk + 2 * pair + 1):
            bw = (bt * rows_ref[16 + h : 17 + h]).astype(BF16)
            parts.append(jnp.dot(bw, xc[:, cols], preferred_element_type=F32))
            tots.append(rows_ref[h : h + 1, BLOCK - 1 :])
        tot = lane_pair(tots[0], tots[1], (1, 2 * WIDTH))
        st = lane_pair(parts[0], parts[1], (STATE, 2 * WIDTH))
        sum_ref[:STATE, cols] = sum_ref[:STATE, cols] * jnp.exp(tot) + st
        sum_ref[STATE:, cols] = sum_ref[STATE:, cols] + tot


def diag_kernel(chunk, xc_ref, c_ref, bt_ref, rows_ref, cols_ref, skip_ref, y_ref):
    half = BLOCK // 2
    xc = xc_ref[...]
    scores = jnp.dot(c_ref[...], bt_ref[...], preferred_element_type=F32)
    for low, width in ((0, half), (half, BLOCK)):
        part = scores[low : low + half, :width]
        row = lax.broadcasted_iota(jnp.int32, (half, width), 0) + low
        col = lax.broadcasted_iota(jnp.int32, (half, width), 1)
        keep = row >= col
        for pair in range(HEADS // 2):
            cols = slice(2 * WIDTH * pair, 2 * WIDTH * (pair + 1))
            outs = []
            for h in (HEADS * chunk + 2 * pair, HEADS * chunk + 2 * pair + 1):
                gap = cols_ref[low : low + half, h : h + 1] - rows_ref[h : h + 1, :width]
                spread = jnp.exp(jnp.where(keep, gap, -1e30))
                m = (part * spread * rows_ref[8 + h : 9 + h, :width]).astype(BF16)
                outs.append(jnp.dot(m, xc[:width, cols], preferred_element_type=F32))
            y = lane_pair(outs[0], outs[1], (half, 2 * WIDTH))
            y_ref[low : low + half, cols] = (
                y + skip_ref[:, cols] * xc[low : low + half, cols].astype(F32)
            )


def join_kernel(chunk, yd_ref, c_ref, cols_ref, local_ref, in_ref, y_ref):
    hb = (in_ref[:STATE] * jnp.exp(local_ref[0, STATE : STATE + 1]) + local_ref[0, :STATE]).astype(BF16)
    off = jnp.dot(c_ref[...], hb, preferred_element_type=F32)
    for pair in range(HEADS // 2):
        cols = slice(2 * WIDTH * pair, 2 * WIDTH * (pair + 1))
        h = 8 + HEADS * chunk + 2 * pair
        scale = lane_pair(cols_ref[:, h : h + 1], cols_ref[:, h + 1 : h + 2], (BLOCK, 2 * WIDTH))
        y_ref[:, cols] = (yd_ref[:, cols] + off[:, cols] * scale).astype(BF16)


def gate_kernel(y_ref, z_ref, gated_ref, sq_ref):
    total = jnp.zeros(sq_ref.shape, F32)
    for g in range(y_ref.shape[0]):
        at = slice(CHUNKS * LANES * g, CHUNKS * LANES * g + LANES)
        gated = y_ref[g].astype(F32) * silu(z_ref[:, at].astype(F32))
        gated_ref[g] = gated
        sq = gated * gated
        total = total + sq[:, :128] + sq[:, 128:]
    sq_ref[...] = total


def norm_kernel(y_ref, z_ref, gated_ref, sq_ref, gain_ref, out_ref, late):
    groups = y_ref.shape[0]
    total = sq_ref[...]
    for g in range(groups):
        at = slice(CHUNKS * LANES * g + LANES, CHUNKS * LANES * (g + 1))
        gated = y_ref[g].astype(F32) * silu(z_ref[:, at].astype(F32))
        late[g] = gated
        sq = gated * gated
        total = total + sq[:, :128] + sq[:, 128:]
    mean = jnp.sum(total, axis=1, keepdims=True) * (1.0 / (groups * CHUNKS * LANES))
    scale = lax.rsqrt(mean + 1e-05)
    for g in range(groups):
        at = slice(CHUNKS * LANES * g, CHUNKS * LANES * g + LANES)
        out_ref[:, at] = (gated_ref[g] * scale * gain_ref[:, at]).astype(BF16)
        at = slice(CHUNKS * LANES * g + LANES, CHUNKS * LANES * (g + 1))
        out_ref[:, at] = (late[g] * scale * gain_ref[:, at]).astype(BF16)


def shift(value, axis, by):
    count = lax.axis_size(axis)
    return lax.ppermute(value, axis, [(i, i + by) for i in range(count - by)])


def combine(earlier, later):
    state = earlier[:STATE] * jnp.exp(later[STATE : STATE + 1]) + later[:STATE]
    return jnp.concatenate([state, earlier[STATE:] + later[STATE:]], 0)


def entering(summary, axis):
    reach, window, before = 1, summary, None
    while reach < lax.axis_size(axis):
        got = shift(window, axis, reach)
        before = got if before is None else combine(got, before)
        if 2 * reach < lax.axis_size(axis):
            window = combine(got, window)
        reach *= 2
    return before


def full(shape):
    return pl.BlockSpec(shape, lambda k: tuple(0 for _ in shape))


def rows_of(width):
    return pl.BlockSpec((BLOCK, width), lambda k: (k, 0))


def lanes_of(height):
    return pl.BlockSpec((height, BLOCK), lambda k: (0, k))


PARAMS = pltpu.CompilerParams(dimension_semantics=("arbitrary",), vmem_limit_bytes=40 << 20)


def per_device(
    x_in, dt_raw, bc_in, z_in, conv_x, bias_x, conv_bc, bias_bc, dt_bias, a_log, d_skip, norm_gain
):
    groups = lax.axis_size("head")
    rows = x_in.shape[0]
    seg = rows * groups
    nblk = seg // BLOCK
    heads = dt_bias.shape[0]
    x_parts = x_in.reshape(rows, groups, CHUNKS, LANES)

    def to_groups(chunk):
        part = lax.all_to_all(x_parts[:, :, chunk], "head", 1, 1, tiled=True)
        return part.transpose(1, 0, 2).reshape(seg, LANES)

    def to_tokens(value):
        part = value.reshape(groups, rows, LANES).transpose(1, 0, 2)
        return lax.all_to_all(part, "head", 1, 1, tiled=True).transpose(1, 0, 2)

    gathered = lax.all_gather(jnp.concatenate([bc_in, dt_raw], 1), "head", axis=0, tiled=True)
    x_seg = [to_groups(j) for j in range(CHUNKS)]

    pick = (
        jnp.arange(groups * heads)[None, :] == jnp.arange(heads)[:, None] + heads * lax.axis_index("head")
    ).astype(BF16)
    par = jnp.stack([dt_bias, a_log])[:, :, None]
    par = jnp.broadcast_to(par, (2, heads, BLOCK))
    bc_rim = shift(gathered[seg - RIM :, : 2 * STATE], "ctx", 1)
    c_mat, b_t, row_tab, col_tab = pl.pallas_call(
        prep_kernel,
        grid=(nblk,),
        in_specs=[
            rows_of(gathered.shape[1]),
            full((RIM, 2 * STATE)),
            full((4, 2 * STATE)),
            full((1, 2 * STATE)),
            full(pick.shape),
            full(par.shape),
        ],
        out_specs=[rows_of(STATE), lanes_of(STATE), lanes_of(3 * heads), rows_of(2 * heads)],
        out_shape=[
            jax.ShapeDtypeStruct((seg, STATE), BF16),
            jax.ShapeDtypeStruct((STATE, seg), BF16),
            jax.ShapeDtypeStruct((3 * heads, seg), F32),
            jax.ShapeDtypeStruct((seg, 2 * heads), F32),
        ],
        scratch_shapes=[pltpu.VMEM((RIM, 2 * STATE), BF16)],
        compiler_params=PARAMS,
        name="prep",
    )(gathered, bc_rim, conv_bc, bias_bc[None, :], pick, par)

    y_tok = []
    for j in range(CHUNKS):
        at = slice(LANES * j, LANES * (j + 1))
        rim = shift(x_seg[j][seg - RIM :], "ctx", 1)
        xc, local, summary = pl.pallas_call(
            lambda *refs, j=j: state_kernel(j, *refs),
            grid=(nblk,),
            in_specs=[
                rows_of(LANES),
                full((RIM, LANES)),
                full((4, LANES)),
                full((1, LANES)),
                lanes_of(STATE),
                lanes_of(3 * heads),
            ],
            out_specs=[
                rows_of(LANES),
                pl.BlockSpec((1, STATE + 8, LANES), lambda k: (k, 0, 0)),
                full((STATE + 8, LANES)),
            ],
            out_shape=[
                jax.ShapeDtypeStruct((seg, LANES), BF16),
                jax.ShapeDtypeStruct((nblk, STATE + 8, LANES), F32),
                jax.ShapeDtypeStruct((STATE + 8, LANES), F32),
            ],
            scratch_shapes=[pltpu.VMEM((RIM, LANES), BF16)],
            compiler_params=PARAMS,
            name=f"state{j}",
        )(x_seg[j], rim, conv_x[:, at], bias_x[None, at], b_t, row_tab)
        incoming = entering(summary, "ctx")
        skip = jnp.repeat(d_skip[HEADS * j : HEADS * (j + 1)], WIDTH)[None, :]
        y_diag = pl.pallas_call(
            lambda *refs, j=j: diag_kernel(j, *refs),
            grid=(nblk,),
            in_specs=[
                rows_of(LANES),
                rows_of(STATE),
                lanes_of(STATE),
                lanes_of(3 * heads),
                rows_of(2 * heads),
                full((1, LANES)),
            ],
            out_specs=rows_of(LANES),
            out_shape=jax.ShapeDtypeStruct((seg, LANES), F32),
            compiler_params=PARAMS,
            name=f"diag{j}",
        )(xc, c_mat, b_t, row_tab, col_tab, skip)
        y = pl.pallas_call(
            lambda *refs, j=j: join_kernel(j, *refs),
            grid=(nblk,),
            in_specs=[
                rows_of(LANES),
                rows_of(STATE),
                rows_of(2 * heads),
                pl.BlockSpec((1, STATE + 8, LANES), lambda k: (k, 0, 0)),
                full((STATE + 8, LANES)),
            ],
            out_specs=rows_of(LANES),
            out_shape=jax.ShapeDtypeStruct((seg, LANES), BF16),
            compiler_params=PARAMS,
            name=f"join{j}",
        )(y_diag, c_mat, col_tab, local, incoming)
        y_tok.append(to_tokens(y))

    gated, squares = pl.pallas_call(
        gate_kernel,
        out_shape=[
            jax.ShapeDtypeStruct((groups, rows, LANES), F32),
            jax.ShapeDtypeStruct((rows, 128), F32),
        ],
        compiler_params=pltpu.CompilerParams(vmem_limit_bytes=40 << 20),
        name="gate",
    )(y_tok[0], z_in)
    return pl.pallas_call(
        norm_kernel,
        out_shape=jax.ShapeDtypeStruct(z_in.shape, BF16),
        scratch_shapes=[pltpu.VMEM((groups, rows, LANES), F32)],
        compiler_params=pltpu.CompilerParams(vmem_limit_bytes=40 << 20),
        name="norm",
    )(y_tok[1], z_in, gated, squares, norm_gain[None, :])


def solution(mesh):
    token = P(("ctx", "head"), None)
    in_specs = (
        token,
        token,
        token,
        token,
        P(None, "head"),
        P("head"),
        P(),
        P(),
        P("head"),
        P("head"),
        P("head"),
        P(),
    )
    return jax.shard_map(per_device, mesh=mesh, in_specs=in_specs, out_specs=token, check_vma=False)
```

time: 417 us -> 335 us (0.80)
  the two profiles are of different devices: /device:TPU:64 before, /device:TPU:4 now
where the time goes in v1:
time: 335 us; the launch traced here: 334 us
  waiting for transfers between devices  203 us (61%)
  starting transfers between devices  69.9 us (21%)
  Pallas kernels  22.6 us (7%)
  local copies, waits for them, and re-layouts  20.7 us (6%)
  between operations  14.2 us (4%)
  other arithmetic  3.76 us (1%)
    all_gather x1, waiting for transfers between devices, per_device(): lax.all_gather(jnp.concatenate([bc_in, dt_raw], 1), 'head', axis=0, tiled...  81 us
    ppermute x13, waiting for transfers between devices, shift(): return lax.ppermute(value, axis, [(i, i + by) for i in range(count - by)])  43.6 us
    all_to_all x2, waiting for transfers between devices, to_tokens(): return lax.all_to_all(part, 'head', 1, 1, tiled=True).transpose(1, 0, 2)  42.5 us
    all_to_all x2, waiting for transfers between devices, to_groups(): part = lax.all_to_all(x_parts[:, :, chunk], 'head', 1, 1, tiled=True)  36 us
    ppermute x13, starting transfers between devices, shift(): return lax.ppermute(value, axis, [(i, i + by) for i in range(count - by)])  32.4 us
    all_to_all x2, starting transfers between devices, to_groups(): part = lax.all_to_all(x_parts[:, :, chunk], 'head', 1, 1, tiled=True)  22.5 us
    all_to_all x2, starting transfers between devices, to_tokens(): return lax.all_to_all(part, 'head', 1, 1, tiled=True).transpose(1, 0, 2)  14.9 us
    unnamed x50, local copies, waits for them, and re-layouts  13.5 us
  transfers between devices with their start and end apart: 18, of which 12 were waited for; matrix products, arithmetic and copies ran while one was open for 2% of the time, Pallas kernels for 6%

profile of v1, /device:TPU:4, one launch (start us, length us, event | category | flops | bytes accessed | tf_op | source)
XLA Modules:
  0.0 334.3 jit_solution(7390656716250603701)
XLA Ops:
  6.5 2.9 reshape.21
  9.4 3.1 fusion.3
  12.5 1.8 copy.20
  14.2 15.2 %all-to-all-start = ((bf16[96,16,256]{2,0,1:T(8,128)(2,1)}), bf16[96,16,256]{2,0,1:T(8,128)(2,1)S(1)}, u32[]{:S(2)}, u32[]{:S(2)}) async-start(bf16[96,16,256]{2,0,1:T(8,128)(2,1)} %bitcast.41), calls=%async_computation | async-start | bytes 1572864 | tf_op jit(solution)/shard_map/all_to_all | solution.py:200
  29.5 3.2 copy.19
  32.7 36.0 %all-to-all-done = bf16[96,16,256]{2,0,1:T(8,128)(2,1)S(1)} async-done(((bf16[96,16,256]{2,0,1:T(8,128)(2,1)}), bf16[96,16,256]{2,0,1:T(8,128)(2,1)S(1)}, u32[]{:S(2)}, u32[]{:S(2)}) %all-to-all-start) | async-done | bytes 786464 | tf_op jit(solution)/shard_map/all_to_all | solution.py:200
  68.7 7.3 %all-to-all-start.2 = ((bf16[96,16,256]{2,0,1:T(8,128)(2,1)}), bf16[96,16,256]{2,0,1:T(8,128)(2,1)S(1)}, u32[]{:S(2)}, u32[]{:S(2)}) async-start(bf16[96,16,256]{2,0,1:T(8,128)(2,1)} %bitcast.40), calls=%async_computation.2 | async-start | bytes 1572864 | tf_op jit(solution)/shard_map/all_to_all | solution.py:200
  77.0 81.0 %all-gather.2.cloned.1.call-done.g_ref = bf16[1536,384]{1,0:T(8,128)(2,1)} async-done(((bf16[96,384]{1,0:T(8,128)(2,1)}), bf16[1536,384]{1,0:T(8,128)(2,1)}) %all-gather.2.cloned.1.call-update) | async-done | bytes 1179664 | tf_op jit(solution)/shard_map/all_gather | solution.py:207
  158.7 1.9 collective-permute-start.1
  160.6 3.9 %collective-permute-start = (bf16[16,256]{1,0:T(8,128)(2,1)S(1)}, bf16[16,256]{1,0:T(8,128)(2,1)S(1)}, u32[]{:S(2)}, u32[]{:S(2)}) collective-permute-start(bf16[16,256]{1,0:T(8,128)(2,1)S(1)} %slice.221), channel_id=1, source_target_pairs={{0,16},{16,32},{32,48},{48,64},{64,80},{80,96},{96,112},{112,128},... | collective-permute-start | bytes 24584 | tf_op jit(solution)/shard_map/ppermute | solution.py:155
  165.8 1.3 copy-done.7
  167.1 5.9 %prep.1 = (bf16[1536,128]{1,0:T(8,128)(2,1)S(1)}, bf16[128,1536]{1,0:T(8,128)(2,1)S(1)}, f32[24,1536]{1,0:T(8,128)S(1)}, f32[1536,16]{1,0:T(8,128)S(1)}) custom-call(bf16[1536,384]{1,0:T(8,128)(2,1)S(1)} %copy-done.7, bf16[16,256]{1,0:T(8,128)(2,1)S(1)} %collective-permute-done.1.rim_ref, f32[4,256]{1,0:T(4,128)S(1)} %copy-done.11, f32[1,256]{1,0:T(1,128)S(1)} %bitcast.53, ...), custom_call_target="tpu_custom_call" | custom-call | tf_op jit(solution)/shard_map/prep/pallas_call | solution.py:216
  173.0 1.9 collective-permute-start.7
  175.0 3.0 state1.1
  178.8 2.6 collective-permute-start.2
  181.5 3.0 state0.1
  184.5 1.9 collective-permute-start.8
  186.4 2.7 diag1.1.refs_0_
  189.1 2.7 diag0.1.refs_0_
  191.9 3.5 %collective-permute-start.3 = (f32[136,256]{1,0:T(8,128)S(1)}, f32[136,256]{1,0:T(8,128)S(1)}, u32[]{:S(2)}, u32[]{:S(2)}) collective-permute-start(f32[136,256]{1,0:T(8,128)S(1)} %pad_maximum_fusion), channel_id=1, source_target_pairs={{0,32},{16,48},{32,64},{48,80},{64,96},{80,112},{96,128},{112,144}... | collective-permute-start | bytes 417800 | tf_op jit(solution)/shard_map/ppermute | solution.py:155
  195.4 2.6 collective-permute-start.9
  198.0 7.5 %collective-permute-done.9 = f32[136,256]{1,0:T(8,128)S(1)} collective-permute-done((f32[136,256]{1,0:T(8,128)S(1)}, f32[136,256]{1,0:T(8,128)S(1)}, u32[]{:S(2)}, u32[]{:S(2)}) %collective-permute-start.9) | collective-permute-done | bytes 139296 | tf_op jit(solution)/shard_map/ppermute | solution.py:155
  205.5 3.1 collective-permute-start.10
  209.4 5.7 %collective-permute-done.10 = f32[136,256]{1,0:T(8,128)S(1)} collective-permute-done((f32[136,256]{1,0:T(8,128)S(1)}, f32[136,256]{1,0:T(8,128)S(1)}, u32[]{:S(2)}, u32[]{:S(2)}) %collective-permute-start.10) | collective-permute-done | bytes 139296 | tf_op jit(solution)/shard_map/ppermute | solution.py:155
  215.2 3.3 %collective-permute-start.11 = (f32[136,256]{1,0:T(8,128)S(1)}, f32[136,256]{1,0:T(8,128)S(1)}, u32[]{:S(2)}, u32[]{:S(2)}) collective-permute-start(f32[136,256]{1,0:T(8,128)S(1)} %pad_maximum_fusion.7), channel_id=1, source_target_pairs={{0,128},{16,144},{32,160},{48,176},{64,192},{80,208},{96,224},{112... | collective-permute-start | bytes 417800 | tf_op jit(solution)/shard_map/ppermute | solution.py:155
  218.5 3.6 %collective-permute-done.11 = f32[136,256]{1,0:T(8,128)S(1)} collective-permute-done((f32[136,256]{1,0:T(8,128)S(1)}, f32[136,256]{1,0:T(8,128)S(1)}, u32[]{:S(2)}, u32[]{:S(2)}) %collective-permute-start.11) | collective-permute-done | bytes 139296 | tf_op jit(solution)/shard_map/ppermute | solution.py:155
  222.2 1.3 collective-permute-start.12
  223.5 7.1 %collective-permute-done.12 = f32[136,256]{1,0:T(8,128)S(1)} collective-permute-done((f32[136,256]{1,0:T(8,128)S(1)}, f32[136,256]{1,0:T(8,128)S(1)}, u32[]{:S(2)}, u32[]{:S(2)}) %collective-permute-start.12) | collective-permute-done | bytes 139296 | tf_op jit(solution)/shard_map/ppermute | solution.py:155
  230.7 1.4 join0.1
  232.2 0.9 copy-done.1
  233.1 7.2 %all-to-all-start.3 = ((bf16[96,16,256]{2,0,1:T(8,128)(2,1)}), bf16[96,16,256]{2,0,1:T(8,128)(2,1)S(1)}, u32[]{:S(2)}, u32[]{:S(2)}) async-start(bf16[96,16,256]{2,0,1:T(8,128)(2,1)} %bitcast.47), calls=%async_computation.3 | async-start | bytes 1572864 | tf_op jit(solution)/shard_map/all_to_all | solution.py:205
  240.3 1.0 pad_maximum_fusion.1
  241.3 1.9 collective-permute-start.4
  243.3 7.9 %collective-permute-done.4 = f32[136,256]{1,0:T(8,128)S(1)} collective-permute-done((f32[136,256]{1,0:T(8,128)S(1)}, f32[136,256]{1,0:T(8,128)S(1)}, u32[]{:S(2)}, u32[]{:S(2)}) %collective-permute-start.4) | collective-permute-done | bytes 139296 | tf_op jit(solution)/shard_map/ppermute | solution.py:155
  251.2 0.9 multiply_add_fusion.4
  252.1 3.2 collective-permute-start.5
  255.3 3.8 %collective-permute-done.5 = f32[136,256]{1,0:T(8,128)S(1)} collective-permute-done((f32[136,256]{1,0:T(8,128)S(1)}, f32[136,256]{1,0:T(8,128)S(1)}, u32[]{:S(2)}, u32[]{:S(2)}) %collective-permute-start.5) | collective-permute-done | bytes 139296 | tf_op jit(solution)/shard_map/ppermute | solution.py:155
  259.1 1.3 collective-permute-start.6
  260.4 7.1 %collective-permute-done.6 = f32[136,256]{1,0:T(8,128)S(1)} collective-permute-done((f32[136,256]{1,0:T(8,128)S(1)}, f32[136,256]{1,0:T(8,128)S(1)}, u32[]{:S(2)}, u32[]{:S(2)}) %collective-permute-start.6) | collective-permute-done | bytes 139296 | tf_op jit(solution)/shard_map/ppermute | solution.py:155
  267.7 1.4 join1.1
  270.0 6.0 %all-to-all-done.3 = bf16[96,16,256]{2,0,1:T(8,128)(2,1)S(1)} async-done(((bf16[96,16,256]{2,0,1:T(8,128)(2,1)}), bf16[96,16,256]{2,0,1:T(8,128)(2,1)S(1)}, u32[]{:S(2)}, u32[]{:S(2)}) %all-to-all-start.3) | async-done | bytes 786464 | tf_op jit(solution)/shard_map/all_to_all | solution.py:205
  276.1 7.7 %all-to-all-start.1 = ((bf16[96,16,256]{2,0,1:T(8,128)(2,1)}), bf16[96,16,256]{2,0,1:T(8,128)(2,1)S(1)}, u32[]{:S(2)}, u32[]{:S(2)}) async-start(bf16[96,16,256]{2,0,1:T(8,128)(2,1)} %bitcast.48), calls=%async_computation.1 | async-start | bytes 1572864 | tf_op jit(solution)/shard_map/all_to_all | solution.py:205
  284.4 1.1 copy-done.5
  285.5 36.4 %all-to-all-done.1 = bf16[96,16,256]{2,0,1:T(8,128)(2,1)S(1)} async-done(((bf16[96,16,256]{2,0,1:T(8,128)(2,1)}), bf16[96,16,256]{2,0,1:T(8,128)(2,1)S(1)}, u32[]{:S(2)}, u32[]{:S(2)}) %all-to-all-start.1) | async-done | bytes 786464 | tf_op jit(solution)/shard_map/all_to_all | solution.py:205
  322.0 0.9 copy-done.3
  322.9 1.1 copy-done.4
  324.0 1.4 copy-done.6
  325.4 2.1 norm.1
  (109 shorter events, 6.5 us)
Async XLA Ops:
  14.2 54.5 %all-to-all-start = ((bf16[96,16,256]{2,0,1:T(8,128)(2,1)}), bf16[96,16,256]{2,0,1:T(8,128)(2,1)S(1)}, u32[]{:S(2)}, u32[]{:S(2)}) async-start(bf16[96,16,256]{2,0,1:T(8,128)(2,1)} %bitcast.41), calls=%async_computation | async-start | bytes 1572864 | tf_op jit(solution)/shard_map/all_to_all | solution.py:200
  29.4 46.7 %copy-start.17 = (bf16[96,256]{1,0:T(8,128)(2,1)S(1)}, bf16[96,256]{1,0:T(8,128)(2,1)}, u32[]{:S(2)}) copy-start(bf16[96,256]{1,0:T(8,128)(2,1)} %param.14) | copy-start | bytes 147460
  29.4 46.7 %copy-start.18 = (bf16[96,128]{1,0:T(8,128)(2,1)S(1)}, bf16[96,128]{1,0:T(8,128)(2,1)}, u32[]{:S(2)}) copy-start(bf16[96,128]{1,0:T(8,128)(2,1)} %param.13) | copy-start | bytes 73732
  29.4 47.4 %copy-start.21 = (f32[8]{0:T(128)S(1)}, f32[8]{0:T(128)}, u32[]{:S(2)}) copy-start(f32[8]{0:T(128)} %param.22) | copy-start | bytes 100
  29.5 47.5 %copy-start.20 = (f32[512]{0:T(512)S(1)}, f32[512]{0:T(512)}, u32[]{:S(2)}) copy-start(f32[512]{0:T(512)} %param.17) | copy-start | bytes 6148
  29.5 47.5 %copy-start.19 = (f32[4,512]{1,0:T(4,128)S(1)}, f32[4,512]{1,0:T(4,128)}, u32[]{:S(2)}) copy-start(f32[4,512]{1,0:T(4,128)} %param.16) | copy-start | bytes 24580
  29.5 135.0 %copy-start.22 = (f32[8]{0:T(128)S(1)}, f32[8]{0:T(128)}, u32[]{:S(2)}) copy-start(f32[8]{0:T(128)} %param.21) | copy-start | bytes 100
  29.5 135.0 %copy-start.23 = (f32[8]{0:T(128)S(1)}, f32[8]{0:T(128)}, u32[]{:S(2)}) copy-start(f32[8]{0:T(128)} %param.20) | copy-start | bytes 100
  29.5 136.3 %copy-start.11 = (f32[4,256]{1,0:T(4,128)S(1)}, f32[4,256]{1,0:T(4,128)}, u32[]{:S(2)}) copy-start(f32[4,256]{1,0:T(4,128)} %taps_ref.1) | copy-start | bytes 12292
  29.5 136.3 %copy-start.12 = (f32[256]{0:T(256)S(1)}, f32[256]{0:T(256)}, u32[]{:S(2)}) copy-start(f32[256]{0:T(256)} %param.19) | copy-start | bytes 3076
  68.7 104.3 %all-to-all-start.2 = ((bf16[96,16,256]{2,0,1:T(8,128)(2,1)}), bf16[96,16,256]{2,0,1:T(8,128)(2,1)S(1)}, u32[]{:S(2)}, u32[]{:S(2)}) async-start(bf16[96,16,256]{2,0,1:T(8,128)(2,1)} %bitcast.40), calls=%async_computation.2 | async-start | bytes 1572864 | tf_op jit(solution)/shard_map/all_to_all | solution.py:200
  76.1 82.0 %all-gather.2.cloned.1.call-start = ((), (), s32[]{:S(2)}) async-start(), calls=%async_computation.4 | async-start | bytes 1253376 | tf_op jit(solution)/shard_map/all_gather | solution.py:207
  158.7 7.1 %collective-permute-start.1 = (bf16[16,256]{1,0:T(8,128)(2,1)S(1)}, bf16[16,256]{1,0:T(8,128)(2,1)S(1)}, u32[]{:S(2)}, u32[]{:S(2)}) collective-permute-start(bf16[16,256]{1,0:T(8,128)(2,1)S(1)} %slice.222), channel_id=1, source_target_pairs={{0,16},{16,32},{32,48},{48,64},{64,80},{80,96},{96,112},{112,128},... | collective-permute-start | bytes 24584 | tf_op jit(solution)/shard_map/ppermute | solution.py:155
  160.6 14.3 %collective-permute-start = (bf16[16,256]{1,0:T(8,128)(2,1)S(1)}, bf16[16,256]{1,0:T(8,128)(2,1)S(1)}, u32[]{:S(2)}, u32[]{:S(2)}) collective-permute-start(bf16[16,256]{1,0:T(8,128)(2,1)S(1)} %slice.221), channel_id=1, source_target_pairs={{0,16},{16,32},{32,48},{48,64},{64,80},{80,96},{96,112},{112,128},... | collective-permute-start | bytes 24584 | tf_op jit(solution)/shard_map/ppermute | solution.py:155
  165.8 1.3 copy-start.7
  173.0 8.5 %collective-permute-start.7 = (bf16[16,256]{1,0:T(8,128)(2,1)S(1)}, bf16[16,256]{1,0:T(8,128)(2,1)S(1)}, u32[]{:S(2)}, u32[]{:S(2)}) collective-permute-start(bf16[16,256]{1,0:T(8,128)(2,1)S(1)} %slice.241), channel_id=1, source_target_pairs={{0,16},{16,32},{32,48},{48,64},{64,80},{80,96},{96,112},{112,128},... | collective-permute-start | bytes 24584 | tf_op jit(solution)/shard_map/ppermute | solution.py:155
  177.9 0.9 copy-start.8
  178.8 12.9 %collective-permute-start.2 = (f32[136,256]{1,0:T(8,128)S(1)}, f32[136,256]{1,0:T(8,128)S(1)}, u32[]{:S(2)}, u32[]{:S(2)}) collective-permute-start(f32[136,256]{1,0:T(8,128)S(1)} %get-tuple-element.23), channel_id=1, source_target_pairs={{0,16},{16,32},{32,48},{48,64},{64,80},{80,96},{96,112},{112,128},... | collective-permute-start | bytes 417800 | tf_op jit(solution)/shard_map/ppermute | solution.py:155
  184.5 10.9 %collective-permute-start.8 = (f32[136,256]{1,0:T(8,128)S(1)}, f32[136,256]{1,0:T(8,128)S(1)}, u32[]{:S(2)}, u32[]{:S(2)}) collective-permute-start(f32[136,256]{1,0:T(8,128)S(1)} %get-tuple-element.26), channel_id=1, source_target_pairs={{0,16},{16,32},{32,48},{48,64},{64,80},{80,96},{96,112},{112,128},... | collective-permute-start | bytes 417800 | tf_op jit(solution)/shard_map/ppermute | solution.py:155
  191.8 23.4 %copy-start.13 = (f32[136,256]{1,0:T(8,128)}, f32[136,256]{1,0:T(8,128)S(1)}, u32[]{:S(2)}) copy-start(f32[136,256]{1,0:T(8,128)S(1)} %collective-permute-done.2) | copy-start | bytes 417796
  191.9 16.8 %collective-permute-start.3 = (f32[136,256]{1,0:T(8,128)S(1)}, f32[136,256]{1,0:T(8,128)S(1)}, u32[]{:S(2)}, u32[]{:S(2)}) collective-permute-start(f32[136,256]{1,0:T(8,128)S(1)} %pad_maximum_fusion), channel_id=1, source_target_pairs={{0,32},{16,48},{32,64},{48,80},{64,96},{80,112},{96,128},{112,144}... | collective-permute-start | bytes 417800 | tf_op jit(solution)/shard_map/ppermute | solution.py:155
  195.4 10.1 %collective-permute-start.9 = (f32[136,256]{1,0:T(8,128)S(1)}, f32[136,256]{1,0:T(8,128)S(1)}, u32[]{:S(2)}, u32[]{:S(2)}) collective-permute-start(f32[136,256]{1,0:T(8,128)S(1)} %pad_maximum_fusion.5), channel_id=1, source_target_pairs={{0,32},{16,48},{32,64},{48,80},{64,96},{80,112},{96,128},{112,144}... | collective-permute-start | bytes 417800 | tf_op jit(solution)/shard_map/ppermute | solution.py:155
  205.5 9.6 %collective-permute-start.10 = (f32[136,256]{1,0:T(8,128)S(1)}, f32[136,256]{1,0:T(8,128)S(1)}, u32[]{:S(2)}, u32[]{:S(2)}) collective-permute-start(f32[136,256]{1,0:T(8,128)S(1)} %pad_maximum_fusion.6), channel_id=1, source_target_pairs={{0,64},{16,80},{32,96},{48,112},{64,128},{80,144},{96,160},{112,17... | collective-permute-start | bytes 417800 | tf_op jit(solution)/shard_map/ppermute | solution.py:155
  208.7 22.1 %copy-start.15 = (f32[136,256]{1,0:T(8,128)}, f32[136,256]{1,0:T(8,128)S(1)}, u32[]{:S(2)}) copy-start(f32[136,256]{1,0:T(8,128)S(1)} %collective-permute-done.3) | copy-start | bytes 417796
  215.2 6.9 %collective-permute-start.11 = (f32[136,256]{1,0:T(8,128)S(1)}, f32[136,256]{1,0:T(8,128)S(1)}, u32[]{:S(2)}, u32[]{:S(2)}) collective-permute-start(f32[136,256]{1,0:T(8,128)S(1)} %pad_maximum_fusion.7), channel_id=1, source_target_pairs={{0,128},{16,144},{32,160},{48,176},{64,192},{80,208},{96,224},{112... | collective-permute-start | bytes 417800 | tf_op jit(solution)/shard_map/ppermute | solution.py:155
  222.2 8.5 %collective-permute-start.12 = (f32[136,256]{1,0:T(8,128)S(1)}, f32[136,256]{1,0:T(8,128)S(1)}, u32[]{:S(2)}, u32[]{:S(2)}) collective-permute-start(f32[136,256]{1,0:T(8,128)S(1)} %pad_maximum_fusion.8), channel_id=1, source_target_pairs={{0,256},{16,272},{32,288},{48,304},{64,320},{80,336},{96,352},{112... | collective-permute-start | bytes 417800 | tf_op jit(solution)/shard_map/ppermute | solution.py:155
  232.2 0.9 copy-start.1
  233.1 43.0 %all-to-all-start.3 = ((bf16[96,16,256]{2,0,1:T(8,128)(2,1)}), bf16[96,16,256]{2,0,1:T(8,128)(2,1)S(1)}, u32[]{:S(2)}, u32[]{:S(2)}) async-start(bf16[96,16,256]{2,0,1:T(8,128)(2,1)} %bitcast.47), calls=%async_computation.3 | async-start | bytes 1572864 | tf_op jit(solution)/shard_map/all_to_all | solution.py:205
  240.3 20.1 %copy-start.14 = (f32[136,256]{1,0:T(8,128)S(1)}, f32[136,256]{1,0:T(8,128)}, u32[]{:S(2)}) copy-start(f32[136,256]{1,0:T(8,128)} %copy-done.13) | copy-start | bytes 417796
  240.3 27.3 %copy-start.16 = (f32[136,256]{1,0:T(8,128)S(1)}, f32[136,256]{1,0:T(8,128)}, u32[]{:S(2)}) copy-start(f32[136,256]{1,0:T(8,128)} %copy-done.15) | copy-start | bytes 417796
  240.3 27.4 %copy-start.9 = (f32[6,136,256]{2,1,0:T(8,128)S(1)}, f32[6,136,256]{2,1,0:T(8,128)}, u32[]{:S(2)}) copy-start(f32[6,136,256]{2,1,0:T(8,128)} %copy-done.8) | copy-start | bytes 2506756
  241.3 9.8 %collective-permute-start.4 = (f32[136,256]{1,0:T(8,128)S(1)}, f32[136,256]{1,0:T(8,128)S(1)}, u32[]{:S(2)}, u32[]{:S(2)}) collective-permute-start(f32[136,256]{1,0:T(8,128)S(1)} %pad_maximum_fusion.1), channel_id=1, source_target_pairs={{0,64},{16,80},{32,96},{48,112},{64,128},{80,144},{96,160},{112,17... | collective-permute-start | bytes 417800 | tf_op jit(solution)/shard_map/ppermute | solution.py:155
  252.1 7.0 %collective-permute-start.5 = (f32[136,256]{1,0:T(8,128)S(1)}, f32[136,256]{1,0:T(8,128)S(1)}, u32[]{:S(2)}, u32[]{:S(2)}) collective-permute-start(f32[136,256]{1,0:T(8,128)S(1)} %pad_maximum_fusion.2), channel_id=1, source_target_pairs={{0,128},{16,144},{32,160},{48,176},{64,192},{80,208},{96,224},{112... | collective-permute-start | bytes 417800 | tf_op jit(solution)/shard_map/ppermute | solution.py:155
  259.1 8.5 %collective-permute-start.6 = (f32[136,256]{1,0:T(8,128)S(1)}, f32[136,256]{1,0:T(8,128)S(1)}, u32[]{:S(2)}, u32[]{:S(2)}) collective-permute-start(f32[136,256]{1,0:T(8,128)S(1)} %pad_maximum_fusion.3), channel_id=1, source_target_pairs={{0,256},{16,272},{32,288},{48,304},{64,320},{80,336},{96,352},{112... | collective-permute-start | bytes 417800 | tf_op jit(solution)/shard_map/ppermute | solution.py:155
  269.1 0.9 copy-start.2
  270.0 13.8 %copy-start = (bf16[96,8192]{1,0:T(8,128)(2,1)S(1)}, bf16[96,8192]{1,0:T(8,128)(2,1)}, u32[]{:S(2)}) copy-start(bf16[96,8192]{1,0:T(8,128)(2,1)} %z_ref.3) | copy-start | bytes 4718596
  276.1 45.9 %all-to-all-start.1 = ((bf16[96,16,256]{2,0,1:T(8,128)(2,1)}), bf16[96,16,256]{2,0,1:T(8,128)(2,1)S(1)}, u32[]{:S(2)}, u32[]{:S(2)}) async-start(bf16[96,16,256]{2,0,1:T(8,128)(2,1)} %bitcast.48), calls=%async_computation.1 | async-start | bytes 1572864 | tf_op jit(solution)/shard_map/all_to_all | solution.py:205
  283.8 39.1 %copy-start.10 = (f32[8192]{0:T(1024)S(1)}, f32[8192]{0:T(1024)}, u32[]{:S(2)}) copy-start(f32[8192]{0:T(1024)} %param.23) | copy-start | bytes 98308
  284.4 1.1 copy-start.5
  322.0 0.9 copy-start.3
  322.9 1.1 copy-start.4
  324.0 1.4 copy-start.6
Sparse Core Ops, SparseCore 0:
  79.0 78.9 all-gather.1

commit v2 on v1

--- a/solution.py
+++ b/solution.py
@@ -30,20 +30,31 @@
     return silu(summed).astype(BF16)
 
 
-def prep_kernel(g_ref, rim_ref, taps_ref, bias_ref, pick_ref, par_ref, c_ref, bt_ref, rows_ref, cols_ref, carry):
+def pack_kernel(chunk, x_ref, *refs):
+    out_ref = refs[-1]
+    rows = x_ref.shape[0]
+    for g in range(out_ref.shape[0]):
+        start = LANES * (CHUNKS * g + chunk)
+        out_ref[g, :rows] = x_ref[:, start : start + LANES]
+    if chunk == 0:
+        dt = refs[0][...].astype(F32).T.astype(BF16)
+        heads = dt.shape[0] // out_ref.shape[0]
+        for g in range(out_ref.shape[0]):
+            out_ref[g, rows:, :rows] = dt[heads * g : heads * (g + 1)]
+            out_ref[g, rows:, rows:] = jnp.zeros((heads, LANES - rows), BF16)
+
+
+def prep_kernel(g_ref, rim_ref, taps_ref, bias_ref, dt_ref, par_ref, c_ref, bt_ref, rows_ref, cols_ref, carry):
     @pl.when(pl.program_id(0) == 0)
     def _():
         carry[...] = rim_ref[...]
 
-    raw = g_ref[:, : 2 * STATE]
+    raw = g_ref[...]
     bcc = causal_conv(carry[...], raw, taps_ref[...], bias_ref[...])
     carry[...] = raw[BLOCK - RIM :]
     c_ref[...] = bcc[:, STATE:]
     bt_ref[...] = bcc[:, :STATE].astype(F32).T.astype(BF16)
-    dt_raw = lax.dot_general(
-        pick_ref[...], g_ref[:, 2 * STATE :], (((1,), (1,)), ((), ())), preferred_element_type=F32
-    )
-    shifted = dt_raw + par_ref[0]
+    shifted = dt_ref[...].astype(F32) + par_ref[0]
     dt = jnp.maximum(shifted, 0.0) + jnp.log1p(jnp.exp(-jnp.abs(shifted)))
     cs = dt * -jnp.exp(par_ref[1])
     lane = lax.broadcasted_iota(jnp.int32, cs.shape, 1)
@@ -111,8 +122,9 @@
             )
 
 
-def join_kernel(chunk, yd_ref, c_ref, cols_ref, local_ref, in_ref, y_ref):
-    hb = (in_ref[:STATE] * jnp.exp(local_ref[0, STATE : STATE + 1]) + local_ref[0, :STATE]).astype(BF16)
+def join_kernel(chunk, yd_ref, c_ref, cols_ref, local_ref, near_ref, far_ref, y_ref):
+    entry = far_ref[:STATE] * jnp.exp(near_ref[STATE : STATE + 1]) + near_ref[:STATE]
+    hb = (entry * jnp.exp(local_ref[0, STATE : STATE + 1]) + local_ref[0, :STATE]).astype(BF16)
     off = jnp.dot(c_ref[...], hb, preferred_element_type=F32)
     for pair in range(HEADS // 2):
         cols = slice(2 * WIDTH * pair, 2 * WIDTH * (pair + 1))
@@ -121,33 +133,36 @@
         y_ref[:, cols] = (yd_ref[:, cols] + off[:, cols] * scale).astype(BF16)
 
 
-def gate_kernel(y_ref, z_ref, gated_ref, sq_ref):
-    total = jnp.zeros(sq_ref.shape, F32)
-    for g in range(y_ref.shape[0]):
-        at = slice(CHUNKS * LANES * g, CHUNKS * LANES * g + LANES)
-        gated = y_ref[g].astype(F32) * silu(z_ref[:, at].astype(F32))
-        gated_ref[g] = gated
-        sq = gated * gated
-        total = total + sq[:, :128] + sq[:, 128:]
-    sq_ref[...] = total
-
-
-def norm_kernel(y_ref, z_ref, gated_ref, sq_ref, gain_ref, out_ref, late):
-    groups = y_ref.shape[0]
-    total = sq_ref[...]
+def norm_kernel(first_ref, second_ref, z_ref, gain_ref, out_ref, gated_ref):
+    groups = first_ref.shape[0]
+    total = jnp.zeros((z_ref.shape[0], 128), F32)
     for g in range(groups):
-        at = slice(CHUNKS * LANES * g + LANES, CHUNKS * LANES * (g + 1))
-        gated = y_ref[g].astype(F32) * silu(z_ref[:, at].astype(F32))
-        late[g] = gated
-        sq = gated * gated
-        total = total + sq[:, :128] + sq[:, 128:]
+        for j, y_ref in enumerate((first_ref, second_ref)):
+            start = LANES * (CHUNKS * g + j)
+            at = slice(start, start + LANES)
+            gated = y_ref[g].astype(F32) * silu(z_ref[:, at].astype(F32))
+            gated_ref[:, at] = gated
+            sq = gated * gated
+            total = total + sq[:, :128] + sq[:, 128:]
     mean = jnp.sum(total, axis=1, keepdims=True) * (1.0 / (groups * CHUNKS * LANES))
-    scale = lax.rsqrt(mean + 1e-05)
-    for g in range(groups):
-        at = slice(CHUNKS * LANES * g, CHUNKS * LANES * g + LANES)
-        out_ref[:, at] = (gated_ref[g] * scale * gain_ref[:, at]).astype(BF16)
-        at = slice(CHUNKS * LANES * g + LANES, CHUNKS * LANES * (g + 1))
-        out_ref[:, at] = (late[g] * scale * gain_ref[:, at]).astype(BF16)
+    out_ref[...] = (gated_ref[...] * lax.rsqrt(mean + 1e-05) * gain_ref[...]).astype(BF16)
+
+
+def join_pair(earlier, later):
+    state = earlier[:STATE] * jnp.exp(later[STATE : STATE + 1]) + later[:STATE]
+    return jnp.concatenate([state, earlier[STATE:] + later[STATE:]], 0)
+
+
+def first_kernel(own_ref, one_ref, two_ref, three_ref, before_ref, window_ref):
+    before = join_pair(three_ref[...], join_pair(two_ref[...], one_ref[...]))
+    before_ref[...] = before
+    window_ref[...] = join_pair(before, own_ref[...])
+
+
+def second_kernel(own_ref, near_ref, one_ref, two_ref, three_ref, before_ref, window_ref):
+    reached = join_pair(three_ref[...], join_pair(two_ref[...], one_ref[...]))
+    before_ref[...] = join_pair(reached, near_ref[...])
+    window_ref[...] = join_pair(reached, own_ref[...])
 
 
 def shift(value, axis, by):
@@ -155,20 +170,13 @@
     return lax.ppermute(value, axis, [(i, i + by) for i in range(count - by)])
 
 
-def combine(earlier, later):
-    state = earlier[:STATE] * jnp.exp(later[STATE : STATE + 1]) + later[:STATE]
-    return jnp.concatenate([state, earlier[STATE:] + later[STATE:]], 0)
-
-
-def entering(summary, axis):
-    reach, window, before = 1, summary, None
-    while reach < lax.axis_size(axis):
-        got = shift(window, axis, reach)
-        before = got if before is None else combine(got, before)
-        if 2 * reach < lax.axis_size(axis):
-            window = combine(got, window)
-        reach *= 2
-    return before
+def entering(summary):
+    pair = [jax.ShapeDtypeStruct(summary.shape, F32)] * 2
+    steps = [shift(summary, "ctx", by) for by in (1, 2, 3)]
+    before, window = pl.pallas_call(first_kernel, out_shape=pair, compiler_params=WHOLE, name="first")(summary, *steps)
+    steps = [shift(window, "ctx", by) for by in (4, 8, 12)]
+    before, window = pl.pallas_call(second_kernel, out_shape=pair, compiler_params=WHOLE, name="second")(window, before, *steps)
+    return before, shift(window, "ctx", 16)
 
 
 def full(shape):
@@ -183,7 +191,8 @@
     return pl.BlockSpec((height, BLOCK), lambda k: (0, k))
 
 
-PARAMS = pltpu.CompilerParams(dimension_semantics=("arbitrary",), vmem_limit_bytes=40 << 20)
+WHOLE = pltpu.CompilerParams(vmem_limit_bytes=16 << 20)
+PARAMS = pltpu.CompilerParams(dimension_semantics=("arbitrary",), vmem_limit_bytes=16 << 20)
 
 
 def per_device(
@@ -194,25 +203,34 @@
     seg = rows * groups
     nblk = seg // BLOCK
     heads = dt_bias.shape[0]
-    x_parts = x_in.reshape(rows, groups, CHUNKS, LANES)
-
-    def to_groups(chunk):
-        part = lax.all_to_all(x_parts[:, :, chunk], "head", 1, 1, tiled=True)
-        return part.transpose(1, 0, 2).reshape(seg, LANES)
+
+    def to_groups(value):
+        return lax.all_to_all(value.transpose(1, 0, 2), "head", 1, 1, tiled=True).transpose(1, 0, 2)
 
     def to_tokens(value):
         part = value.reshape(groups, rows, LANES).transpose(1, 0, 2)
         return lax.all_to_all(part, "head", 1, 1, tiled=True).transpose(1, 0, 2)
 
-    gathered = lax.all_gather(jnp.concatenate([bc_in, dt_raw], 1), "head", axis=0, tiled=True)
-    x_seg = [to_groups(j) for j in range(CHUNKS)]
-
-    pick = (
-        jnp.arange(groups * heads)[None, :] == jnp.arange(heads)[:, None] + heads * lax.axis_index("head")
-    ).astype(BF16)
+    def pack(chunk, height, *values):
+        return pl.pallas_call(
+            lambda *refs: pack_kernel(chunk, *refs),
+            out_shape=jax.ShapeDtypeStruct((groups, height, LANES), BF16),
+            compiler_params=WHOLE,
+            name=f"pack{chunk}",
+        )(*values)
+
+    early = pack(0, rows + heads, x_in, dt_raw)
+    late = pack(1, rows, x_in)
+    early, late, bc_in = lax.optimization_barrier((early, late, bc_in))
+    first = to_groups(early)
+    gathered = lax.all_gather(bc_in, "head", axis=0, tiled=True)
+    first, gathered, late = lax.optimization_barrier((first, gathered, late))
+    second = to_groups(late)
+    x_seg = [first[:, :rows].reshape(seg, LANES), second.reshape(seg, LANES)]
+    dt_seg = first[:, rows:, :rows].transpose(1, 0, 2).reshape(heads, seg)
     par = jnp.stack([dt_bias, a_log])[:, :, None]
     par = jnp.broadcast_to(par, (2, heads, BLOCK))
-    bc_rim = shift(gathered[seg - RIM :, : 2 * STATE], "ctx", 1)
+    bc_rim = shift(gathered[seg - RIM :], "ctx", 1)
     c_mat, b_t, row_tab, col_tab = pl.pallas_call(
         prep_kernel,
         grid=(nblk,),
@@ -221,7 +239,7 @@
             full((RIM, 2 * STATE)),
             full((4, 2 * STATE)),
             full((1, 2 * STATE)),
-            full(pick.shape),
+            lanes_of(heads),
             full(par.shape),
         ],
         out_specs=[rows_of(STATE), lanes_of(STATE), lanes_of(3 * heads), rows_of(2 * heads)],
@@ -234,7 +252,7 @@
         scratch_shapes=[pltpu.VMEM((RIM, 2 * STATE), BF16)],
         compiler_params=PARAMS,
         name="prep",
-    )(gathered, bc_rim, conv_bc, bias_bc[None, :], pick, par)
+    )(gathered, bc_rim, conv_bc, bias_bc[None, :], dt_seg, par)
 
     y_tok = []
     for j in range(CHUNKS):
@@ -265,7 +283,7 @@
             compiler_params=PARAMS,
             name=f"state{j}",
         )(x_seg[j], rim, conv_x[:, at], bias_x[None, at], b_t, row_tab)
-        incoming = entering(summary, "ctx")
+        near, far = entering(summary)
         skip = jnp.repeat(d_skip[HEADS * j : HEADS * (j + 1)], WIDTH)[None, :]
         y_diag = pl.pallas_call(
             lambda *refs, j=j: diag_kernel(j, *refs),
@@ -292,30 +310,31 @@
                 rows_of(2 * heads),
                 pl.BlockSpec((1, STATE + 8, LANES), lambda k: (k, 0, 0)),
                 full((STATE + 8, LANES)),
+                full((STATE + 8, LANES)),
             ],
             out_specs=rows_of(LANES),
             out_shape=jax.ShapeDtypeStruct((seg, LANES), BF16),
             compiler_params=PARAMS,
             name=f"join{j}",
-        )(y_diag, c_mat, col_tab, local, incoming)
+        )(y_diag, c_mat, col_tab, local, near, far)
         y_tok.append(to_tokens(y))
 
-    gated, squares = pl.pallas_call(
-        gate_kernel,
-        out_shape=[
-            jax.ShapeDtypeStruct((groups, rows, LANES), F32),
-            jax.ShapeDtypeStruct((rows, 128), F32),
-        ],
-        compiler_params=pltpu.CompilerParams(vmem_limit_bytes=40 << 20),
-        name="gate",
-    )(y_tok[0], z_in)
+    step = 32
     return pl.pallas_call(
         norm_kernel,
+        grid=(rows // step,),
+        in_specs=[
+            pl.BlockSpec((groups, step, LANES), lambda k: (0, k, 0)),
+            pl.BlockSpec((groups, step, LANES), lambda k: (0, k, 0)),
+            pl.BlockSpec((step, z_in.shape[1]), lambda k: (k, 0)),
+            full((1, z_in.shape[1])),
+        ],
+        out_specs=pl.BlockSpec((step, z_in.shape[1]), lambda k: (k, 0)),
         out_shape=jax.ShapeDtypeStruct(z_in.shape, BF16),
-        scratch_shapes=[pltpu.VMEM((groups, rows, LANES), F32)],
-        compiler_params=pltpu.CompilerParams(vmem_limit_bytes=40 << 20),
+        scratch_shapes=[pltpu.VMEM((step, z_in.shape[1]), F32)],
+        compiler_params=PARAMS,
         name="norm",
-    )(y_tok[1], z_in, gated, squares, norm_gain[None, :])
+    )(y_tok[0], y_tok[1], z_in, norm_gain[None, :])
 
 
 def solution(mesh):

time: 335 us -> 285 us (0.85)
  the two profiles are of different devices: /device:TPU:4 before, /device:TPU:36 now
where the time goes in v2:
time: 285 us; the launch traced here: 284 us
  blocking collectives  118 us (41%)
  starting transfers between devices  76.7 us (27%)
  waiting for transfers between devices  52.7 us (18%)
  Pallas kernels  28.8 us (10%)
  local copies, waits for them, and re-layouts  6.8 us (2%)
    all_gather x1, blocking collectives, per_device(): gathered = lax.all_gather(bc_in, 'head', axis=0, tiled=True)  65.9 us
    ppermute x17, waiting for transfers between devices, shift(): return lax.ppermute(value, axis, [(i, i + by) for i in range(count - by)])  52.7 us
    all_to_all x1, blocking collectives, to_tokens(): return lax.all_to_all(part, 'head', 1, 1, tiled=True).transpose(1, 0, 2)  52.3 us
    ppermute x17, starting transfers between devices, shift(): return lax.ppermute(value, axis, [(i, i + by) for i in range(count - by)])  37.6 us
    all_to_all x2, starting transfers between devices, to_groups(): lax.all_to_all(value.transpose(1, 0, 2), 'head', 1, 1, tiled=True)  27.1 us
    all_to_all x1, starting transfers between devices, to_tokens(): return lax.all_to_all(part, 'head', 1, 1, tiled=True).transpose(1, 0, 2)  12 us
    pallas_call x2, Pallas kernels, per_device(): pl.pallas_call(lambda *refs, j=j: join_kernel(j, *refs), grid=(nblk,), in...  6.17 us
    unnamed x40, local copies, waits for them, and re-layouts  6.16 us
  transfers between devices with their start and end apart: 20, of which 15 were waited for; matrix products, arithmetic and copies ran while one was open for 0% of the time, Pallas kernels for 8%

profile of v2, /device:TPU:36, one launch (start us, length us, event | category | flops | bytes accessed | tf_op | source)
XLA Modules:
  0.0 283.5 jit_solution(4009803997556436938)
XLA Ops:
  0.0 1.4 copy-done
  1.4 1.0 pack1.1
  2.4 1.0 pack0.1
  3.4 15.2 %all-to-all-start = ((bf16[104,16,256]{2,0,1:T(8,128)(2,1)}), bf16[104,16,256]{2,0,1:T(8,128)(2,1)S(1)}, u32[]{:S(2)}, u32[]{:S(2)}) async-start(bf16[104,16,256]{2,0,1:T(8,128)(2,1)} %bitcast), calls=%async_computation | async-start | bytes 1703936 | tf_op jit(solution)/shard_map/all_to_all | solution.py:208
  18.6 65.9 %all_gather.3.g_ref = bf16[1536,256]{1,0:T(8,128)(2,1)S(1)} all-gather(bf16[96,256]{1,0:T(8,128)(2,1)S(1)} %copy-done.14), channel_id=1, replica_groups=mesh['ctx'=32,'head'=16] {'head'}, dimensions={0}, use_global_device_ids=true | all-gather | bytes 835584 | tf_op jit(solution)/shard_map/all_gather | solution.py:226
  84.5 11.8 %all-to-all-start.2 = ((bf16[96,16,256]{2,0,1:T(8,128)(2,1)}), bf16[96,16,256]{2,0,1:T(8,128)(2,1)S(1)}, u32[]{:S(2)}, u32[]{:S(2)}) async-start(bf16[96,16,256]{2,0,1:T(8,128)(2,1)} %bitcast.11), calls=%async_computation.2 | async-start | bytes 1572864 | tf_op jit(solution)/shard_map/all_to_all | solution.py:208
  97.4 1.9 collective-permute-start
  99.3 3.6 %collective-permute-start.1 = (bf16[16,256]{1,0:T(8,128)(2,1)S(1)}, bf16[16,256]{1,0:T(8,128)(2,1)S(1)}, u32[]{:S(2)}, u32[]{:S(2)}) collective-permute-start(bf16[16,256]{1,0:T(8,128)(2,1)S(1)} %slice.37), channel_id=1, source_target_pairs={{0,16},{16,32},{32,48},{48,64},{64,80},{80,96},{96,112},{112,128},... | collective-permute-start | bytes 24584 | tf_op jit(solution)/shard_map/ppermute | solution.py:170
  103.1 3.4 %collective-permute-done.1.rim_ref = bf16[16,256]{1,0:T(8,128)(2,1)S(1)} collective-permute-done((bf16[16,256]{1,0:T(8,128)(2,1)S(1)}, bf16[16,256]{1,0:T(8,128)(2,1)S(1)}, u32[]{:S(2)}, u32[]{:S(2)}) %collective-permute-start.1) | collective-permute-done | bytes 8224 | tf_op jit(solution)/shard_map/ppermute | solution.py:170
  106.5 5.1 %prep.1 = (bf16[1536,128]{1,0:T(8,128)(2,1)S(1)}, bf16[128,1536]{1,0:T(8,128)(2,1)S(1)}, f32[24,1536]{1,0:T(8,128)S(1)}, f32[1536,16]{1,0:T(8,128)S(1)}) custom-call(bf16[1536,256]{1,0:T(8,128)(2,1)S(1)} %all_gather.3.g_ref, bf16[16,256]{1,0:T(8,128)(2,1)S(1)} %collective-permute-done.1.rim_ref, f32[4,256]{1,0:T(4,128)S(1)} %copy-done.12, ...), custom_call_target="tpu_custom_call" | custom-call | tf_op jit(solution)/shard_map/prep/pallas_call | solution.py:234
  111.6 1.1 copy-done.2
  112.7 2.9 %state0.1 = (bf16[1536,256]{1,0:T(8,128)(2,1)S(1)}, f32[6,136,256]{2,1,0:T(8,128)S(1)}, f32[136,256]{1,0:T(8,128)S(1)}) custom-call(bf16[1536,256]{1,0:T(8,128)(2,1)S(1)} %bitcast.26, bf16[16,256]{1,0:T(8,128)(2,1)S(1)} %collective-permute-done.refs_1_, f32[4,256]{1,0:T(4,128)S(1)} %get-tuple-element.54.refs_2_, f32[1,256]{1,0:T(1,128)S(1)} %bitcast.32, ...), custom_call_target="tpu_custom_call" | custom-call | tf_op jit(solution)/shard_map/state0/pallas_call | solution.py:261
  116.6 1.9 collective-permute-start.2
  118.5 1.9 collective-permute-start.3
  120.4 3.6 %collective-permute-start.4 = (f32[136,256]{1,0:T(8,128)S(1)}, f32[136,256]{1,0:T(8,128)S(1)}, u32[]{:S(2)}, u32[]{:S(2)}) collective-permute-start(f32[136,256]{1,0:T(8,128)S(1)} %get-tuple-element.40.own_ref), channel_id=1, source_target_pairs={{0,48},{16,64},{32,80},{48,96},{64,112},{80,128},{96,144},{112,160... | collective-permute-start | bytes 417800 | tf_op jit(solution)/shard_map/ppermute | solution.py:170
  124.1 1.0 collective-permute-done.2.one_ref
  125.0 4.1 %collective-permute-done.3.two_ref = f32[136,256]{1,0:T(8,128)S(1)} collective-permute-done((f32[136,256]{1,0:T(8,128)S(1)}, f32[136,256]{1,0:T(8,128)S(1)}, u32[]{:S(2)}, u32[]{:S(2)}) %collective-permute-start.3) | collective-permute-done | bytes 139296 | tf_op jit(solution)/shard_map/ppermute | solution.py:170
  129.2 1.7 collective-permute-done.4.three_ref
  130.9 3.2 %collective-permute-start.5 = (f32[136,256]{1,0:T(8,128)S(1)}, f32[136,256]{1,0:T(8,128)S(1)}, u32[]{:S(2)}, u32[]{:S(2)}) collective-permute-start(f32[136,256]{1,0:T(8,128)S(1)} %get-tuple-element.41.own_ref), channel_id=1, source_target_pairs={{0,64},{16,80},{32,96},{48,112},{64,128},{80,144},{96,160},{112,17... | collective-permute-start | bytes 417800 | tf_op jit(solution)/shard_map/ppermute | solution.py:170
  134.2 3.0 %collective-permute-start.6 = (f32[136,256]{1,0:T(8,128)S(1)}, f32[136,256]{1,0:T(8,128)S(1)}, u32[]{:S(2)}, u32[]{:S(2)}) collective-permute-start(f32[136,256]{1,0:T(8,128)S(1)} %get-tuple-element.41.own_ref), channel_id=1, source_target_pairs={{0,128},{16,144},{32,160},{48,176},{64,192},{80,208},{96,224},{112... | collective-permute-start | bytes 417800 | tf_op jit(solution)/shard_map/ppermute | solution.py:170
  137.2 1.9 collective-permute-start.7
  139.1 2.5 collective-permute-done.5.one_ref
  141.9 6.2 %collective-permute-done.7.three_ref = f32[136,256]{1,0:T(8,128)S(1)} collective-permute-done((f32[136,256]{1,0:T(8,128)S(1)}, f32[136,256]{1,0:T(8,128)S(1)}, u32[]{:S(2)}, u32[]{:S(2)}) %collective-permute-start.7) | collective-permute-done | bytes 139296 | tf_op jit(solution)/shard_map/ppermute | solution.py:170
  148.7 1.3 collective-permute-start.8
  150.3 2.7 diag0.1.refs_0_
  152.9 4.6 %collective-permute-done.8.refs_5_ = f32[136,256]{1,0:T(8,128)} collective-permute-done((f32[136,256]{1,0:T(8,128)}, f32[136,256]{1,0:T(8,128)}, u32[]{:S(2)}, u32[]{:S(2)}) %collective-permute-start.8) | collective-permute-done | bytes 139296 | tf_op jit(solution)/shard_map/ppermute | solution.py:170
  157.5 3.8 %join0.1 = bf16[1536,256]{1,0:T(8,128)(2,1)} custom-call(f32[1536,256]{1,0:T(8,128)S(1)} %diag0.1.refs_0_, bf16[1536,128]{1,0:T(8,128)(2,1)S(1)} %get-tuple-element.37.refs_1_, f32[1536,16]{1,0:T(8,128)S(1)} %get-tuple-element.38.refs_4_.refs_2_, f32[6,136,256]{2,1,0:T(8,128)S(1)} %copy-done.7, f32[136,256]{1,0:T(8,128)S(1)} %get-tuple-element.43.refs_4_, ...), custom_call_target="tpu_custom_call" | custom-call | tf_op jit(solution)/shard_map/join0/pallas_call | solution.py:304
  161.3 12.0 %all-to-all-start.1 = ((bf16[96,16,256]{2,0,1:T(8,128)(2,1)}), bf16[96,16,256]{2,0,1:T(8,128)(2,1)S(1)}, u32[]{:S(2)}, u32[]{:S(2)}) async-start(bf16[96,16,256]{2,0,1:T(8,128)(2,1)} %bitcast.9), calls=%async_computation.1 | async-start | bytes 1572864 | tf_op jit(solution)/shard_map/all_to_all | solution.py:212
  173.3 1.9 collective-permute-start.9
  175.3 5.2 %collective-permute-done.9.refs_1_ = bf16[16,256]{1,0:T(8,128)(2,1)S(1)} collective-permute-done((bf16[16,256]{1,0:T(8,128)(2,1)S(1)}, bf16[16,256]{1,0:T(8,128)(2,1)S(1)}, u32[]{:S(2)}, u32[]{:S(2)}) %collective-permute-start.9) | collective-permute-done | bytes 8224 | tf_op jit(solution)/shard_map/ppermute | solution.py:170
  180.4 2.9 %state1.1 = (bf16[1536,256]{1,0:T(8,128)(2,1)S(1)}, f32[6,136,256]{2,1,0:T(8,128)S(1)}, f32[136,256]{1,0:T(8,128)S(1)}) custom-call(bf16[1536,256]{1,0:T(8,128)(2,1)S(1)} %bitcast.24, bf16[16,256]{1,0:T(8,128)(2,1)S(1)} %collective-permute-done.9.refs_1_, f32[4,256]{1,0:T(4,128)S(1)} %get-tuple-element.53.refs_2_, f32[1,256]{1,0:T(1,128)S(1)} %bitcast.31, ...), custom_call_target="tpu_custom_call" | custom-call | tf_op jit(solution)/shard_map/state1/pallas_call | solution.py:261
  185.2 2.0 collective-permute-start.10
  187.2 1.9 collective-permute-start.11
  189.2 1.9 collective-permute-start.12
  191.1 2.7 collective-permute-done.10.one_ref
  193.8 4.1 %collective-permute-done.11.two_ref = f32[136,256]{1,0:T(8,128)S(1)} collective-permute-done((f32[136,256]{1,0:T(8,128)S(1)}, f32[136,256]{1,0:T(8,128)S(1)}, u32[]{:S(2)}, u32[]{:S(2)}) %collective-permute-start.11) | collective-permute-done | bytes 139296 | tf_op jit(solution)/shard_map/ppermute | solution.py:170
  197.9 1.8 collective-permute-done.12.three_ref
  199.7 1.9 collective-permute-start.13
  201.7 2.3 collective-permute-start.14
  203.9 1.9 collective-permute-start.15
  205.9 4.7 %collective-permute-done.13.one_ref = f32[136,256]{1,0:T(8,128)S(1)} collective-permute-done((f32[136,256]{1,0:T(8,128)S(1)}, f32[136,256]{1,0:T(8,128)S(1)}, u32[]{:S(2)}, u32[]{:S(2)}) %collective-permute-start.13) | collective-permute-done | bytes 139296 | tf_op jit(solution)/shard_map/ppermute | solution.py:170
  210.6 5.8 %collective-permute-done.15.three_ref = f32[136,256]{1,0:T(8,128)S(1)} collective-permute-done((f32[136,256]{1,0:T(8,128)S(1)}, f32[136,256]{1,0:T(8,128)S(1)}, u32[]{:S(2)}, u32[]{:S(2)}) %collective-permute-start.15) | collective-permute-done | bytes 139296 | tf_op jit(solution)/shard_map/ppermute | solution.py:170
  217.1 1.3 collective-permute-start.16
  218.6 2.7 diag1.1.refs_0_
  221.2 4.8 %collective-permute-done.16.refs_5_ = f32[136,256]{1,0:T(8,128)} collective-permute-done((f32[136,256]{1,0:T(8,128)}, f32[136,256]{1,0:T(8,128)}, u32[]{:S(2)}, u32[]{:S(2)}) %collective-permute-start.16) | collective-permute-done | bytes 139296 | tf_op jit(solution)/shard_map/ppermute | solution.py:170
  226.0 2.4 join1.1
  228.4 52.3 %all_to_all.20 = bf16[96,16,256]{2,0,1:T(8,128)(2,1)S(1)} all-to-all(bf16[96,16,256]{2,0,1:T(8,128)(2,1)S(1)} %bitcast.28), channel_id=1, replica_groups=mesh['ctx'=32,'head'=16] {'head'}, dimensions={1} | all-to-all | bytes 1572864 | tf_op jit(solution)/shard_map/all_to_all | solution.py:212
  280.7 2.9 %norm.1 = bf16[96,8192]{1,0:T(8,128)(2,1)} custom-call(bf16[16,96,256]{2,1,0:T(8,128)(2,1)S(1)} %bitcast.27, bf16[16,96,256]{2,1,0:T(8,128)(2,1)S(1)} %bitcast.29, bf16[96,8192]{1,0:T(8,128)(2,1)S(1)} %copy-done.3, f32[1,8192]{1,0:T(1,128)S(1)} %bitcast.30), custom_call_target="tpu_custom_call" | custom-call | tf_op jit(solution)/shard_map/norm/pallas_call | solution.py:323
  (64 shorter events, 6.0 us)
Async XLA Ops:
  0.0 1.4 copy-start
  1.4 1.0 copy-start.11
  2.4 16.2 %copy-start.14 = (bf16[96,256]{1,0:T(8,128)(2,1)S(1)}, bf16[96,256]{1,0:T(8,128)(2,1)}, u32[]{:S(2)}) copy-start(bf16[96,256]{1,0:T(8,128)(2,1)} %param.14) | copy-start | bytes 147460
  3.4 81.1 %all-to-all-start = ((bf16[104,16,256]{2,0,1:T(8,128)(2,1)}), bf16[104,16,256]{2,0,1:T(8,128)(2,1)S(1)}, u32[]{:S(2)}, u32[]{:S(2)}) async-start(bf16[104,16,256]{2,0,1:T(8,128)(2,1)} %bitcast), calls=%async_computation | async-start | bytes 1703936 | tf_op jit(solution)/shard_map/all_to_all | solution.py:208
  18.6 77.8 %copy-start.18 = (f32[8]{0:T(128)S(1)}, f32[8]{0:T(128)}, u32[]{:S(2)}) copy-start(f32[8]{0:T(128)} %param.21) | copy-start | bytes 100
  18.6 77.8 %copy-start.19 = (f32[8]{0:T(128)S(1)}, f32[8]{0:T(128)}, u32[]{:S(2)}) copy-start(f32[8]{0:T(128)} %param.20) | copy-start | bytes 100
  18.6 77.8 %copy-start.16 = (f32[512]{0:T(512)S(1)}, f32[512]{0:T(512)}, u32[]{:S(2)}) copy-start(f32[512]{0:T(512)} %param.17) | copy-start | bytes 6148
  18.6 77.8 %copy-start.15 = (f32[4,512]{1,0:T(4,128)S(1)}, f32[4,512]{1,0:T(4,128)}, u32[]{:S(2)}) copy-start(f32[4,512]{1,0:T(4,128)} %param.16) | copy-start | bytes 24580
  84.5 22.0 %copy-start.12 = (f32[4,256]{1,0:T(4,128)S(1)}, f32[4,256]{1,0:T(4,128)}, u32[]{:S(2)}) copy-start(f32[4,256]{1,0:T(4,128)} %taps_ref.1) | copy-start | bytes 12292
  84.5 22.0 %copy-start.13 = (f32[256]{0:T(256)S(1)}, f32[256]{0:T(256)}, u32[]{:S(2)}) copy-start(f32[256]{0:T(256)} %param.19) | copy-start | bytes 3076
  84.5 76.8 %all-to-all-start.2 = ((bf16[96,16,256]{2,0,1:T(8,128)(2,1)}), bf16[96,16,256]{2,0,1:T(8,128)(2,1)S(1)}, u32[]{:S(2)}, u32[]{:S(2)}) async-start(bf16[96,16,256]{2,0,1:T(8,128)(2,1)} %bitcast.11), calls=%async_computation.2 | async-start | bytes 1572864 | tf_op jit(solution)/shard_map/all_to_all | solution.py:208
  96.5 0.9 copy-start.1
  97.4 14.2 %collective-permute-start = (bf16[16,256]{1,0:T(8,128)(2,1)S(1)}, bf16[16,256]{1,0:T(8,128)(2,1)S(1)}, u32[]{:S(2)}, u32[]{:S(2)}) collective-permute-start(bf16[16,256]{1,0:T(8,128)(2,1)S(1)} %slice.44), channel_id=1, source_target_pairs={{0,16},{16,32},{32,48},{48,64},{64,80},{80,96},{96,112},{112,128},... | collective-permute-start | bytes 24584 | tf_op jit(solution)/shard_map/ppermute | solution.py:170
  99.3 7.1 %collective-permute-start.1 = (bf16[16,256]{1,0:T(8,128)(2,1)S(1)}, bf16[16,256]{1,0:T(8,128)(2,1)S(1)}, u32[]{:S(2)}, u32[]{:S(2)}) collective-permute-start(bf16[16,256]{1,0:T(8,128)(2,1)S(1)} %slice.37), channel_id=1, source_target_pairs={{0,16},{16,32},{32,48},{48,64},{64,80},{80,96},{96,112},{112,128},... | collective-permute-start | bytes 24584 | tf_op jit(solution)/shard_map/ppermute | solution.py:170
  106.5 43.5 %copy-start.17 = (f32[8]{0:T(128)S(1)}, f32[8]{0:T(128)}, u32[]{:S(2)}) copy-start(f32[8]{0:T(128)} %param.22) | copy-start | bytes 100
  111.6 1.1 copy-start.2
  115.7 0.9 copy-start.6
  116.6 8.5 %collective-permute-start.2 = (f32[136,256]{1,0:T(8,128)S(1)}, f32[136,256]{1,0:T(8,128)S(1)}, u32[]{:S(2)}, u32[]{:S(2)}) collective-permute-start(f32[136,256]{1,0:T(8,128)S(1)} %get-tuple-element.40.own_ref), channel_id=1, source_target_pairs={{0,16},{16,32},{32,48},{48,64},{64,80},{80,96},{96,112},{112,128},... | collective-permute-start | bytes 417800 | tf_op jit(solution)/shard_map/ppermute | solution.py:170
  118.5 10.7 %collective-permute-start.3 = (f32[136,256]{1,0:T(8,128)S(1)}, f32[136,256]{1,0:T(8,128)S(1)}, u32[]{:S(2)}, u32[]{:S(2)}) collective-permute-start(f32[136,256]{1,0:T(8,128)S(1)} %get-tuple-element.40.own_ref), channel_id=1, source_target_pairs={{0,32},{16,48},{32,64},{48,80},{64,96},{80,112},{96,128},{112,144}... | collective-permute-start | bytes 417800 | tf_op jit(solution)/shard_map/ppermute | solution.py:170
  120.4 10.5 %collective-permute-start.4 = (f32[136,256]{1,0:T(8,128)S(1)}, f32[136,256]{1,0:T(8,128)S(1)}, u32[]{:S(2)}, u32[]{:S(2)}) collective-permute-start(f32[136,256]{1,0:T(8,128)S(1)} %get-tuple-element.40.own_ref), channel_id=1, source_target_pairs={{0,48},{16,64},{32,80},{48,96},{64,112},{80,128},{96,144},{112,160... | collective-permute-start | bytes 417800 | tf_op jit(solution)/shard_map/ppermute | solution.py:170
  130.9 10.7 %collective-permute-start.5 = (f32[136,256]{1,0:T(8,128)S(1)}, f32[136,256]{1,0:T(8,128)S(1)}, u32[]{:S(2)}, u32[]{:S(2)}) collective-permute-start(f32[136,256]{1,0:T(8,128)S(1)} %get-tuple-element.41.own_ref), channel_id=1, source_target_pairs={{0,64},{16,80},{32,96},{48,112},{64,128},{80,144},{96,160},{112,17... | collective-permute-start | bytes 417800 | tf_op jit(solution)/shard_map/ppermute | solution.py:170
  134.2 7.7 %collective-permute-start.6 = (f32[136,256]{1,0:T(8,128)S(1)}, f32[136,256]{1,0:T(8,128)S(1)}, u32[]{:S(2)}, u32[]{:S(2)}) collective-permute-start(f32[136,256]{1,0:T(8,128)S(1)} %get-tuple-element.41.own_ref), channel_id=1, source_target_pairs={{0,128},{16,144},{32,160},{48,176},{64,192},{80,208},{96,224},{112... | collective-permute-start | bytes 417800 | tf_op jit(solution)/shard_map/ppermute | solution.py:170
  137.2 10.9 %collective-permute-start.7 = (f32[136,256]{1,0:T(8,128)S(1)}, f32[136,256]{1,0:T(8,128)S(1)}, u32[]{:S(2)}, u32[]{:S(2)}) collective-permute-start(f32[136,256]{1,0:T(8,128)S(1)} %get-tuple-element.41.own_ref), channel_id=1, source_target_pairs={{0,192},{16,208},{32,224},{48,240},{64,256},{80,272},{96,288},{112... | collective-permute-start | bytes 417800 | tf_op jit(solution)/shard_map/ppermute | solution.py:170
  148.7 8.8 %collective-permute-start.8 = (f32[136,256]{1,0:T(8,128)}, f32[136,256]{1,0:T(8,128)}, u32[]{:S(2)}, u32[]{:S(2)}) collective-permute-start(f32[136,256]{1,0:T(8,128)} %get-tuple-element.44), channel_id=1, source_target_pairs={{0,256},{16,272},{32,288},{48,304},{64,320},{80,336},{96,352},{112... | collective-permute-start | bytes 417800 | tf_op jit(solution)/shard_map/ppermute | solution.py:170
  150.3 7.2 %copy-start.7 = (f32[6,136,256]{2,1,0:T(8,128)S(1)}, f32[6,136,256]{2,1,0:T(8,128)}, u32[]{:S(2)}) copy-start(f32[6,136,256]{2,1,0:T(8,128)} %copy-done.6) | copy-start | bytes 2506756
  161.3 67.1 %all-to-all-start.1 = ((bf16[96,16,256]{2,0,1:T(8,128)(2,1)}), bf16[96,16,256]{2,0,1:T(8,128)(2,1)S(1)}, u32[]{:S(2)}, u32[]{:S(2)}) async-start(bf16[96,16,256]{2,0,1:T(8,128)(2,1)} %bitcast.9), calls=%async_computation.1 | async-start | bytes 1572864 | tf_op jit(solution)/shard_map/all_to_all | solution.py:212
  173.3 7.1 %collective-permute-start.9 = (bf16[16,256]{1,0:T(8,128)(2,1)S(1)}, bf16[16,256]{1,0:T(8,128)(2,1)S(1)}, u32[]{:S(2)}, u32[]{:S(2)}) collective-permute-start(bf16[16,256]{1,0:T(8,128)(2,1)S(1)} %slice.45), channel_id=1, source_target_pairs={{0,16},{16,32},{32,48},{48,64},{64,80},{80,96},{96,112},{112,128},... | collective-permute-start | bytes 24584 | tf_op jit(solution)/shard_map/ppermute | solution.py:170
  183.4 0.9 copy-start.4
  184.3 0.9 copy-start.8
  185.2 33.4 %copy-start.9 = (bf16[1536,256]{1,0:T(8,128)(2,1)S(1)}, bf16[1536,256]{1,0:T(8,128)(2,1)}, u32[]{:S(2)}) copy-start(bf16[1536,256]{1,0:T(8,128)(2,1)} %copy-done.8) | copy-start | bytes 2359300
  185.2 8.6 %collective-permute-start.10 = (f32[136,256]{1,0:T(8,128)S(1)}, f32[136,256]{1,0:T(8,128)S(1)}, u32[]{:S(2)}, u32[]{:S(2)}) collective-permute-start(f32[136,256]{1,0:T(8,128)S(1)} %get-tuple-element.48.own_ref), channel_id=1, source_target_pairs={{0,16},{16,32},{32,48},{48,64},{64,80},{80,96},{96,112},{112,128},... | collective-permute-start | bytes 417800 | tf_op jit(solution)/shard_map/ppermute | solution.py:170
  187.2 10.7 %collective-permute-start.11 = (f32[136,256]{1,0:T(8,128)S(1)}, f32[136,256]{1,0:T(8,128)S(1)}, u32[]{:S(2)}, u32[]{:S(2)}) collective-permute-start(f32[136,256]{1,0:T(8,128)S(1)} %get-tuple-element.48.own_ref), channel_id=1, source_target_pairs={{0,32},{16,48},{32,64},{48,80},{64,96},{80,112},{96,128},{112,144}... | collective-permute-start | bytes 417800 | tf_op jit(solution)/shard_map/ppermute | solution.py:170
  189.2 10.5 %collective-permute-start.12 = (f32[136,256]{1,0:T(8,128)S(1)}, f32[136,256]{1,0:T(8,128)S(1)}, u32[]{:S(2)}, u32[]{:S(2)}) collective-permute-start(f32[136,256]{1,0:T(8,128)S(1)} %get-tuple-element.48.own_ref), channel_id=1, source_target_pairs={{0,48},{16,64},{32,80},{48,96},{64,112},{80,128},{96,144},{112,160... | collective-permute-start | bytes 417800 | tf_op jit(solution)/shard_map/ppermute | solution.py:170
  199.7 10.8 %collective-permute-start.13 = (f32[136,256]{1,0:T(8,128)S(1)}, f32[136,256]{1,0:T(8,128)S(1)}, u32[]{:S(2)}, u32[]{:S(2)}) collective-permute-start(f32[136,256]{1,0:T(8,128)S(1)} %get-tuple-element.49.own_ref), channel_id=1, source_target_pairs={{0,64},{16,80},{32,96},{48,112},{64,128},{80,144},{96,160},{112,17... | collective-permute-start | bytes 417800 | tf_op jit(solution)/shard_map/ppermute | solution.py:170
  201.7 8.9 %collective-permute-start.14 = (f32[136,256]{1,0:T(8,128)S(1)}, f32[136,256]{1,0:T(8,128)S(1)}, u32[]{:S(2)}, u32[]{:S(2)}) collective-permute-start(f32[136,256]{1,0:T(8,128)S(1)} %get-tuple-element.49.own_ref), channel_id=1, source_target_pairs={{0,128},{16,144},{32,160},{48,176},{64,192},{80,208},{96,224},{112... | collective-permute-start | bytes 417800 | tf_op jit(solution)/shard_map/ppermute | solution.py:170
  203.9 12.5 %collective-permute-start.15 = (f32[136,256]{1,0:T(8,128)S(1)}, f32[136,256]{1,0:T(8,128)S(1)}, u32[]{:S(2)}, u32[]{:S(2)}) collective-permute-start(f32[136,256]{1,0:T(8,128)S(1)} %get-tuple-element.49.own_ref), channel_id=1, source_target_pairs={{0,192},{16,208},{32,224},{48,240},{64,256},{80,272},{96,288},{112... | collective-permute-start | bytes 417800 | tf_op jit(solution)/shard_map/ppermute | solution.py:170
  217.1 8.9 %collective-permute-start.16 = (f32[136,256]{1,0:T(8,128)}, f32[136,256]{1,0:T(8,128)}, u32[]{:S(2)}, u32[]{:S(2)}) collective-permute-start(f32[136,256]{1,0:T(8,128)} %get-tuple-element.52), channel_id=1, source_target_pairs={{0,256},{16,272},{32,288},{48,304},{64,320},{80,336},{96,352},{112... | collective-permute-start | bytes 417800 | tf_op jit(solution)/shard_map/ppermute | solution.py:170
  218.6 7.5 %copy-start.5 = (f32[6,136,256]{2,1,0:T(8,128)S(1)}, f32[6,136,256]{2,1,0:T(8,128)}, u32[]{:S(2)}) copy-start(f32[6,136,256]{2,1,0:T(8,128)} %copy-done.4) | copy-start | bytes 2506756
  226.0 54.6 %copy-start.10 = (f32[8192]{0:T(1024)S(1)}, f32[8192]{0:T(1024)}, u32[]{:S(2)}) copy-start(f32[8192]{0:T(1024)} %param.23) | copy-start | bytes 98308
  228.4 52.3 %copy-start.3 = (bf16[96,8192]{1,0:T(8,128)(2,1)S(1)}, bf16[96,8192]{1,0:T(8,128)(2,1)}, u32[]{:S(2)}) copy-start(bf16[96,8192]{1,0:T(8,128)(2,1)} %z_ref.1) | copy-start | bytes 4718596

commit v3 on v2

v3 whole, which is shorter than its diff:
```python
import jax
import jax.numpy as jnp
from jax import lax
from jax.experimental import pallas as pl
from jax.experimental.pallas import tpu as pltpu
from jax.sharding import PartitionSpec as P

BLOCK = 256
STATE = 128
WIDTH = 64
HEADS = 8
LANES = HEADS * WIDTH
PART = 256
RIM = 16
F32 = jnp.float32
BF16 = jnp.bfloat16


def silu(u):
    return u / (1.0 + jnp.exp(-u))


def causal_conv(before, rows, taps, offset):
    count = rows.shape[0]
    padded = jnp.concatenate([before, rows], 0).astype(F32)
    summed = offset + taps[0:1] * padded[RIM - 3 : RIM - 3 + count]
    summed = summed + taps[1:2] * padded[RIM - 2 : RIM - 2 + count]
    summed = summed + taps[2:3] * padded[RIM - 1 : RIM - 1 + count]
    summed = summed + taps[3:4] * padded[RIM : RIM + count]
    return silu(summed).astype(BF16)


def pack_kernel(x_ref, dt_ref, out_ref):
    rows = x_ref.shape[0]
    dt = dt_ref[...].astype(F32).T.astype(BF16)
    for g in range(out_ref.shape[0]):
        out_ref[g, :rows] = x_ref[:, LANES * g : LANES * (g + 1)]
        out_ref[g, rows:, :rows] = dt[HEADS * g : HEADS * (g + 1)]
        out_ref[g, rows:, rows:] = jnp.zeros((HEADS, LANES - rows), BF16)


def prep_kernel(g_ref, rim_ref, taps_ref, bias_ref, dt_ref, par_ref, c_ref, bt_ref, rows_ref, cols_ref, carry):
    @pl.when(pl.program_id(0) == 0)
    def _():
        carry[...] = rim_ref[...]

    raw = g_ref[...]
    bcc = causal_conv(carry[...], raw, taps_ref[...], bias_ref[...])
    carry[...] = raw[BLOCK - RIM :]
    c_ref[...] = bcc[:, STATE:]
    bt_ref[...] = bcc[:, :STATE].astype(F32).T.astype(BF16)
    shifted = dt_ref[...].astype(F32) + par_ref[0]
    dt = jnp.maximum(shifted, 0.0) + jnp.log1p(jnp.exp(-jnp.abs(shifted)))
    cs = dt * -jnp.exp(par_ref[1])
    lane = lax.broadcasted_iota(jnp.int32, cs.shape, 1)
    step = 1
    while step < BLOCK:
        cs = cs + jnp.where(lane >= step, pltpu.roll(cs, step, 1), 0.0)
        step *= 2
    tot = cs[:, BLOCK - 1 :]
    rows_ref[0:8] = cs
    rows_ref[8:16] = dt
    rows_ref[16:24] = jnp.exp(tot - cs) * dt
    cols_ref[...] = jnp.concatenate([cs, jnp.exp(cs)], 0).T


def lane_pair(first, second, shape):
    lane = lax.broadcasted_iota(jnp.int32, shape, 1)
    return jnp.where(lane < WIDTH, first, second)


def state_kernel(x_ref, rim_ref, taps_ref, bias_ref, bt_ref, rows_ref, xc_ref, local_ref, part_ref, carry, run):
    @pl.when(pl.program_id(0) == 0)
    def _():
        carry[...] = rim_ref[...]
        run[...] = jnp.zeros_like(run)

    raw = x_ref[...]
    xc = causal_conv(carry[...], raw, taps_ref[...], bias_ref[...])
    carry[...] = raw[BLOCK - RIM :]
    xc_ref[...] = xc
    local_ref[0] = run[...]
    bt = bt_ref[...].astype(F32)
    for pair in range(HEADS // 2):
        cols = slice(2 * WIDTH * pair, 2 * WIDTH * (pair + 1))
        parts, tots = [], []
        for h in (2 * pair, 2 * pair + 1):
            bw = (bt * rows_ref[16 + h : 17 + h]).astype(BF16)
            parts.append(jnp.dot(bw, xc[:, cols], preferred_element_type=F32))
            tots.append(rows_ref[h : h + 1, BLOCK - 1 :])
        tot = lane_pair(tots[0], tots[1], (1, 2 * WIDTH))
        st = lane_pair(parts[0], parts[1], (STATE, 2 * WIDTH))
        run[:STATE, cols] = run[:STATE, cols] * jnp.exp(tot) + st
        run[STATE:, cols] = run[STATE:, cols] + tot

    @pl.when(pl.program_id(0) == pl.num_programs(0) - 1)
    def _():
        part_ref[...] = jnp.zeros_like(part_ref)
        for i in range(STATE // 8):
            for j in range(LANES // PART):
                p = i * (LANES // PART) + j
                part_ref[p, :, :PART] = run[8 * i : 8 * (i + 1), PART * j : PART * (j + 1)]
                for half in range(PART // 128):
                    start = PART * j + 128 * half
                    part_ref[p, half : half + 1, PART:] = run[STATE : STATE + 1, start : start + 128]


def scan_kernel(part_ref, out_ref):
    run = jnp.zeros(out_ref.shape[1:], F32)
    for s in range(part_ref.shape[0]):
        out_ref[s] = run
        gain = jnp.concatenate([part_ref[s, half : half + 1, PART:] for half in range(PART // 128)], 1)
        run = run * jnp.exp(gain) + part_ref[s, :, :PART]


def diag_kernel(xc_ref, c_ref, bt_ref, rows_ref, cols_ref, skip_ref, y_ref):
    half = BLOCK // 2
    xc = xc_ref[...]
    scores = jnp.dot(c_ref[...], bt_ref[...], preferred_element_type=F32)
    for low, width in ((0, half), (half, BLOCK)):
        part = scores[low : low + half, :width]
        row = lax.broadcasted_iota(jnp.int32, (half, width), 0) + low
        col = lax.broadcasted_iota(jnp.int32, (half, width), 1)
        keep = row >= col
        for pair in range(HEADS // 2):
            cols = slice(2 * WIDTH * pair, 2 * WIDTH * (pair + 1))
            outs = []
            for h in (2 * pair, 2 * pair + 1):
                gap = cols_ref[low : low + half, h : h + 1] - rows_ref[h : h + 1, :width]
                spread = jnp.exp(jnp.where(keep, gap, -1e30))
                m = (part * spread * rows_ref[8 + h : 9 + h, :width]).astype(BF16)
                outs.append(jnp.dot(m, xc[:width, cols], preferred_element_type=F32))
            y = lane_pair(outs[0], outs[1], (half, 2 * WIDTH))
            y_ref[low : low + half, cols] = (
                y + skip_ref[:, cols] * xc[low : low + half, cols].astype(F32)
            )


def join_kernel(yd_ref, c_ref, cols_ref, local_ref, in_ref, y_ref, entry):
    @pl.when(pl.program_id(0) == 0)
    def _():
        for i in range(STATE // 8):
            for j in range(LANES // PART):
                piece = in_ref[i * (LANES // PART) + j]
                entry[8 * i : 8 * (i + 1), PART * j : PART * (j + 1)] = piece

    hb = (entry[...] * jnp.exp(local_ref[0, STATE : STATE + 1]) + local_ref[0, :STATE]).astype(BF16)
    off = jnp.dot(c_ref[...], hb, preferred_element_type=F32)
    for pair in range(HEADS // 2):
        cols = slice(2 * WIDTH * pair, 2 * WIDTH * (pair + 1))
        h = 8 + 2 * pair
        scale = lane_pair(cols_ref[:, h : h + 1], cols_ref[:, h + 1 : h + 2], (BLOCK, 2 * WIDTH))
        y_ref[:, cols] = (yd_ref[:, cols] + off[:, cols] * scale).astype(BF16)


def norm_kernel(y_ref, z_ref, gain_ref, out_ref, gated_ref):
    groups = y_ref.shape[0]
    total = jnp.zeros((z_ref.shape[0], 128), F32)
    for g in range(groups):
        at = slice(LANES * g, LANES * (g + 1))
        gated = y_ref[g].astype(F32) * silu(z_ref[:, at].astype(F32))
        gated_ref[:, at] = gated
        sq = gated * gated
        for start in range(0, LANES, 128):
            total = total + sq[:, start : start + 128]
    mean = jnp.sum(total, axis=1, keepdims=True) * (1.0 / (groups * LANES))
    out_ref[...] = (gated_ref[...] * lax.rsqrt(mean + 1e-05) * gain_ref[...]).astype(BF16)


def shift(value, axis, by):
    count = lax.axis_size(axis)
    return lax.ppermute(value, axis, [(i, i + by) for i in range(count - by)])


def entering(parts):
    count, height, _ = parts.shape
    got = lax.all_to_all(parts, "ctx", 0, 0, tiled=True)
    before = pl.pallas_call(
        scan_kernel,
        out_shape=jax.ShapeDtypeStruct((count, height, PART), F32),
        compiler_params=WHOLE,
        name="scan",
    )(got)
    return lax.all_to_all(before, "ctx", 0, 0, tiled=True)


def full(shape):
    return pl.BlockSpec(shape, lambda k: tuple(0 for _ in shape))


def rows_of(width):
    return pl.BlockSpec((BLOCK, width), lambda k: (k, 0))


def lanes_of(height):
    return pl.BlockSpec((height, BLOCK), lambda k: (0, k))


WHOLE = pltpu.CompilerParams(vmem_limit_bytes=16 << 20)
PARAMS = pltpu.CompilerParams(dimension_semantics=("arbitrary",), vmem_limit_bytes=16 << 20)


def per_device(
    x_in, dt_raw, bc_in, z_in, conv_x, bias_x, conv_bc, bias_bc, dt_bias, a_log, d_skip, norm_gain
):
    groups = lax.axis_size("head")
    rows = x_in.shape[0]
    seg = rows * groups
    nblk = seg // BLOCK
    heads = dt_bias.shape[0]

    def exchange(value):
        return lax.all_to_all(value.transpose(1, 0, 2), "head", 1, 1, tiled=True).transpose(1, 0, 2)

    packed = pl.pallas_call(
        pack_kernel,
        out_shape=jax.ShapeDtypeStruct((groups, rows + heads, LANES), BF16),
        compiler_params=WHOLE,
        name="pack",
    )(x_in, dt_raw)
    packed, bc_in = lax.optimization_barrier((packed, bc_in))
    first = exchange(packed)
    gathered = lax.all_gather(bc_in, "head", axis=0, tiled=True)
    x_seg = first[:, :rows].reshape(seg, LANES)
    dt_seg = first[:, rows:, :rows].transpose(1, 0, 2).reshape(heads, seg)
    par = jnp.stack([dt_bias, a_log])[:, :, None]
    par = jnp.broadcast_to(par, (2, heads, BLOCK))
    bc_rim = shift(gathered[seg - RIM :], "ctx", 1)
    c_mat, b_t, row_tab, col_tab = pl.pallas_call(
        prep_kernel,
        grid=(nblk,),
        in_specs=[
            rows_of(gathered.shape[1]),
            full((RIM, 2 * STATE)),
            full((4, 2 * STATE)),
            full((1, 2 * STATE)),
            lanes_of(heads),
            full(par.shape),
        ],
        out_specs=[rows_of(STATE), lanes_of(STATE), lanes_of(3 * heads), rows_of(2 * heads)],
        out_shape=[
            jax.ShapeDtypeStruct((seg, STATE), BF16),
            jax.ShapeDtypeStruct((STATE, seg), BF16),
            jax.ShapeDtypeStruct((3 * heads, seg), F32),
            jax.ShapeDtypeStruct((seg, 2 * heads), F32),
        ],
        scratch_shapes=[pltpu.VMEM((RIM, 2 * STATE), BF16)],
        compiler_params=PARAMS,
        name="prep",
    )(gathered, bc_rim, conv_bc, bias_bc[None, :], dt_seg, par)

    rim = shift(x_seg[seg - RIM :], "ctx", 1)
    pieces = (STATE // 8) * (LANES // PART)
    xc, local, parts = pl.pallas_call(
        state_kernel,
        grid=(nblk,),
        in_specs=[
            rows_of(LANES),
            full((RIM, LANES)),
            full((4, LANES)),
            full((1, LANES)),
            lanes_of(STATE),
            lanes_of(3 * heads),
        ],
        out_specs=[
            rows_of(LANES),
            pl.BlockSpec((1, STATE + 8, LANES), lambda k: (k, 0, 0)),
            full((pieces, 8, PART + 128)),
        ],
        out_shape=[
            jax.ShapeDtypeStruct((seg, LANES), BF16),
            jax.ShapeDtypeStruct((nblk, STATE + 8, LANES), F32),
            jax.ShapeDtypeStruct((pieces, 8, PART + 128), F32),
        ],
        scratch_shapes=[pltpu.VMEM((RIM, LANES), BF16), pltpu.VMEM((STATE + 8, LANES), F32)],
        compiler_params=PARAMS,
        name="state",
    )(x_seg, rim, conv_x, bias_x[None, :], b_t, row_tab)
    incoming = entering(parts)
    skip = jnp.repeat(d_skip, WIDTH)[None, :]
    y_diag = pl.pallas_call(
        diag_kernel,
        grid=(nblk,),
        in_specs=[
            rows_of(LANES),
            rows_of(STATE),
            lanes_of(STATE),
            lanes_of(3 * heads),
            rows_of(2 * heads),
            full((1, LANES)),
        ],
        out_specs=rows_of(LANES),
        out_shape=jax.ShapeDtypeStruct((seg, LANES), F32),
        compiler_params=PARAMS,
        name="diag",
    )(xc, c_mat, b_t, row_tab, col_tab, skip)
    y = pl.pallas_call(
        join_kernel,
        grid=(nblk,),
        in_specs=[
            rows_of(LANES),
            rows_of(STATE),
            rows_of(2 * heads),
            pl.BlockSpec((1, STATE + 8, LANES), lambda k: (k, 0, 0)),
            full((pieces, 8, PART)),
        ],
        out_specs=rows_of(LANES),
        out_shape=jax.ShapeDtypeStruct((seg, LANES), BF16),
        scratch_shapes=[pltpu.VMEM((STATE, LANES), F32)],
        compiler_params=PARAMS,
        name="join",
    )(y_diag, c_mat, col_tab, local, incoming)
    y_tok = exchange(y.reshape(groups, rows, LANES))
    step = 32
    return pl.pallas_call(
        norm_kernel,
        grid=(rows // step,),
        in_specs=[
            pl.BlockSpec((groups, step, LANES), lambda k: (0, k, 0)),
            pl.BlockSpec((step, z_in.shape[1]), lambda k: (k, 0)),
            full((1, z_in.shape[1])),
        ],
        out_specs=pl.BlockSpec((step, z_in.shape[1]), lambda k: (k, 0)),
        out_shape=jax.ShapeDtypeStruct(z_in.shape, BF16),
        scratch_shapes=[pltpu.VMEM((step, z_in.shape[1]), F32)],
        compiler_params=PARAMS,
        name="norm",
    )(y_tok, z_in, norm_gain[None, :])


def solution(mesh):
    token = P(("ctx", "head"), None)
    in_specs = (
        token,
        token,
        token,
        token,
        P(None, "head"),
        P("head"),
        P(),
        P(),
        P("head"),
        P("head"),
        P("head"),
        P(),
    )
    return jax.shard_map(per_device, mesh=mesh, in_specs=in_specs, out_specs=token, check_vma=False)
```

time: 285 us -> 272 us (0.954)
  the two profiles are of different devices: /device:TPU:36 before, /device:TPU:32 now
where the time goes in v3:
time: 272 us; the launch traced here: 271 us
  blocking collectives  206 us (76%)
  starting transfers between devices  25.4 us (9%)
  Pallas kernels  22.2 us (8%)
  local copies, waits for them, and re-layouts  16.9 us (6%)
    all_gather x1, blocking collectives, per_device(): gathered = lax.all_gather(bc_in, 'head', axis=0, tiled=True)  103 us
    all_to_all x1, blocking collectives, exchange(): lax.all_to_all(value.transpose(1, 0, 2), 'head', 1, 1, tiled=True)  86 us
    all_to_all x1, blocking collectives, entering(): got = lax.all_to_all(parts, 'ctx', 0, 0, tiled=True)  16.8 us
    all_to_all x1, starting transfers between devices, exchange(): lax.all_to_all(value.transpose(1, 0, 2), 'head', 1, 1, tiled=True)  15.4 us
    unnamed x48, local copies, waits for them, and re-layouts  14.2 us
    ppermute x2, starting transfers between devices, shift(): return lax.ppermute(value, axis, [(i, i + by) for i in range(count - by)])  5.49 us
  transfers between devices with their start and end apart: 4, of which 1 were waited for; matrix products, arithmetic and copies ran while one was open for 1% of the time, Pallas kernels for 3%

profile of v3, /device:TPU:32, one launch (start us, length us, event | category | flops | bytes accessed | tf_op | source)
XLA Modules:
  0.0 270.6 jit_solution(2127192302874062883)
XLA Ops:
  0.0 1.4 copy-done.5
  1.4 0.7 copy-done.15
  2.1 1.3 pack.1
  3.5 15.4 %all-to-all-start = ((bf16[104,16,512]{2,0,1:T(8,128)(2,1)}), bf16[104,16,512]{2,0,1:T(8,128)(2,1)}, u32[]{:S(2)}, u32[]{:S(2)}) async-start(bf16[104,16,512]{2,0,1:T(8,128)(2,1)} %bitcast), calls=%async_computation | async-start | bytes 3407872 | tf_op jit(solution)/shard_map/all_to_all | solution.py:213
  18.8 0.0 copy-done.20
  18.8 102.8 %all_gather.3.g_ref = bf16[1536,256]{1,0:T(8,128)(2,1)S(1)} all-gather(bf16[96,256]{1,0:T(8,128)(2,1)S(1)} %copy-done.20), channel_id=1, replica_groups=mesh['ctx'=32,'head'=16] {'head'}, dimensions={0}, use_global_device_ids=true | all-gather | bytes 835584 | tf_op jit(solution)/shard_map/all_gather | solution.py:223
  121.6 1.3 collective-permute-start.1
  123.0 0.0 all-to-all-done
  123.0 0.0 copy-start.17
  123.0 0.0 copy-start.19
  123.0 0.0 copy-start.16
  123.0 0.0 copy-start.18
  123.0 1.6 slice.16
  124.6 4.2 %collective-permute-start = (bf16[16,512]{1,0:T(8,128)(2,1)S(1)}, bf16[16,512]{1,0:T(8,128)(2,1)S(1)}, u32[]{:S(2)}, u32[]{:S(2)}) collective-permute-start(bf16[16,512]{1,0:T(8,128)(2,1)S(1)} %slice.17), channel_id=1, source_target_pairs={{0,16},{16,32},{32,48},{48,64},{64,80},{80,96},{96,112},{112,128},... | collective-permute-start | bytes 49160 | tf_op jit(solution)/shard_map/ppermute | solution.py:172
  128.8 0.8 slice_bitcast_fusion
  129.6 0.1 reshape.11.dt_ref
  129.7 0.0 collective-permute-done.1.rim_ref
  129.7 0.1 broadcast_in_dim.20.par_ref
  129.8 0.0 copy-done.19
  129.8 5.0 %prep.1 = (bf16[1536,128]{1,0:T(8,128)(2,1)S(1)}, bf16[128,1536]{1,0:T(8,128)(2,1)S(1)}, f32[24,1536]{1,0:T(8,128)S(1)}, f32[1536,16]{1,0:T(8,128)S(1)}) custom-call(bf16[1536,256]{1,0:T(8,128)(2,1)S(1)} %all_gather.3.g_ref, bf16[16,256]{1,0:T(8,128)(2,1)S(1)} %collective-permute-done.1.rim_ref, f32[4,256]{1,0:T(4,128)S(1)} %copy-done.17, ...), custom_call_target="tpu_custom_call" | custom-call | tf_op jit(solution)/shard_map/prep/pallas_call | solution.py:229
  134.8 0.9 copy-done
  135.7 0.8 copy-done.9
  136.5 0.0 collective-permute-done.rim_ref
  136.5 0.0 copy-done.16
  136.5 0.0 copy-start.21
  136.5 5.1 %state.1 = (bf16[1536,512]{1,0:T(8,128)(2,1)S(1)}, f32[6,136,512]{2,1,0:T(8,128)S(1)}, f32[32,8,384]{2,1,0:T(8,128)S(1)}) custom-call(bf16[1536,512]{1,0:T(8,128)(2,1)S(1)} %bitcast.15, bf16[16,512]{1,0:T(8,128)(2,1)S(1)} %collective-permute-done.rim_ref, f32[4,512]{1,0:T(4,128)S(1)} %copy-done.16, f32[1,512]{1,0:T(1,128)S(1)} %bitcast.19, ...), custom_call_target="tpu_custom_call" | custom-call | tf_op jit(solution)/shard_map/state/pallas_call | solution.py:254
  141.6 1.2 copy-done.3
  142.8 1.1 copy-done.7
  143.9 16.8 %all_to_all.20.part_ref = f32[32,8,384]{2,1,0:T(8,128)S(1)} all-to-all(f32[32,8,384]{2,1,0:T(8,128)S(1)} %get-tuple-element.22), channel_id=1, replica_groups=mesh['ctx'=32,'head'=16] {'ctx'}, dimensions={0} | all-to-all | bytes 786432 | tf_op jit(solution)/shard_map/all_to_all | solution.py:177
  160.7 0.8 scan.1
  161.5 0.0 copy-done.12
  161.5 4.6 %all-to-all-start.2 = ((f32[32,8,256]{2,1,0:T(8,128)}), f32[32,8,256]{2,1,0:T(8,128)}, u32[]{:S(2)}, u32[]{:S(2)}) async-start(f32[32,8,256]{2,1,0:T(8,128)} %scan.1), calls=%async_computation.2 | async-start | bytes 524288 | tf_op jit(solution)/shard_map/all_to_all | solution.py:184
  166.1 0.1 broadcast_in_dim.21
  166.2 0.1 broadcast_in_dim_reshape.3.skip_ref
  166.3 1.1 copy-done.1
  167.4 1.4 copy-done.8
  168.8 1.0 copy-done.10
  169.8 0.9 copy-done.13
  170.7 3.9 %diag.1.yd_ref = f32[1536,512]{1,0:T(8,128)S(1)} custom-call(bf16[1536,512]{1,0:T(8,128)(2,1)S(1)} %copy-done.8, bf16[1536,128]{1,0:T(8,128)(2,1)S(1)} %copy-done.10, bf16[128,1536]{1,0:T(8,128)(2,1)S(1)} %get-tuple-element.16.bt_ref, f32[24,1536]{1,0:T(8,128)S(1)} %copy-done.13, f32[1536,16]{1,0:T(8,128)S(1)} %copy-done.1, ...), custom_call_target="tpu_custom_call" | custom-call | tf_op jit(solution)/shard_map/diag/pallas_call | solution.py:281
  174.6 0.4 all-to-all-done.2.in_ref
  175.0 1.1 copy-done.2
  176.1 1.4 copy-done.4
  177.6 1.0 copy-done.11
  178.6 3.2 %join.1 = bf16[1536,512]{1,0:T(8,128)(2,1)S(1)} custom-call(f32[1536,512]{1,0:T(8,128)S(1)} %diag.1.yd_ref, bf16[1536,128]{1,0:T(8,128)(2,1)S(1)} %copy-done.11, f32[1536,16]{1,0:T(8,128)S(1)} %copy-done.2, f32[6,136,512]{2,1,0:T(8,128)S(1)} %copy-done.4, f32[32,8,256]{2,1,0:T(8,128)} %all-to-all-done.2.in_ref), custom_call_target="tpu_custom_call" | custom-call | tf_op jit(solution)/shard_map/join/pallas_call | solution.py:297
  181.8 0.0 copy-start.6
  181.8 0.0 copy-start.14
  181.8 86.0 %all_to_all.21 = bf16[96,16,512]{2,0,1:T(8,128)(2,1)S(1)} all-to-all(bf16[96,16,512]{2,0,1:T(8,128)(2,1)S(1)} %bitcast.17), channel_id=1, replica_groups=mesh['ctx'=32,'head'=16] {'head'}, dimensions={1} | all-to-all | bytes 3145728 | tf_op jit(solution)/shard_map/all_to_all | solution.py:213
  267.8 2.9 %norm.1 = bf16[96,8192]{1,0:T(8,128)(2,1)} custom-call(bf16[16,96,512]{2,1,0:T(8,128)(2,1)S(1)} %bitcast.16, bf16[96,8192]{1,0:T(8,128)(2,1)S(1)} %copy-done.6, f32[1,8192]{1,0:T(1,128)S(1)} %bitcast.18), custom_call_target="tpu_custom_call" | custom-call | tf_op jit(solution)/shard_map/norm/pallas_call | solution.py:315
  (28 shorter events, 0.1 us)
Async XLA Ops:
  0.0 1.4 copy-start.5
  1.4 0.7 copy-start.15
  3.5 15.4 %copy-start.20 = (bf16[96,256]{1,0:T(8,128)(2,1)S(1)}, bf16[96,256]{1,0:T(8,128)(2,1)}, u32[]{:S(2)}) copy-start(bf16[96,256]{1,0:T(8,128)(2,1)} %param.14) | copy-start | bytes 147460
  3.5 119.5 %copy-start.22 = (f32[8]{0:T(128)S(1)}, f32[8]{0:T(128)}, u32[]{:S(2)}) copy-start(f32[8]{0:T(128)} %param.21) | copy-start | bytes 100
  3.5 119.5 %copy-start.23 = (f32[8]{0:T(128)S(1)}, f32[8]{0:T(128)}, u32[]{:S(2)}) copy-start(f32[8]{0:T(128)} %param.20) | copy-start | bytes 100
  3.5 119.5 %all-to-all-start = ((bf16[104,16,512]{2,0,1:T(8,128)(2,1)}), bf16[104,16,512]{2,0,1:T(8,128)(2,1)}, u32[]{:S(2)}, u32[]{:S(2)}) async-start(bf16[104,16,512]{2,0,1:T(8,128)(2,1)} %bitcast), calls=%async_computation | async-start | bytes 3407872 | tf_op jit(solution)/shard_map/all_to_all | solution.py:213
  121.6 8.1 %collective-permute-start.1 = (bf16[16,256]{1,0:T(8,128)(2,1)S(1)}, bf16[16,256]{1,0:T(8,128)(2,1)S(1)}, u32[]{:S(2)}, u32[]{:S(2)}) collective-permute-start(bf16[16,256]{1,0:T(8,128)(2,1)S(1)} %slice.18), channel_id=1, source_target_pairs={{0,16},{16,32},{32,48},{48,64},{64,80},{80,96},{96,112},{112,128},... | collective-permute-start | bytes 24584 | tf_op jit(solution)/shard_map/ppermute | solution.py:172
  123.0 6.8 %copy-start.17 = (f32[4,256]{1,0:T(4,128)S(1)}, f32[4,256]{1,0:T(4,128)}, u32[]{:S(2)}) copy-start(f32[4,256]{1,0:T(4,128)} %taps_ref.2) | copy-start | bytes 12292
  123.0 6.8 %copy-start.19 = (f32[256]{0:T(256)S(1)}, f32[256]{0:T(256)}, u32[]{:S(2)}) copy-start(f32[256]{0:T(256)} %param.19) | copy-start | bytes 3076
  123.0 13.5 %copy-start.16 = (f32[4,512]{1,0:T(4,128)S(1)}, f32[4,512]{1,0:T(4,128)}, u32[]{:S(2)}) copy-start(f32[4,512]{1,0:T(4,128)} %taps_ref.3) | copy-start | bytes 24580
  123.0 13.5 %copy-start.18 = (f32[512]{0:T(512)S(1)}, f32[512]{0:T(512)}, u32[]{:S(2)}) copy-start(f32[512]{0:T(512)} %param.17) | copy-start | bytes 6148
  124.6 11.9 %collective-permute-start = (bf16[16,512]{1,0:T(8,128)(2,1)S(1)}, bf16[16,512]{1,0:T(8,128)(2,1)S(1)}, u32[]{:S(2)}, u32[]{:S(2)}) collective-permute-start(bf16[16,512]{1,0:T(8,128)(2,1)S(1)} %slice.17), channel_id=1, source_target_pairs={{0,16},{16,32},{32,48},{48,64},{64,80},{80,96},{96,112},{112,128},... | collective-permute-start | bytes 49160 | tf_op jit(solution)/shard_map/ppermute | solution.py:172
  134.8 0.9 copy-start
  135.7 0.8 copy-start.9
  136.5 25.0 %copy-start.12 = (f32[24,1536]{1,0:T(8,128)}, f32[24,1536]{1,0:T(8,128)S(1)}, u32[]{:S(2)}) copy-start(f32[24,1536]{1,0:T(8,128)S(1)} %get-tuple-element.17.rows_ref) | copy-start | bytes 442372
  136.5 29.6 %copy-start.21 = (f32[8]{0:T(128)S(1)}, f32[8]{0:T(128)}, u32[]{:S(2)}) copy-start(f32[8]{0:T(128)} %param.22) | copy-start | bytes 100
  141.6 1.2 copy-start.3
  142.8 1.1 copy-start.7
  161.5 13.5 %all-to-all-start.2 = ((f32[32,8,256]{2,1,0:T(8,128)}), f32[32,8,256]{2,1,0:T(8,128)}, u32[]{:S(2)}, u32[]{:S(2)}) async-start(f32[32,8,256]{2,1,0:T(8,128)} %scan.1), calls=%async_computation.2 | async-start | bytes 524288 | tf_op jit(solution)/shard_map/all_to_all | solution.py:184
  166.3 1.1 copy-start.1
  167.4 1.4 copy-start.8
  168.8 1.0 copy-start.10
  169.8 0.9 copy-start.13
  175.0 1.1 copy-start.2
  176.1 1.4 copy-start.4
  177.6 1.0 copy-start.11
  181.8 86.0 %copy-start.6 = (bf16[96,8192]{1,0:T(8,128)(2,1)S(1)}, bf16[96,8192]{1,0:T(8,128)(2,1)}, u32[]{:S(2)}) copy-start(bf16[96,8192]{1,0:T(8,128)(2,1)} %z_ref.1) | copy-start | bytes 4718596
  181.8 86.0 %copy-start.14 = (f32[8192]{0:T(1024)S(1)}, f32[8192]{0:T(1024)}, u32[]{:S(2)}) copy-start(f32[8192]{0:T(1024)} %param.23) | copy-start | bytes 98308

commit v4 on v3

--- a/solution.py
+++ b/solution.py
@@ -11,7 +11,7 @@
 HEADS = 8
 LANES = HEADS * WIDTH
 PART = 256
-RIM = 16
+RIM = 8
 F32 = jnp.float32
 BF16 = jnp.bfloat16
 
@@ -22,7 +22,7 @@
 
 def causal_conv(before, rows, taps, offset):
     count = rows.shape[0]
-    padded = jnp.concatenate([before, rows], 0).astype(F32)
+    padded = jnp.concatenate([before, rows.astype(F32)], 0)
     summed = offset + taps[0:1] * padded[RIM - 3 : RIM - 3 + count]
     summed = summed + taps[1:2] * padded[RIM - 2 : RIM - 2 + count]
     summed = summed + taps[2:3] * padded[RIM - 1 : RIM - 1 + count]
@@ -30,38 +30,44 @@
     return silu(summed).astype(BF16)
 
 
-def pack_kernel(x_ref, dt_ref, out_ref):
+def pack_kernel(x_ref, dt_ref, tail_ref, out_ref):
     rows = x_ref.shape[0]
-    dt = dt_ref[...].astype(F32).T.astype(BF16)
+    dt = dt_ref[...].astype(F32).T
+    wide = LANES - 128
+    row = lax.broadcasted_iota(jnp.int32, (RIM, wide), 0)
     for g in range(out_ref.shape[0]):
-        out_ref[g, :rows] = x_ref[:, LANES * g : LANES * (g + 1)]
-        out_ref[g, rows:, :rows] = dt[HEADS * g : HEADS * (g + 1)]
-        out_ref[g, rows:, rows:] = jnp.zeros((HEADS, LANES - rows), BF16)
-
-
-def prep_kernel(g_ref, rim_ref, taps_ref, bias_ref, dt_ref, par_ref, c_ref, bt_ref, rows_ref, cols_ref, carry):
+        start = LANES * g
+        out_ref[g, :rows] = x_ref[:, start : start + LANES]
+        tail = tail_ref[:, start : start + LANES].astype(F32)
+        rest = jnp.concatenate([tail[:, wide:], jnp.zeros((RIM, wide - 128), F32)], 1)
+        spare = jnp.where(row < 6, pltpu.roll(rest, 6, 0), 0.0)
+        spare = jnp.where(row < 3, pltpu.roll(tail[:, :wide], 3, 0), spare)
+        head = jnp.concatenate([dt[HEADS * g : HEADS * (g + 1)], jnp.zeros((HEADS, 128 - rows), F32)], 1)
+        out_ref[g, rows:] = jnp.concatenate([head, spare], 1).astype(BF16)
+
+
+def prep_kernel(g_ref, rim_ref, taps_ref, bias_ref, c_ref, bt_ref, carry):
     @pl.when(pl.program_id(0) == 0)
     def _():
-        carry[...] = rim_ref[...]
+        carry[...] = rim_ref[...].astype(F32)
 
     raw = g_ref[...]
     bcc = causal_conv(carry[...], raw, taps_ref[...], bias_ref[...])
-    carry[...] = raw[BLOCK - RIM :]
+    carry[...] = raw[BLOCK - RIM :].astype(F32)
     c_ref[...] = bcc[:, STATE:]
     bt_ref[...] = bcc[:, :STATE].astype(F32).T.astype(BF16)
-    shifted = dt_ref[...].astype(F32) + par_ref[0]
+
+
+def step_tables(dt_raw, par):
+    shifted = dt_raw.astype(F32) + par[0]
     dt = jnp.maximum(shifted, 0.0) + jnp.log1p(jnp.exp(-jnp.abs(shifted)))
-    cs = dt * -jnp.exp(par_ref[1])
+    cs = dt * -jnp.exp(par[1])
     lane = lax.broadcasted_iota(jnp.int32, cs.shape, 1)
     step = 1
     while step < BLOCK:
         cs = cs + jnp.where(lane >= step, pltpu.roll(cs, step, 1), 0.0)
         step *= 2
-    tot = cs[:, BLOCK - 1 :]
-    rows_ref[0:8] = cs
-    rows_ref[8:16] = dt
-    rows_ref[16:24] = jnp.exp(tot - cs) * dt
-    cols_ref[...] = jnp.concatenate([cs, jnp.exp(cs)], 0).T
+    return cs, dt
 
 
 def lane_pair(first, second, shape):
@@ -69,15 +75,26 @@
     return jnp.where(lane < WIDTH, first, second)
 
 
-def state_kernel(x_ref, rim_ref, taps_ref, bias_ref, bt_ref, rows_ref, xc_ref, local_ref, part_ref, carry, run):
+def state_kernel(
+    x_ref, spare_ref, taps_ref, bias_ref, bt_ref, dt_ref, par_ref,
+    xc_ref, local_ref, part_ref, rows_ref, cols_ref, carry, run
+):
     @pl.when(pl.program_id(0) == 0)
     def _():
-        carry[...] = rim_ref[...]
+        spare = spare_ref[...].astype(F32)
+        most = pltpu.roll(spare[:, 128:], 5, 0)
+        rest = pltpu.roll(spare[:, 128:256], 2, 0)
+        carry[...] = jnp.concatenate([most, rest], 1)
         run[...] = jnp.zeros_like(run)
 
+    cs, dt = step_tables(dt_ref[...], par_ref)
+    weight = jnp.exp(cs[:, BLOCK - 1 :] - cs) * dt
+    rows_ref[:HEADS] = cs
+    rows_ref[HEADS:] = dt
+    cols_ref[...] = jnp.concatenate([cs, jnp.exp(cs)], 0).T
     raw = x_ref[...]
     xc = causal_conv(carry[...], raw, taps_ref[...], bias_ref[...])
-    carry[...] = raw[BLOCK - RIM :]
+    carry[...] = raw[BLOCK - RIM :].astype(F32)
     xc_ref[...] = xc
     local_ref[0] = run[...]
     bt = bt_ref[...].astype(F32)
@@ -85,9 +102,9 @@
         cols = slice(2 * WIDTH * pair, 2 * WIDTH * (pair + 1))
         parts, tots = [], []
         for h in (2 * pair, 2 * pair + 1):
-            bw = (bt * rows_ref[16 + h : 17 + h]).astype(BF16)
+            bw = (bt * weight[h : h + 1]).astype(BF16)
             parts.append(jnp.dot(bw, xc[:, cols], preferred_element_type=F32))
-            tots.append(rows_ref[h : h + 1, BLOCK - 1 :])
+            tots.append(cs[h : h + 1, BLOCK - 1 :])
         tot = lane_pair(tots[0], tots[1], (1, 2 * WIDTH))
         st = lane_pair(parts[0], parts[1], (STATE, 2 * WIDTH))
         run[:STATE, cols] = run[:STATE, cols] * jnp.exp(tot) + st
@@ -153,12 +170,16 @@
         y_ref[:, cols] = (yd_ref[:, cols] + off[:, cols] * scale).astype(BF16)
 
 
-def norm_kernel(y_ref, z_ref, gain_ref, out_ref, gated_ref):
+def gate_kernel(z_ref, out_ref):
+    out_ref[...] = silu(z_ref[...].astype(F32))
+
+
+def norm_kernel(y_ref, gate_ref, gain_ref, out_ref, gated_ref):
     groups = y_ref.shape[0]
-    total = jnp.zeros((z_ref.shape[0], 128), F32)
+    total = jnp.zeros((gate_ref.shape[0], 128), F32)
     for g in range(groups):
         at = slice(LANES * g, LANES * (g + 1))
-        gated = y_ref[g].astype(F32) * silu(z_ref[:, at].astype(F32))
+        gated = y_ref[g].astype(F32) * gate_ref[:, at]
         gated_ref[:, at] = gated
         sq = gated * gated
         for start in range(0, LANES, 128):
@@ -184,6 +205,10 @@
     return lax.all_to_all(before, "ctx", 0, 0, tiled=True)
 
 
+def held(value):
+    return pltpu.with_memory_space_constraint(value, pltpu.HBM)
+
+
 def full(shape):
     return pl.BlockSpec(shape, lambda k: tuple(0 for _ in shape))
 
@@ -212,46 +237,38 @@
     def exchange(value):
         return lax.all_to_all(value.transpose(1, 0, 2), "head", 1, 1, tiled=True).transpose(1, 0, 2)
 
+    tail = shift(x_in[rows - RIM :], "ctx", 1)
+    gathered = lax.all_gather(bc_in, "head", axis=0, tiled=True)
+    tail, gathered = lax.optimization_barrier((tail, gathered))
     packed = pl.pallas_call(
         pack_kernel,
-        out_shape=jax.ShapeDtypeStruct((groups, rows + heads, LANES), BF16),
+        out_shape=jax.ShapeDtypeStruct((groups, rows + RIM, LANES), BF16),
         compiler_params=WHOLE,
         name="pack",
-    )(x_in, dt_raw)
-    packed, bc_in = lax.optimization_barrier((packed, bc_in))
+    )(x_in, dt_raw, tail)
     first = exchange(packed)
-    gathered = lax.all_gather(bc_in, "head", axis=0, tiled=True)
     x_seg = first[:, :rows].reshape(seg, LANES)
     dt_seg = first[:, rows:, :rows].transpose(1, 0, 2).reshape(heads, seg)
     par = jnp.stack([dt_bias, a_log])[:, :, None]
     par = jnp.broadcast_to(par, (2, heads, BLOCK))
     bc_rim = shift(gathered[seg - RIM :], "ctx", 1)
-    c_mat, b_t, row_tab, col_tab = pl.pallas_call(
+    c_mat, b_t = pl.pallas_call(
         prep_kernel,
         grid=(nblk,),
         in_specs=[
-            rows_of(gathered.shape[1]),
+            rows_of(2 * STATE),
             full((RIM, 2 * STATE)),
             full((4, 2 * STATE)),
             full((1, 2 * STATE)),
-            lanes_of(heads),
-            full(par.shape),
-        ],
-        out_specs=[rows_of(STATE), lanes_of(STATE), lanes_of(3 * heads), rows_of(2 * heads)],
-        out_shape=[
-            jax.ShapeDtypeStruct((seg, STATE), BF16),
-            jax.ShapeDtypeStruct((STATE, seg), BF16),
-            jax.ShapeDtypeStruct((3 * heads, seg), F32),
-            jax.ShapeDtypeStruct((seg, 2 * heads), F32),
-        ],
-        scratch_shapes=[pltpu.VMEM((RIM, 2 * STATE), BF16)],
+        ],
+        out_specs=[rows_of(STATE), lanes_of(STATE)],
+        out_shape=[pltpu.HBM((seg, STATE), BF16), pltpu.HBM((STATE, seg), BF16)],
+        scratch_shapes=[pltpu.VMEM((RIM, 2 * STATE), F32)],
         compiler_params=PARAMS,
         name="prep",
-    )(gathered, bc_rim, conv_bc, bias_bc[None, :], dt_seg, par)
-
-    rim = shift(x_seg[seg - RIM :], "ctx", 1)
+    )(gathered, bc_rim, conv_bc, bias_bc[None, :])
     pieces = (STATE // 8) * (LANES // PART)
-    xc, local, parts = pl.pallas_call(
+    xc, local, parts, row_tab, col_tab = pl.pallas_call(
         state_kernel,
         grid=(nblk,),
         in_specs=[
@@ -260,22 +277,28 @@
             full((4, LANES)),
             full((1, LANES)),
             lanes_of(STATE),
-            lanes_of(3 * heads),
+            lanes_of(heads),
+            full(par.shape),
         ],
         out_specs=[
             rows_of(LANES),
             pl.BlockSpec((1, STATE + 8, LANES), lambda k: (k, 0, 0)),
             full((pieces, 8, PART + 128)),
+            lanes_of(2 * heads),
+            rows_of(2 * heads),
         ],
         out_shape=[
-            jax.ShapeDtypeStruct((seg, LANES), BF16),
-            jax.ShapeDtypeStruct((nblk, STATE + 8, LANES), F32),
+            pltpu.HBM((seg, LANES), BF16),
+            pltpu.HBM((nblk, STATE + 8, LANES), F32),
             jax.ShapeDtypeStruct((pieces, 8, PART + 128), F32),
-        ],
-        scratch_shapes=[pltpu.VMEM((RIM, LANES), BF16), pltpu.VMEM((STATE + 8, LANES), F32)],
+            pltpu.HBM((2 * heads, seg), F32),
+            pltpu.HBM((seg, 2 * heads), F32),
+        ],
+        scratch_shapes=[pltpu.VMEM((RIM, LANES), F32), pltpu.VMEM((STATE + 8, LANES), F32)],
         compiler_params=PARAMS,
         name="state",
-    )(x_seg, rim, conv_x, bias_x[None, :], b_t, row_tab)
+    )(x_seg, first[groups - 1, rows:], conv_x, bias_x[None, :], held(b_t), dt_seg, par)
+    c_mat, b_t, xc, local, row_tab, col_tab = [held(v) for v in (c_mat, b_t, xc, local, row_tab, col_tab)]
     incoming = entering(parts)
     skip = jnp.repeat(d_skip, WIDTH)[None, :]
     y_diag = pl.pallas_call(
@@ -285,12 +308,12 @@
             rows_of(LANES),
             rows_of(STATE),
             lanes_of(STATE),
-            lanes_of(3 * heads),
+            lanes_of(2 * heads),
             rows_of(2 * heads),
             full((1, LANES)),
         ],
         out_specs=rows_of(LANES),
-        out_shape=jax.ShapeDtypeStruct((seg, LANES), F32),
+        out_shape=pltpu.HBM((seg, LANES), F32),
         compiler_params=PARAMS,
         name="diag",
     )(xc, c_mat, b_t, row_tab, col_tab, skip)
@@ -309,9 +332,18 @@
         scratch_shapes=[pltpu.VMEM((STATE, LANES), F32)],
         compiler_params=PARAMS,
         name="join",
-    )(y_diag, c_mat, col_tab, local, incoming)
+    )(held(y_diag), c_mat, col_tab, local, incoming)
     y_tok = exchange(y.reshape(groups, rows, LANES))
     step = 32
+    gate = pl.pallas_call(
+        gate_kernel,
+        grid=(rows // step,),
+        in_specs=[pl.BlockSpec((step, z_in.shape[1]), lambda k: (k, 0))],
+        out_specs=pl.BlockSpec((step, z_in.shape[1]), lambda k: (k, 0)),
+        out_shape=jax.ShapeDtypeStruct(z_in.shape, F32),
+        compiler_params=PARAMS,
+        name="gate",
+    )(z_in)
     return pl.pallas_call(
         norm_kernel,
         grid=(rows // step,),
@@ -325,7 +357,7 @@
         scratch_shapes=[pltpu.VMEM((step, z_in.shape[1]), F32)],
         compiler_params=PARAMS,
         name="norm",
-    )(y_tok, z_in, norm_gain[None, :])
+    )(y_tok, gate, norm_gain[None, :])
 
 
 def solution(mesh):

time: 272 us -> 260 us (0.956)
  the two profiles are of different devices: /device:TPU:32 before, /device:TPU:2 now
where the time goes in v4:
time: 260 us; the launch traced here: 259 us
  waiting for transfers between devices  138 us (53%)
  blocking collectives  56.8 us (22%)
  Pallas kernels  32.9 us (13%)
  starting transfers between devices  25.6 us (10%)
  local copies, waits for them, and re-layouts  5.32 us (2%)
    all_to_all x2, waiting for transfers between devices, exchange(): lax.all_to_all(value.transpose(1, 0, 2), 'head', 1, 1, tiled=True)  133 us
    all_gather x1, blocking collectives, per_device(): gathered = lax.all_gather(bc_in, 'head', axis=0, tiled=True)  40.4 us
    all_to_all x2, starting transfers between devices, exchange(): lax.all_to_all(value.transpose(1, 0, 2), 'head', 1, 1, tiled=True)  16.6 us
    all_to_all x1, blocking collectives, entering(): got = lax.all_to_all(parts, 'ctx', 0, 0, tiled=True)  16.3 us
    pallas_call x1, Pallas kernels, per_device(): pl.pallas_call(state_kernel, grid=(nblk,), in_specs=[rows_of(LANES), full...  9.48 us
    pallas_call x1, Pallas kernels, per_device(): pl.pallas_call(diag_kernel, grid=(nblk,), in_specs=[rows_of(LANES), rows_...  7.01 us
    pallas_call x1, Pallas kernels, per_device(): pl.pallas_call(join_kernel, grid=(nblk,), in_specs=[rows_of(LANES), rows_...  6.31 us
  transfers between devices with their start and end apart: 5, of which 4 were waited for; matrix products, arithmetic and copies ran while one was open for 0% of the time, Pallas kernels for 4%

profile of v4, /device:TPU:2, one launch (start us, length us, event | category | flops | bytes accessed | tf_op | source)
XLA Modules:
  0.0 259.1 jit_solution(16609096312410122979)
XLA Ops:
  0.0 0.9 slice.15
  0.9 1.9 collective-permute-start
  2.8 40.4 %all_gather.3.g_ref = bf16[1536,256]{1,0:T(8,128)(2,1)S(1)} all-gather(bf16[96,256]{1,0:T(8,128)(2,1)} %param.14), channel_id=1, replica_groups=mesh['ctx'=32,'head'=16] {'head'}, dimensions={0}, use_global_device_ids=true | all-gather | bytes 835584 | tf_op jit(solution)/shard_map/all_gather | solution.py:241
  43.3 0.0 collective-permute-done.tail_ref
  43.3 0.0 copy-start
  43.3 1.4 copy-done
  44.7 0.0 copy-start.3
  44.7 0.7 copy-done.3
  45.4 1.3 pack.1
  46.8 0.0 copy-start.9
  46.8 0.0 copy-start.10
  46.8 0.0 copy-start.5
  46.8 0.0 copy-start.7
  46.8 7.1 %all-to-all-start = ((bf16[104,16,512]{2,0,1:T(8,128)(2,1)}), bf16[104,16,512]{2,0,1:T(8,128)(2,1)S(1)}, u32[]{:S(2)}, u32[]{:S(2)}) async-start(bf16[104,16,512]{2,0,1:T(8,128)(2,1)} %bitcast), calls=%async_computation | async-start | bytes 3407872 | tf_op jit(solution)/shard_map/all_to_all | solution.py:238
  53.9 1.9 collective-permute-start.1
  55.9 0.0 copy-done.9
  55.9 0.0 copy-done.10
  55.9 5.1 %collective-permute-done.1.rim_ref = bf16[8,256]{1,0:T(8,128)(2,1)S(1)} collective-permute-done((bf16[8,256]{1,0:T(8,128)(2,1)S(1)}, bf16[8,256]{1,0:T(8,128)(2,1)S(1)}, u32[]{:S(2)}, u32[]{:S(2)}) %collective-permute-start.1) | collective-permute-done | bytes 4128 | tf_op jit(solution)/shard_map/ppermute | solution.py:193
  61.0 0.0 copy-done.5
  61.0 0.0 copy-done.7
  61.0 3.3 %prep.1 = (bf16[1536,128]{1,0:T(8,128)(2,1)}, bf16[128,1536]{1,0:T(8,128)(2,1)}) custom-call(bf16[1536,256]{1,0:T(8,128)(2,1)S(1)} %all_gather.3.g_ref, bf16[8,256]{1,0:T(8,128)(2,1)S(1)} %collective-permute-done.1.rim_ref, f32[4,256]{1,0:T(4,128)S(1)} %copy-done.5, f32[1,256]{1,0:T(1,128)S(1)} %bitcast.19), custom_call_target="tpu_custom_call" | custom-call | tf_op jit(solution)/shard_map/prep/pallas_call | solution.py:255
  64.3 60.4 %all-to-all-done = bf16[104,16,512]{2,0,1:T(8,128)(2,1)S(1)} async-done(((bf16[104,16,512]{2,0,1:T(8,128)(2,1)}), bf16[104,16,512]{2,0,1:T(8,128)(2,1)S(1)}, u32[]{:S(2)}, u32[]{:S(2)}) %all-to-all-start) | async-done | bytes 1703968 | tf_op jit(solution)/shard_map/all_to_all | solution.py:238
  124.7 0.0 copy-start.4
  124.7 0.0 copy-start.6
  124.7 0.1 slice.20
  124.9 0.1 reshape.11.dt_ref
  125.0 0.1 broadcast_in_dim.20.par_ref
  125.0 0.3 copy-done.4
  125.4 0.0 copy-done.6
  125.4 0.0 copy-start.8
  125.4 9.5 %state.1 = (bf16[1536,512]{1,0:T(8,128)(2,1)}, f32[6,136,512]{2,1,0:T(8,128)}, f32[32,8,384]{2,1,0:T(8,128)S(1)}, f32[16,1536]{1,0:T(8,128)}, f32[1536,16]{1,0:T(8,128)}) custom-call(bf16[1536,512]{1,0:T(8,128)(2,1)S(1)} %bitcast.16, bf16[8,512]{1,0:T(8,128)(2,1)S(1)} %slice_bitcast_fusion.1.spare_ref, f32[4,512]{1,0:T(4,128)S(1)} %copy-done.4, ...), custom_call_target="tpu_custom_call" | custom-call | tf_op jit(solution)/shard_map/state/pallas_call | solution.py:271
  134.9 16.3 %all_to_all.20.part_ref = f32[32,8,384]{2,1,0:T(8,128)S(1)} all-to-all(f32[32,8,384]{2,1,0:T(8,128)S(1)} %get-tuple-element.22), channel_id=1, replica_groups=mesh['ctx'=32,'head'=16] {'ctx'}, dimensions={0} | all-to-all | bytes 786432 | tf_op jit(solution)/shard_map/all_to_all | solution.py:198
  151.2 0.8 scan.1
  152.0 5.1 %all-to-all-start.2 = ((f32[32,8,256]{2,1,0:T(8,128)}), f32[32,8,256]{2,1,0:T(8,128)S(1)}, u32[]{:S(2)}, u32[]{:S(2)}) async-start(f32[32,8,256]{2,1,0:T(8,128)} %scan.1), calls=%async_computation.2 | async-start | bytes 524288 | tf_op jit(solution)/shard_map/all_to_all | solution.py:205
  157.1 0.0 copy-done.8
  157.1 0.1 broadcast_in_dim.21
  157.2 0.1 broadcast_in_dim_reshape.3.skip_ref
  157.3 7.0 %diag.1.yd_ref = f32[1536,512]{1,0:T(8,128)} custom-call(bf16[1536,512]{1,0:T(8,128)(2,1)} %get-tuple-element.17.xc_ref, bf16[1536,128]{1,0:T(8,128)(2,1)} %get-tuple-element.18.c_ref, bf16[128,1536]{1,0:T(8,128)(2,1)} %get-tuple-element.16.bt_ref, f32[16,1536]{1,0:T(8,128)} %get-tuple-element.19.rows_ref, f32[1536,16]{1,0:T(8,128)} %get-tuple-element.20.cols_ref, ...), custom_call_target="tpu_custom_call" | custom-call | tf_op jit(solution)/shard_map/diag/pallas_call | solution.py:304
  164.3 0.6 all-to-all-done.2.in_ref
  164.8 6.3 %join.1 = bf16[1536,512]{1,0:T(8,128)(2,1)} custom-call(f32[1536,512]{1,0:T(8,128)} %diag.1.yd_ref, bf16[1536,128]{1,0:T(8,128)(2,1)} %get-tuple-element.18.c_ref, f32[1536,16]{1,0:T(8,128)} %get-tuple-element.20.cols_ref, f32[6,136,512]{2,1,0:T(8,128)} %get-tuple-element.21.local_ref, f32[32,8,256]{2,1,0:T(8,128)S(1)} %all-to-all-done.2.in_ref), custom_call_target="tpu_custom_call" | custom-call | tf_op jit(solution)/shard_map/join/pallas_call | solution.py:320
  171.2 9.5 %all-to-all-start.3 = ((bf16[96,16,512]{2,0,1:T(8,128)(2,1)}), bf16[96,16,512]{2,0,1:T(8,128)(2,1)}, u32[]{:S(2)}, u32[]{:S(2)}) async-start(bf16[96,16,512]{2,0,1:T(8,128)(2,1)} %bitcast.10), calls=%async_computation.3 | async-start | bytes 3145728 | tf_op jit(solution)/shard_map/all_to_all | solution.py:238
  180.6 0.0 copy-start.1
  180.6 1.4 copy-done.1
  182.0 0.0 copy-start.2
  182.0 0.9 gate.1.gate_ref
  182.9 72.4 %all-to-all-done.3 = bf16[96,16,512]{2,0,1:T(8,128)(2,1)} async-done(((bf16[96,16,512]{2,0,1:T(8,128)(2,1)}), bf16[96,16,512]{2,0,1:T(8,128)(2,1)}, u32[]{:S(2)}, u32[]{:S(2)}) %all-to-all-start.3) | async-done | bytes 1572896 | tf_op jit(solution)/shard_map/all_to_all | solution.py:238
  255.3 0.0 copy-done.2
  255.3 3.8 %norm.1 = bf16[96,8192]{1,0:T(8,128)(2,1)} custom-call(bf16[16,96,512]{2,1,0:T(8,128)(2,1)} %bitcast.11.y_ref, f32[96,8192]{1,0:T(8,128)S(1)} %gate.1.gate_ref, f32[1,8192]{1,0:T(1,128)S(1)} %bitcast.17), custom_call_target="tpu_custom_call" | custom-call | tf_op jit(solution)/shard_map/norm/pallas_call | solution.py:347
  (5 shorter events, 0.0 us)
Async XLA Ops:
  0.9 42.4 %collective-permute-start = (bf16[8,8192]{1,0:T(8,128)(2,1)S(1)}, bf16[8,8192]{1,0:T(8,128)(2,1)S(1)}, u32[]{:S(2)}, u32[]{:S(2)}) collective-permute-start(bf16[8,8192]{1,0:T(8,128)(2,1)S(1)} %slice.15), channel_id=1, source_target_pairs={{0,16},{16,32},{32,48},{48,64},{64,80},{80,96},{96,112},{112,128},... | collective-permute-start | bytes 393224 | tf_op jit(solution)/shard_map/ppermute | solution.py:193
  43.3 1.4 copy-start
  44.7 0.7 copy-start.3
  46.8 9.1 %copy-start.9 = (f32[8]{0:T(128)S(1)}, f32[8]{0:T(128)}, u32[]{:S(2)}) copy-start(f32[8]{0:T(128)} %param.21) | copy-start | bytes 100
  46.8 9.1 %copy-start.10 = (f32[8]{0:T(128)S(1)}, f32[8]{0:T(128)}, u32[]{:S(2)}) copy-start(f32[8]{0:T(128)} %param.20) | copy-start | bytes 100
  46.8 14.2 %copy-start.5 = (f32[4,256]{1,0:T(4,128)S(1)}, f32[4,256]{1,0:T(4,128)}, u32[]{:S(2)}) copy-start(f32[4,256]{1,0:T(4,128)} %taps_ref.2) | copy-start | bytes 12292
  46.8 14.2 %copy-start.7 = (f32[256]{0:T(256)S(1)}, f32[256]{0:T(256)}, u32[]{:S(2)}) copy-start(f32[256]{0:T(256)} %param.19) | copy-start | bytes 3076
  46.8 77.9 %all-to-all-start = ((bf16[104,16,512]{2,0,1:T(8,128)(2,1)}), bf16[104,16,512]{2,0,1:T(8,128)(2,1)S(1)}, u32[]{:S(2)}, u32[]{:S(2)}) async-start(bf16[104,16,512]{2,0,1:T(8,128)(2,1)} %bitcast), calls=%async_computation | async-start | bytes 3407872 | tf_op jit(solution)/shard_map/all_to_all | solution.py:238
  53.9 7.0 %collective-permute-start.1 = (bf16[8,256]{1,0:T(8,128)(2,1)S(1)}, bf16[8,256]{1,0:T(8,128)(2,1)S(1)}, u32[]{:S(2)}, u32[]{:S(2)}) collective-permute-start(bf16[8,256]{1,0:T(8,128)(2,1)S(1)} %slice.18), channel_id=1, source_target_pairs={{0,16},{16,32},{32,48},{48,64},{64,80},{80,96},{96,112},{112,128},... | collective-permute-start | bytes 12296 | tf_op jit(solution)/shard_map/ppermute | solution.py:193
  124.7 0.7 copy-start.4
  124.7 0.7 copy-start.6
  125.4 31.7 %copy-start.8 = (f32[8]{0:T(128)S(1)}, f32[8]{0:T(128)}, u32[]{:S(2)}) copy-start(f32[8]{0:T(128)} %param.22) | copy-start | bytes 100
  152.0 12.9 %all-to-all-start.2 = ((f32[32,8,256]{2,1,0:T(8,128)}), f32[32,8,256]{2,1,0:T(8,128)S(1)}, u32[]{:S(2)}, u32[]{:S(2)}) async-start(f32[32,8,256]{2,1,0:T(8,128)} %scan.1), calls=%async_computation.2 | async-start | bytes 524288 | tf_op jit(solution)/shard_map/all_to_all | solution.py:205
  171.2 84.1 %all-to-all-start.3 = ((bf16[96,16,512]{2,0,1:T(8,128)(2,1)}), bf16[96,16,512]{2,0,1:T(8,128)(2,1)}, u32[]{:S(2)}, u32[]{:S(2)}) async-start(bf16[96,16,512]{2,0,1:T(8,128)(2,1)} %bitcast.10), calls=%async_computation.3 | async-start | bytes 3145728 | tf_op jit(solution)/shard_map/all_to_all | solution.py:238
  180.6 1.4 copy-start.1
  182.0 73.3 %copy-start.2 = (f32[8192]{0:T(1024)S(1)}, f32[8192]{0:T(1024)}, u32[]{:S(2)}) copy-start(f32[8192]{0:T(1024)} %param.23) | copy-start | bytes 98308

commit v5 on v4

--- a/solution.py
+++ b/solution.py
@@ -30,19 +30,25 @@
     return silu(summed).astype(BF16)
 
 
-def pack_kernel(x_ref, dt_ref, tail_ref, out_ref):
+def pack_kernel(x_ref, dt_ref, tail_ref, out_ref, dt_t):
     rows = x_ref.shape[0]
-    dt = dt_ref[...].astype(F32).T
+    count = out_ref.shape[0]
+
+    @pl.when(pl.program_id(0) == 0)
+    def _():
+        dt_t[...] = dt_ref[...].astype(F32).T
+
     wide = LANES - 128
     row = lax.broadcasted_iota(jnp.int32, (RIM, wide), 0)
-    for g in range(out_ref.shape[0]):
+    for g in range(count):
         start = LANES * g
         out_ref[g, :rows] = x_ref[:, start : start + LANES]
         tail = tail_ref[:, start : start + LANES].astype(F32)
         rest = jnp.concatenate([tail[:, wide:], jnp.zeros((RIM, wide - 128), F32)], 1)
         spare = jnp.where(row < 6, pltpu.roll(rest, 6, 0), 0.0)
         spare = jnp.where(row < 3, pltpu.roll(tail[:, :wide], 3, 0), spare)
-        head = jnp.concatenate([dt[HEADS * g : HEADS * (g + 1)], jnp.zeros((HEADS, 128 - rows), F32)], 1)
+        first = pl.multiple_of(HEADS * (count * pl.program_id(0) + g), HEADS)
+        head = jnp.concatenate([dt_t[pl.ds(first, HEADS)], jnp.zeros((HEADS, 128 - rows), F32)], 1)
         out_ref[g, rows:] = jnp.concatenate([head, spare], 1).astype(BF16)
 
 
@@ -62,7 +68,7 @@
     shifted = dt_raw.astype(F32) + par[0]
     dt = jnp.maximum(shifted, 0.0) + jnp.log1p(jnp.exp(-jnp.abs(shifted)))
     cs = dt * -jnp.exp(par[1])
-    lane = lax.broadcasted_iota(jnp.int32, cs.shape, 1)
+    lane = lax.broadcasted_iota(jnp.int32, cs.shape, 1) & (BLOCK - 1)
     step = 1
     while step < BLOCK:
         cs = cs + jnp.where(lane >= step, pltpu.roll(cs, step, 1), 0.0)
@@ -77,7 +83,7 @@
 
 def state_kernel(
     x_ref, spare_ref, taps_ref, bias_ref, bt_ref, dt_ref, par_ref,
-    xc_ref, local_ref, part_ref, rows_ref, cols_ref, carry, run
+    xc_ref, local_ref, part_ref, rows_ref, carry, run
 ):
     @pl.when(pl.program_id(0) == 0)
     def _():
@@ -86,12 +92,11 @@
         rest = pltpu.roll(spare[:, 128:256], 2, 0)
         carry[...] = jnp.concatenate([most, rest], 1)
         run[...] = jnp.zeros_like(run)
-
-    cs, dt = step_tables(dt_ref[...], par_ref)
-    weight = jnp.exp(cs[:, BLOCK - 1 :] - cs) * dt
-    rows_ref[:HEADS] = cs
-    rows_ref[HEADS:] = dt
-    cols_ref[...] = jnp.concatenate([cs, jnp.exp(cs)], 0).T
+        rows_ref[:HEADS], rows_ref[HEADS:] = step_tables(dt_ref[...], par_ref)
+
+    here = pl.ds(pl.multiple_of(BLOCK * pl.program_id(0), BLOCK), BLOCK)
+    cs = rows_ref[:HEADS, here]
+    weight = jnp.exp(cs[:, BLOCK - 1 :] - cs) * rows_ref[HEADS:, here]
     raw = x_ref[...]
     xc = causal_conv(carry[...], raw, taps_ref[...], bias_ref[...])
     carry[...] = raw[BLOCK - RIM :].astype(F32)
@@ -130,7 +135,8 @@
         run = run * jnp.exp(gain) + part_ref[s, :, :PART]
 
 
-def diag_kernel(xc_ref, c_ref, bt_ref, rows_ref, cols_ref, skip_ref, y_ref):
+def diag_kernel(xc_ref, c_ref, bt_ref, rows_ref, skip_ref, y_ref):
+    cs_t = rows_ref[:HEADS].T
     half = BLOCK // 2
     xc = xc_ref[...]
     scores = jnp.dot(c_ref[...], bt_ref[...], preferred_element_type=F32)
@@ -143,7 +149,7 @@
             cols = slice(2 * WIDTH * pair, 2 * WIDTH * (pair + 1))
             outs = []
             for h in (2 * pair, 2 * pair + 1):
-                gap = cols_ref[low : low + half, h : h + 1] - rows_ref[h : h + 1, :width]
+                gap = cs_t[low : low + half, h : h + 1] - rows_ref[h : h + 1, :width]
                 spread = jnp.exp(jnp.where(keep, gap, -1e30))
                 m = (part * spread * rows_ref[8 + h : 9 + h, :width]).astype(BF16)
                 outs.append(jnp.dot(m, xc[:width, cols], preferred_element_type=F32))
@@ -153,7 +159,7 @@
             )
 
 
-def join_kernel(yd_ref, c_ref, cols_ref, local_ref, in_ref, y_ref, entry):
+def join_kernel(upper_ref, lower_ref, c_ref, rows_ref, local_ref, in_ref, y_ref, entry):
     @pl.when(pl.program_id(0) == 0)
     def _():
         for i in range(STATE // 8):
@@ -163,11 +169,18 @@
 
     hb = (entry[...] * jnp.exp(local_ref[0, STATE : STATE + 1]) + local_ref[0, :STATE]).astype(BF16)
     off = jnp.dot(c_ref[...], hb, preferred_element_type=F32)
-    for pair in range(HEADS // 2):
-        cols = slice(2 * WIDTH * pair, 2 * WIDTH * (pair + 1))
-        h = 8 + 2 * pair
-        scale = lane_pair(cols_ref[:, h : h + 1], cols_ref[:, h + 1 : h + 2], (BLOCK, 2 * WIDTH))
-        y_ref[:, cols] = (yd_ref[:, cols] + off[:, cols] * scale).astype(BF16)
+    grow = jnp.exp(rows_ref[:HEADS]).T
+
+    def finish(diag_ref):
+        for pair in range(HEADS // 2):
+            cols = slice(2 * WIDTH * pair, 2 * WIDTH * (pair + 1))
+            h = 2 * pair
+            scale = lane_pair(grow[:, h : h + 1], grow[:, h + 1 : h + 2], (BLOCK, 2 * WIDTH))
+            y_ref[:, cols] = (diag_ref[:, cols] + off[:, cols] * scale).astype(BF16)
+
+    early = pl.program_id(0) < pl.num_programs(0) // 2
+    pl.when(early)(lambda: finish(upper_ref))
+    pl.when(jnp.logical_not(early))(lambda: finish(lower_ref))
 
 
 def gate_kernel(z_ref, out_ref):
@@ -193,18 +206,6 @@
     return lax.ppermute(value, axis, [(i, i + by) for i in range(count - by)])
 
 
-def entering(parts):
-    count, height, _ = parts.shape
-    got = lax.all_to_all(parts, "ctx", 0, 0, tiled=True)
-    before = pl.pallas_call(
-        scan_kernel,
-        out_shape=jax.ShapeDtypeStruct((count, height, PART), F32),
-        compiler_params=WHOLE,
-        name="scan",
-    )(got)
-    return lax.all_to_all(before, "ctx", 0, 0, tiled=True)
-
-
 def held(value):
     return pltpu.with_memory_space_constraint(value, pltpu.HBM)
 
@@ -213,12 +214,12 @@
     return pl.BlockSpec(shape, lambda k: tuple(0 for _ in shape))
 
 
-def rows_of(width):
-    return pl.BlockSpec((BLOCK, width), lambda k: (k, 0))
-
-
-def lanes_of(height):
-    return pl.BlockSpec((height, BLOCK), lambda k: (0, k))
+def rows_of(width, first=0):
+    return pl.BlockSpec((BLOCK, width), lambda k: (k + first, 0))
+
+
+def lanes_of(height, first=0):
+    return pl.BlockSpec((height, BLOCK), lambda k: (0, k + first))
 
 
 WHOLE = pltpu.CompilerParams(vmem_limit_bytes=16 << 20)
@@ -240,17 +241,26 @@
     tail = shift(x_in[rows - RIM :], "ctx", 1)
     gathered = lax.all_gather(bc_in, "head", axis=0, tiled=True)
     tail, gathered = lax.optimization_barrier((tail, gathered))
+    steps = 4
     packed = pl.pallas_call(
         pack_kernel,
+        grid=(steps,),
+        in_specs=[
+            pl.BlockSpec((rows, x_in.shape[1] // steps), lambda k: (0, k)),
+            full(dt_raw.shape),
+            pl.BlockSpec((RIM, x_in.shape[1] // steps), lambda k: (0, k)),
+        ],
+        out_specs=pl.BlockSpec((groups // steps, rows + RIM, LANES), lambda k: (k, 0, 0)),
         out_shape=jax.ShapeDtypeStruct((groups, rows + RIM, LANES), BF16),
-        compiler_params=WHOLE,
+        scratch_shapes=[pltpu.VMEM((dt_raw.shape[1], rows), F32)],
+        compiler_params=PARAMS,
         name="pack",
-    )(x_in, dt_raw, tail)
+    )(held(x_in), dt_raw, tail)
     first = exchange(packed)
     x_seg = first[:, :rows].reshape(seg, LANES)
     dt_seg = first[:, rows:, :rows].transpose(1, 0, 2).reshape(heads, seg)
     par = jnp.stack([dt_bias, a_log])[:, :, None]
-    par = jnp.broadcast_to(par, (2, heads, BLOCK))
+    par = jnp.broadcast_to(par, (2, heads, seg))
     bc_rim = shift(gathered[seg - RIM :], "ctx", 1)
     c_mat, b_t = pl.pallas_call(
         prep_kernel,
@@ -268,7 +278,7 @@
         name="prep",
     )(gathered, bc_rim, conv_bc, bias_bc[None, :])
     pieces = (STATE // 8) * (LANES // PART)
-    xc, local, parts, row_tab, col_tab = pl.pallas_call(
+    xc, local, parts, row_tab = pl.pallas_call(
         state_kernel,
         grid=(nblk,),
         in_specs=[
@@ -277,62 +287,74 @@
             full((4, LANES)),
             full((1, LANES)),
             lanes_of(STATE),
-            lanes_of(heads),
+            full(dt_seg.shape),
             full(par.shape),
         ],
         out_specs=[
             rows_of(LANES),
             pl.BlockSpec((1, STATE + 8, LANES), lambda k: (k, 0, 0)),
             full((pieces, 8, PART + 128)),
-            lanes_of(2 * heads),
-            rows_of(2 * heads),
+            full((2 * heads, seg)),
         ],
         out_shape=[
             pltpu.HBM((seg, LANES), BF16),
             pltpu.HBM((nblk, STATE + 8, LANES), F32),
             jax.ShapeDtypeStruct((pieces, 8, PART + 128), F32),
             pltpu.HBM((2 * heads, seg), F32),
-            pltpu.HBM((seg, 2 * heads), F32),
         ],
         scratch_shapes=[pltpu.VMEM((RIM, LANES), F32), pltpu.VMEM((STATE + 8, LANES), F32)],
         compiler_params=PARAMS,
         name="state",
     )(x_seg, first[groups - 1, rows:], conv_x, bias_x[None, :], held(b_t), dt_seg, par)
-    c_mat, b_t, xc, local, row_tab, col_tab = [held(v) for v in (c_mat, b_t, xc, local, row_tab, col_tab)]
-    incoming = entering(parts)
+    c_mat, b_t, local, row_tab = [held(v) for v in (c_mat, b_t, local, row_tab)]
     skip = jnp.repeat(d_skip, WIDTH)[None, :]
-    y_diag = pl.pallas_call(
-        diag_kernel,
-        grid=(nblk,),
-        in_specs=[
-            rows_of(LANES),
-            rows_of(STATE),
-            lanes_of(STATE),
-            lanes_of(2 * heads),
-            rows_of(2 * heads),
-            full((1, LANES)),
-        ],
-        out_specs=rows_of(LANES),
-        out_shape=pltpu.HBM((seg, LANES), F32),
-        compiler_params=PARAMS,
-        name="diag",
-    )(xc, c_mat, b_t, row_tab, col_tab, skip)
+    half = nblk // 2
+
+    def diagonal(first_block):
+        return pl.pallas_call(
+            diag_kernel,
+            grid=(half,),
+            in_specs=[
+                rows_of(LANES, first_block),
+                rows_of(STATE, first_block),
+                lanes_of(STATE, first_block),
+                lanes_of(2 * heads, first_block),
+                full((1, LANES)),
+            ],
+            out_specs=rows_of(LANES),
+            out_shape=pltpu.HBM((half * BLOCK, LANES), F32),
+            compiler_params=PARAMS,
+            name="diag",
+        )(held(xc), c_mat, b_t, row_tab, skip)
+
+    upper = diagonal(0)
+    got = lax.all_to_all(parts, "ctx", 0, 0, tiled=True)
+    got, xc, upper = lax.optimization_barrier((got, xc, upper))
+    before = pl.pallas_call(
+        scan_kernel,
+        out_shape=jax.ShapeDtypeStruct((pieces, 8, PART), F32),
+        compiler_params=WHOLE,
+        name="scan",
+    )(got)
+    incoming = lax.all_to_all(before, "ctx", 0, 0, tiled=True)
+    lower = diagonal(half)
     y = pl.pallas_call(
         join_kernel,
         grid=(nblk,),
         in_specs=[
-            rows_of(LANES),
+            pl.BlockSpec((BLOCK, LANES), lambda k: (jnp.minimum(k, half - 1), 0)),
+            pl.BlockSpec((BLOCK, LANES), lambda k: (jnp.maximum(k - half, 0), 0)),
             rows_of(STATE),
-            rows_of(2 * heads),
+            lanes_of(2 * heads),
             pl.BlockSpec((1, STATE + 8, LANES), lambda k: (k, 0, 0)),
             full((pieces, 8, PART)),
         ],
         out_specs=rows_of(LANES),
-        out_shape=jax.ShapeDtypeStruct((seg, LANES), BF16),
+        out_shape=pltpu.HBM((seg, LANES), BF16),
         scratch_shapes=[pltpu.VMEM((STATE, LANES), F32)],
         compiler_params=PARAMS,
         name="join",
-    )(held(y_diag), c_mat, col_tab, local, incoming)
+    )(held(upper), held(lower), c_mat, row_tab, local, incoming)
     y_tok = exchange(y.reshape(groups, rows, LANES))
     step = 32
     gate = pl.pallas_call(

time: 260 us -> 260 us (level)
  blocking collectives: 56.8 us -> 40.4 us
  starting transfers between devices: 25.6 us -> 33.4 us
  waiting for transfers between devices: 138 us -> 145 us
  Pallas kernels: 32.9 us -> 35.8 us
    all_to_all x1 -> x0, blocking collectives: 16.3 us -> none  [entering(): got = lax.all_to_all(parts, 'ctx', 0, 0, tiled=True)]
    all_to_all x1 -> x2, starting transfers between devices: 5.12 us -> 13 us  [the longest x1 7.84 us: per_device(): got = lax.all_to_all(parts, 'ctx', 0, 0, tiled=True)]
    all_to_all x1 -> x2, waiting for transfers between devices: 0.55 us -> 7.42 us  [the longest x1 4.14 us: per_device(): got = lax.all_to_all(parts, 'ctx', 0, 0, tiled=True)]
    pallas_call x4 -> x5, Pallas kernels: 15.5 us -> 20.3 us  [the longest x2 8.87 us: diagonal(): pl.pallas_call(diag_kernel, grid=(half,), in_specs=[rows_of(LANES, first_...]
  transfers between devices with their start and end apart: 5 -> 6, of which waited for: 4 -> 5; matrix products, arithmetic and copies ran while one was open for 0% -> 0% of each run, Pallas kernels for 4% -> 5%
where the time goes in v5:
time: 260 us; the launch traced here: 259 us
  waiting for transfers between devices  145 us (56%)
  blocking collectives  40.4 us (16%)
  Pallas kernels  35.8 us (14%)
  starting transfers between devices  33.4 us (13%)
  local copies, waits for them, and re-layouts  3.9 us (2%)
    all_to_all x2, waiting for transfers between devices, exchange(): lax.all_to_all(value.transpose(1, 0, 2), 'head', 1, 1, tiled=True)  133 us
    all_gather x1, blocking collectives, per_device(): gathered = lax.all_gather(bc_in, 'head', axis=0, tiled=True)  40.4 us
    all_to_all x2, starting transfers between devices, exchange(): lax.all_to_all(value.transpose(1, 0, 2), 'head', 1, 1, tiled=True)  16.6 us
    pallas_call x2, Pallas kernels, diagonal(): pl.pallas_call(diag_kernel, grid=(half,), in_specs=[rows_of(LANES, first_...  8.87 us
    all_to_all x1, starting transfers between devices, per_device(): got = lax.all_to_all(parts, 'ctx', 0, 0, tiled=True)  7.84 us
    pallas_call x1, Pallas kernels, per_device(): pl.pallas_call(state_kernel, grid=(nblk,), in_specs=[rows_of(LANES), full...  7.46 us
    pallas_call x1, Pallas kernels, per_device(): pl.pallas_call(join_kernel, grid=(nblk,), in_specs=[pl.BlockSpec((BLOCK,...  6.98 us
  transfers between devices with their start and end apart: 6, of which 5 were waited for; matrix products, arithmetic and copies ran while one was open for 0% of the time, Pallas kernels for 5%

profile of v5, /device:TPU:2, one launch (start us, length us, event | category | flops | bytes accessed | tf_op | source)
XLA Modules:
  0.0 259.0 jit_solution(8747950551678236467)
XLA Ops:
  0.0 0.9 slice.15
  0.9 1.9 collective-permute-start
  2.8 40.4 %all_gather.3.g_ref = bf16[1536,256]{1,0:T(8,128)(2,1)S(1)} all-gather(bf16[96,256]{1,0:T(8,128)(2,1)} %param.14), channel_id=1, replica_groups=mesh['ctx'=32,'head'=16] {'head'}, dimensions={0}, use_global_device_ids=true | all-gather | bytes 835584 | tf_op jit(solution)/shard_map/all_gather | solution.py:242
  43.3 0.0 collective-permute-done.tail_ref
  43.3 0.0 copy-start.2
  43.3 0.7 copy-done.2
  44.0 3.7 %pack.1 = bf16[16,104,512]{2,1,0:T(8,128)(2,1)} custom-call(bf16[96,8192]{1,0:T(8,128)(2,1)} %x_ref.1, bf16[96,128]{1,0:T(8,128)(2,1)S(1)} %copy-done.2, bf16[8,8192]{1,0:T(8,128)(2,1)S(1)} %collective-permute-done.tail_ref), custom_call_target="tpu_custom_call" | custom-call | tf_op jit(solution)/shard_map/pack/pallas_call | solution.py:245
  47.7 0.0 copy-start.8
  47.7 0.0 copy-start.9
  47.7 0.0 copy-start.4
  47.7 0.0 copy-start.6
  47.7 7.1 %all-to-all-start = ((bf16[104,16,512]{2,0,1:T(8,128)(2,1)}), bf16[104,16,512]{2,0,1:T(8,128)(2,1)S(1)}, u32[]{:S(2)}, u32[]{:S(2)}) async-start(bf16[104,16,512]{2,0,1:T(8,128)(2,1)} %bitcast), calls=%async_computation | async-start | bytes 3407872 | tf_op jit(solution)/shard_map/all_to_all | solution.py:239
  54.9 1.9 collective-permute-start.1
  56.8 0.0 copy-done.8
  56.8 0.0 copy-done.9
  56.9 5.1 %collective-permute-done.1.rim_ref = bf16[8,256]{1,0:T(8,128)(2,1)S(1)} collective-permute-done((bf16[8,256]{1,0:T(8,128)(2,1)S(1)}, bf16[8,256]{1,0:T(8,128)(2,1)S(1)}, u32[]{:S(2)}, u32[]{:S(2)}) %collective-permute-start.1) | collective-permute-done | bytes 4128 | tf_op jit(solution)/shard_map/ppermute | solution.py:206
  61.9 0.0 copy-done.4
  61.9 0.0 copy-done.6
  61.9 3.3 %prep.1 = (bf16[1536,128]{1,0:T(8,128)(2,1)}, bf16[128,1536]{1,0:T(8,128)(2,1)}) custom-call(bf16[1536,256]{1,0:T(8,128)(2,1)S(1)} %all_gather.3.g_ref, bf16[8,256]{1,0:T(8,128)(2,1)S(1)} %collective-permute-done.1.rim_ref, f32[4,256]{1,0:T(4,128)S(1)} %copy-done.4, f32[1,256]{1,0:T(1,128)S(1)} %bitcast.19), custom_call_target="tpu_custom_call" | custom-call | tf_op jit(solution)/shard_map/prep/pallas_call | solution.py:265
  65.2 60.4 %all-to-all-done = bf16[104,16,512]{2,0,1:T(8,128)(2,1)S(1)} async-done(((bf16[104,16,512]{2,0,1:T(8,128)(2,1)}), bf16[104,16,512]{2,0,1:T(8,128)(2,1)S(1)}, u32[]{:S(2)}, u32[]{:S(2)}) %all-to-all-start) | async-done | bytes 1703968 | tf_op jit(solution)/shard_map/all_to_all | solution.py:239
  125.6 0.0 copy-start.3
  125.7 0.0 copy-start.5
  125.7 0.1 slice.20
  125.8 0.0 copy-start.7
  125.9 0.1 reshape.11.dt_ref
  126.0 0.1 broadcast_in_dim.20.par_ref
  126.0 0.3 copy-done.3
  126.3 0.0 copy-done.5
  126.3 7.5 %state.1 = (bf16[1536,512]{1,0:T(8,128)(2,1)}, f32[6,136,512]{2,1,0:T(8,128)}, f32[32,8,384]{2,1,0:T(8,128)}, f32[16,1536]{1,0:T(8,128)}) custom-call(bf16[1536,512]{1,0:T(8,128)(2,1)S(1)} %bitcast.16, bf16[8,512]{1,0:T(8,128)(2,1)S(1)} %slice_bitcast_fusion.1.spare_ref, f32[4,512]{1,0:T(4,128)S(1)} %copy-done.3, f32[1,512]{1,0:T(1,128)S(1)} %bitcast.18, ...), custom_call_target="tpu_custom_call" | custom-call | tf_op jit(solution)/shard_map/state/pallas_call | solution.py:281
  133.8 7.8 %all-to-all-start.1 = ((f32[32,8,384]{2,1,0:T(8,128)}), f32[32,8,384]{2,1,0:T(8,128)S(1)}, u32[]{:S(2)}, u32[]{:S(2)}) async-start(f32[32,8,384]{2,1,0:T(8,128)} %get-tuple-element.19), calls=%async_computation.1 | async-start | bytes 786432 | tf_op jit(solution)/shard_map/all_to_all | solution.py:331
  141.7 0.0 copy-done.7
  141.7 0.1 broadcast_in_dim.21
  141.7 0.1 broadcast_in_dim_reshape.3.skip_ref
  141.8 4.4 %diag.2.upper_ref = f32[768,512]{1,0:T(8,128)} custom-call(bf16[1536,512]{1,0:T(8,128)(2,1)} %get-tuple-element.24.xc_ref, bf16[1536,128]{1,0:T(8,128)(2,1)} %get-tuple-element.21.c_ref, bf16[128,1536]{1,0:T(8,128)(2,1)} %get-tuple-element.18.bt_ref, f32[16,1536]{1,0:T(8,128)} %get-tuple-element.22.rows_ref, f32[1,512]{1,0:T(1,128)S(1)} %broadcast_in_dim_reshape.3.skip_ref), custom_call_target="tpu_custom_call" | custom-call | tf_op jit(solution)/shard_map/diag/pallas_call | solution.py:314
  146.2 4.1 %all-to-all-done.1.part_ref = f32[32,8,384]{2,1,0:T(8,128)S(1)} async-done(((f32[32,8,384]{2,1,0:T(8,128)}), f32[32,8,384]{2,1,0:T(8,128)S(1)}, u32[]{:S(2)}, u32[]{:S(2)}) %all-to-all-start.1) | async-done | bytes 393248 | tf_op jit(solution)/shard_map/all_to_all | solution.py:331
  150.4 0.8 scan.1
  151.2 5.1 %all-to-all-start.2 = ((f32[32,8,256]{2,1,0:T(8,128)}), f32[32,8,256]{2,1,0:T(8,128)S(1)}, u32[]{:S(2)}, u32[]{:S(2)}) async-start(f32[32,8,256]{2,1,0:T(8,128)} %scan.1), calls=%async_computation.2 | async-start | bytes 524288 | tf_op jit(solution)/shard_map/all_to_all | solution.py:339
  156.3 4.5 %diag.3.lower_ref = f32[768,512]{1,0:T(8,128)} custom-call(bf16[1536,512]{1,0:T(8,128)(2,1)} %get-tuple-element.24.xc_ref, bf16[1536,128]{1,0:T(8,128)(2,1)} %get-tuple-element.21.c_ref, bf16[128,1536]{1,0:T(8,128)(2,1)} %get-tuple-element.18.bt_ref, f32[16,1536]{1,0:T(8,128)} %get-tuple-element.22.rows_ref, f32[1,512]{1,0:T(1,128)S(1)} %broadcast_in_dim_reshape.3.skip_ref), custom_call_target="tpu_custom_call" | custom-call | tf_op jit(solution)/shard_map/diag/pallas_call | solution.py:314
  160.7 3.3 %all-to-all-done.2.in_ref = f32[32,8,256]{2,1,0:T(8,128)S(1)} async-done(((f32[32,8,256]{2,1,0:T(8,128)}), f32[32,8,256]{2,1,0:T(8,128)S(1)}, u32[]{:S(2)}, u32[]{:S(2)}) %all-to-all-start.2) | async-done | bytes 262176 | tf_op jit(solution)/shard_map/all_to_all | solution.py:339
  164.0 7.0 %join.1 = bf16[1536,512]{1,0:T(8,128)(2,1)} custom-call(f32[768,512]{1,0:T(8,128)} %diag.2.upper_ref, f32[768,512]{1,0:T(8,128)} %diag.3.lower_ref, bf16[1536,128]{1,0:T(8,128)(2,1)} %get-tuple-element.21.c_ref, f32[16,1536]{1,0:T(8,128)} %get-tuple-element.22.rows_ref, f32[6,136,512]{2,1,0:T(8,128)} %get-tuple-element.25.local_ref, ...), custom_call_target="tpu_custom_call" | custom-call | tf_op jit(solution)/shard_map/join/pallas_call | solution.py:341
  171.0 9.5 %all-to-all-start.3 = ((bf16[96,16,512]{2,0,1:T(8,128)(2,1)}), bf16[96,16,512]{2,0,1:T(8,128)(2,1)}, u32[]{:S(2)}, u32[]{:S(2)}) async-start(bf16[96,16,512]{2,0,1:T(8,128)(2,1)} %bitcast.23), calls=%async_computation.3 | async-start | bytes 3145728 | tf_op jit(solution)/shard_map/all_to_all | solution.py:239
  180.5 0.0 copy-start
  180.5 1.4 copy-done
  181.9 0.0 copy-start.1
  181.9 0.9 gate.1.gate_ref
  182.8 72.4 %all-to-all-done.3 = bf16[96,16,512]{2,0,1:T(8,128)(2,1)} async-done(((bf16[96,16,512]{2,0,1:T(8,128)(2,1)}), bf16[96,16,512]{2,0,1:T(8,128)(2,1)}, u32[]{:S(2)}, u32[]{:S(2)}) %all-to-all-start.3) | async-done | bytes 1572896 | tf_op jit(solution)/shard_map/all_to_all | solution.py:239
  255.1 0.0 copy-done.1
  255.1 3.8 %norm.1 = bf16[96,8192]{1,0:T(8,128)(2,1)} custom-call(bf16[16,96,512]{2,1,0:T(8,128)(2,1)} %bitcast.11.y_ref, f32[96,8192]{1,0:T(8,128)S(1)} %gate.1.gate_ref, f32[1,8192]{1,0:T(1,128)S(1)} %bitcast.17), custom_call_target="tpu_custom_call" | custom-call | tf_op jit(solution)/shard_map/norm/pallas_call | solution.py:369
  (5 shorter events, 0.0 us)
Async XLA Ops:
  0.9 42.4 %collective-permute-start = (bf16[8,8192]{1,0:T(8,128)(2,1)S(1)}, bf16[8,8192]{1,0:T(8,128)(2,1)S(1)}, u32[]{:S(2)}, u32[]{:S(2)}) collective-permute-start(bf16[8,8192]{1,0:T(8,128)(2,1)S(1)} %slice.15), channel_id=1, source_target_pairs={{0,16},{16,32},{32,48},{48,64},{64,80},{80,96},{96,112},{112,128},... | collective-permute-start | bytes 393224 | tf_op jit(solution)/shard_map/ppermute | solution.py:206
  43.3 0.7 copy-start.2
  47.7 9.1 %copy-start.8 = (f32[8]{0:T(128)S(1)}, f32[8]{0:T(128)}, u32[]{:S(2)}) copy-start(f32[8]{0:T(128)} %param.21) | copy-start | bytes 100
  47.7 9.1 %copy-start.9 = (f32[8]{0:T(128)S(1)}, f32[8]{0:T(128)}, u32[]{:S(2)}) copy-start(f32[8]{0:T(128)} %param.20) | copy-start | bytes 100
  47.7 14.2 %copy-start.4 = (f32[4,256]{1,0:T(4,128)S(1)}, f32[4,256]{1,0:T(4,128)}, u32[]{:S(2)}) copy-start(f32[4,256]{1,0:T(4,128)} %taps_ref.2) | copy-start | bytes 12292
  47.7 14.2 %copy-start.6 = (f32[256]{0:T(256)S(1)}, f32[256]{0:T(256)}, u32[]{:S(2)}) copy-start(f32[256]{0:T(256)} %param.19) | copy-start | bytes 3076
  47.7 77.9 %all-to-all-start = ((bf16[104,16,512]{2,0,1:T(8,128)(2,1)}), bf16[104,16,512]{2,0,1:T(8,128)(2,1)S(1)}, u32[]{:S(2)}, u32[]{:S(2)}) async-start(bf16[104,16,512]{2,0,1:T(8,128)(2,1)} %bitcast), calls=%async_computation | async-start | bytes 3407872 | tf_op jit(solution)/shard_map/all_to_all | solution.py:239
  54.9 7.0 %collective-permute-start.1 = (bf16[8,256]{1,0:T(8,128)(2,1)S(1)}, bf16[8,256]{1,0:T(8,128)(2,1)S(1)}, u32[]{:S(2)}, u32[]{:S(2)}) collective-permute-start(bf16[8,256]{1,0:T(8,128)(2,1)S(1)} %slice.18), channel_id=1, source_target_pairs={{0,16},{16,32},{32,48},{48,64},{64,80},{80,96},{96,112},{112,128},... | collective-permute-start | bytes 12296 | tf_op jit(solution)/shard_map/ppermute | solution.py:206
  125.6 0.7 copy-start.3
  125.7 0.7 copy-start.5
  125.8 15.8 %copy-start.7 = (f32[8]{0:T(128)S(1)}, f32[8]{0:T(128)}, u32[]{:S(2)}) copy-start(f32[8]{0:T(128)} %param.22) | copy-start | bytes 100
  133.8 16.6 %all-to-all-start.1 = ((f32[32,8,384]{2,1,0:T(8,128)}), f32[32,8,384]{2,1,0:T(8,128)S(1)}, u32[]{:S(2)}, u32[]{:S(2)}) async-start(f32[32,8,384]{2,1,0:T(8,128)} %get-tuple-element.19), calls=%async_computation.1 | async-start | bytes 786432 | tf_op jit(solution)/shard_map/all_to_all | solution.py:331
  151.2 12.9 %all-to-all-start.2 = ((f32[32,8,256]{2,1,0:T(8,128)}), f32[32,8,256]{2,1,0:T(8,128)S(1)}, u32[]{:S(2)}, u32[]{:S(2)}) async-start(f32[32,8,256]{2,1,0:T(8,128)} %scan.1), calls=%async_computation.2 | async-start | bytes 524288 | tf_op jit(solution)/shard_map/all_to_all | solution.py:339
  171.0 84.1 %all-to-all-start.3 = ((bf16[96,16,512]{2,0,1:T(8,128)(2,1)}), bf16[96,16,512]{2,0,1:T(8,128)(2,1)}, u32[]{:S(2)}, u32[]{:S(2)}) async-start(bf16[96,16,512]{2,0,1:T(8,128)(2,1)} %bitcast.23), calls=%async_computation.3 | async-start | bytes 3145728 | tf_op jit(solution)/shard_map/all_to_all | solution.py:239
  180.5 1.4 copy-start
  181.9 73.3 %copy-start.1 = (f32[8192]{0:T(1024)S(1)}, f32[8192]{0:T(1024)}, u32[]{:S(2)}) copy-start(f32[8192]{0:T(1024)} %param.23) | copy-start | bytes 98308

commit v6 on v4

--- a/solution.py
+++ b/solution.py
@@ -17,7 +17,8 @@
 
 
 def silu(u):
-    return u / (1.0 + jnp.exp(-u))
+    half = 0.5 * u
+    return half + half * jnp.tanh(half)
 
 
 def causal_conv(before, rows, taps, offset):
@@ -62,7 +63,7 @@
     shifted = dt_raw.astype(F32) + par[0]
     dt = jnp.maximum(shifted, 0.0) + jnp.log1p(jnp.exp(-jnp.abs(shifted)))
     cs = dt * -jnp.exp(par[1])
-    lane = lax.broadcasted_iota(jnp.int32, cs.shape, 1)
+    lane = lax.broadcasted_iota(jnp.int32, cs.shape, 1) & (BLOCK - 1)
     step = 1
     while step < BLOCK:
         cs = cs + jnp.where(lane >= step, pltpu.roll(cs, step, 1), 0.0)
@@ -77,7 +78,7 @@
 
 def state_kernel(
     x_ref, spare_ref, taps_ref, bias_ref, bt_ref, dt_ref, par_ref,
-    xc_ref, local_ref, part_ref, rows_ref, cols_ref, carry, run
+    xc_ref, local_ref, part_ref, rows_ref, carry, run
 ):
     @pl.when(pl.program_id(0) == 0)
     def _():
@@ -86,12 +87,11 @@
         rest = pltpu.roll(spare[:, 128:256], 2, 0)
         carry[...] = jnp.concatenate([most, rest], 1)
         run[...] = jnp.zeros_like(run)
-
-    cs, dt = step_tables(dt_ref[...], par_ref)
-    weight = jnp.exp(cs[:, BLOCK - 1 :] - cs) * dt
-    rows_ref[:HEADS] = cs
-    rows_ref[HEADS:] = dt
-    cols_ref[...] = jnp.concatenate([cs, jnp.exp(cs)], 0).T
+        rows_ref[:HEADS], rows_ref[HEADS:] = step_tables(dt_ref[...], par_ref)
+
+    here = pl.ds(pl.multiple_of(BLOCK * pl.program_id(0), BLOCK), BLOCK)
+    cs = rows_ref[:HEADS, here]
+    weight = jnp.exp(cs[:, BLOCK - 1 :] - cs) * rows_ref[HEADS:, here]
     raw = x_ref[...]
     xc = causal_conv(carry[...], raw, taps_ref[...], bias_ref[...])
     carry[...] = raw[BLOCK - RIM :].astype(F32)
@@ -130,7 +130,8 @@
         run = run * jnp.exp(gain) + part_ref[s, :, :PART]
 
 
-def diag_kernel(xc_ref, c_ref, bt_ref, rows_ref, cols_ref, skip_ref, y_ref):
+def diag_kernel(xc_ref, c_ref, bt_ref, rows_ref, skip_ref, y_ref):
+    cs_t = rows_ref[:HEADS].T
     half = BLOCK // 2
     xc = xc_ref[...]
     scores = jnp.dot(c_ref[...], bt_ref[...], preferred_element_type=F32)
@@ -143,7 +144,7 @@
             cols = slice(2 * WIDTH * pair, 2 * WIDTH * (pair + 1))
             outs = []
             for h in (2 * pair, 2 * pair + 1):
-                gap = cols_ref[low : low + half, h : h + 1] - rows_ref[h : h + 1, :width]
+                gap = cs_t[low : low + half, h : h + 1] - rows_ref[h : h + 1, :width]
                 spread = jnp.exp(jnp.where(keep, gap, -1e30))
                 m = (part * spread * rows_ref[8 + h : 9 + h, :width]).astype(BF16)
                 outs.append(jnp.dot(m, xc[:width, cols], preferred_element_type=F32))
@@ -153,7 +154,7 @@
             )
 
 
-def join_kernel(yd_ref, c_ref, cols_ref, local_ref, in_ref, y_ref, entry):
+def join_kernel(diag_ref, c_ref, rows_ref, local_ref, in_ref, y_ref, entry):
     @pl.when(pl.program_id(0) == 0)
     def _():
         for i in range(STATE // 8):
@@ -163,11 +164,13 @@
 
     hb = (entry[...] * jnp.exp(local_ref[0, STATE : STATE + 1]) + local_ref[0, :STATE]).astype(BF16)
     off = jnp.dot(c_ref[...], hb, preferred_element_type=F32)
+    grow = jnp.exp(rows_ref[:HEADS]).T
+
     for pair in range(HEADS // 2):
         cols = slice(2 * WIDTH * pair, 2 * WIDTH * (pair + 1))
-        h = 8 + 2 * pair
-        scale = lane_pair(cols_ref[:, h : h + 1], cols_ref[:, h + 1 : h + 2], (BLOCK, 2 * WIDTH))
-        y_ref[:, cols] = (yd_ref[:, cols] + off[:, cols] * scale).astype(BF16)
+        h = 2 * pair
+        scale = lane_pair(grow[:, h : h + 1], grow[:, h + 1 : h + 2], (BLOCK, 2 * WIDTH))
+        y_ref[:, cols] = (diag_ref[:, cols] + off[:, cols] * scale).astype(BF16)
 
 
 def gate_kernel(z_ref, out_ref):
@@ -191,18 +194,6 @@
 def shift(value, axis, by):
     count = lax.axis_size(axis)
     return lax.ppermute(value, axis, [(i, i + by) for i in range(count - by)])
-
-
-def entering(parts):
-    count, height, _ = parts.shape
-    got = lax.all_to_all(parts, "ctx", 0, 0, tiled=True)
-    before = pl.pallas_call(
-        scan_kernel,
-        out_shape=jax.ShapeDtypeStruct((count, height, PART), F32),
-        compiler_params=WHOLE,
-        name="scan",
-    )(got)
-    return lax.all_to_all(before, "ctx", 0, 0, tiled=True)
 
 
 def held(value):
@@ -250,7 +241,7 @@
     x_seg = first[:, :rows].reshape(seg, LANES)
     dt_seg = first[:, rows:, :rows].transpose(1, 0, 2).reshape(heads, seg)
     par = jnp.stack([dt_bias, a_log])[:, :, None]
-    par = jnp.broadcast_to(par, (2, heads, BLOCK))
+    par = jnp.broadcast_to(par, (2, heads, seg))
     bc_rim = shift(gathered[seg - RIM :], "ctx", 1)
     c_mat, b_t = pl.pallas_call(
         prep_kernel,
@@ -268,7 +259,7 @@
         name="prep",
     )(gathered, bc_rim, conv_bc, bias_bc[None, :])
     pieces = (STATE // 8) * (LANES // PART)
-    xc, local, parts, row_tab, col_tab = pl.pallas_call(
+    xc, local, parts, row_tab = pl.pallas_call(
         state_kernel,
         grid=(nblk,),
         in_specs=[
@@ -277,30 +268,35 @@
             full((4, LANES)),
             full((1, LANES)),
             lanes_of(STATE),
-            lanes_of(heads),
+            full(dt_seg.shape),
             full(par.shape),
         ],
         out_specs=[
             rows_of(LANES),
             pl.BlockSpec((1, STATE + 8, LANES), lambda k: (k, 0, 0)),
             full((pieces, 8, PART + 128)),
-            lanes_of(2 * heads),
-            rows_of(2 * heads),
+            full((2 * heads, seg)),
         ],
         out_shape=[
             pltpu.HBM((seg, LANES), BF16),
             pltpu.HBM((nblk, STATE + 8, LANES), F32),
             jax.ShapeDtypeStruct((pieces, 8, PART + 128), F32),
             pltpu.HBM((2 * heads, seg), F32),
-            pltpu.HBM((seg, 2 * heads), F32),
         ],
         scratch_shapes=[pltpu.VMEM((RIM, LANES), F32), pltpu.VMEM((STATE + 8, LANES), F32)],
         compiler_params=PARAMS,
         name="state",
     )(x_seg, first[groups - 1, rows:], conv_x, bias_x[None, :], held(b_t), dt_seg, par)
-    c_mat, b_t, xc, local, row_tab, col_tab = [held(v) for v in (c_mat, b_t, xc, local, row_tab, col_tab)]
-    incoming = entering(parts)
+    c_mat, b_t, local, row_tab = [held(v) for v in (c_mat, b_t, local, row_tab)]
     skip = jnp.repeat(d_skip, WIDTH)[None, :]
+    got = lax.all_to_all(parts, "ctx", 0, 0, tiled=True)
+    before = pl.pallas_call(
+        scan_kernel,
+        out_shape=jax.ShapeDtypeStruct((pieces, 8, PART), F32),
+        compiler_params=WHOLE,
+        name="scan",
+    )(got)
+    incoming = lax.all_to_all(before, "ctx", 0, 0, tiled=True)
     y_diag = pl.pallas_call(
         diag_kernel,
         grid=(nblk,),
@@ -309,30 +305,29 @@
             rows_of(STATE),
             lanes_of(STATE),
             lanes_of(2 * heads),
-            rows_of(2 * heads),
             full((1, LANES)),
         ],
         out_specs=rows_of(LANES),
         out_shape=pltpu.HBM((seg, LANES), F32),
         compiler_params=PARAMS,
         name="diag",
-    )(xc, c_mat, b_t, row_tab, col_tab, skip)
+    )(held(xc), c_mat, b_t, row_tab, skip)
     y = pl.pallas_call(
         join_kernel,
         grid=(nblk,),
         in_specs=[
             rows_of(LANES),
             rows_of(STATE),
-            rows_of(2 * heads),
+            lanes_of(2 * heads),
             pl.BlockSpec((1, STATE + 8, LANES), lambda k: (k, 0, 0)),
             full((pieces, 8, PART)),
         ],
         out_specs=rows_of(LANES),
-        out_shape=jax.ShapeDtypeStruct((seg, LANES), BF16),
+        out_shape=pltpu.HBM((seg, LANES), BF16),
         scratch_shapes=[pltpu.VMEM((STATE, LANES), F32)],
         compiler_params=PARAMS,
         name="join",
-    )(held(y_diag), c_mat, col_tab, local, incoming)
+    )(held(y_diag), c_mat, row_tab, local, incoming)
     y_tok = exchange(y.reshape(groups, rows, LANES))
     step = 32
     gate = pl.pallas_call(

time: 260 us -> 259 us (level)
  no operation moved by 1% of the time
where the time goes in v6:
time: 259 us; the launch traced here: 257 us
  waiting for transfers between devices  139 us (54%)
  blocking collectives  56.8 us (22%)
  Pallas kernels  30.9 us (12%)
  starting transfers between devices  25.6 us (10%)
  local copies, waits for them, and re-layouts  5.31 us (2%)
    all_to_all x2, waiting for transfers between devices, exchange(): lax.all_to_all(value.transpose(1, 0, 2), 'head', 1, 1, tiled=True)  133 us
    all_gather x1, blocking collectives, per_device(): gathered = lax.all_gather(bc_in, 'head', axis=0, tiled=True)  40.4 us
    all_to_all x2, starting transfers between devices, exchange(): lax.all_to_all(value.transpose(1, 0, 2), 'head', 1, 1, tiled=True)  16.6 us
    all_to_all x1, blocking collectives, per_device(): got = lax.all_to_all(parts, 'ctx', 0, 0, tiled=True)  16.3 us
    pallas_call x1, Pallas kernels, per_device(): pl.pallas_call(state_kernel, grid=(nblk,), in_specs=[rows_of(LANES), full...  7.24 us
    pallas_call x1, Pallas kernels, per_device(): pl.pallas_call(diag_kernel, grid=(nblk,), in_specs=[rows_of(LANES), rows_...  7.15 us
    pallas_call x1, Pallas kernels, per_device(): pl.pallas_call(join_kernel, grid=(nblk,), in_specs=[rows_of(LANES), rows_...  6.77 us
  transfers between devices with their start and end apart: 5, of which 4 were waited for; matrix products, arithmetic and copies ran while one was open for 0% of the time, Pallas kernels for 4%

profile of v6, /device:TPU:2, one launch (start us, length us, event | category | flops | bytes accessed | tf_op | source)
XLA Modules:
  0.0 257.3 jit_solution(633802169618643041)
XLA Ops:
  0.0 0.9 slice.15
  0.9 1.9 collective-permute-start
  2.8 40.4 %all_gather.3.g_ref = bf16[1536,256]{1,0:T(8,128)(2,1)S(1)} all-gather(bf16[96,256]{1,0:T(8,128)(2,1)} %param.14), channel_id=1, replica_groups=mesh['ctx'=32,'head'=16] {'head'}, dimensions={0}, use_global_device_ids=true | all-gather | bytes 835584 | tf_op jit(solution)/shard_map/all_gather | solution.py:232
  43.3 0.0 collective-permute-done.tail_ref
  43.3 0.0 copy-start
  43.3 1.4 copy-done
  44.7 0.0 copy-start.3
  44.7 0.7 copy-done.3
  45.4 1.3 pack.1
  46.8 0.0 copy-start.9
  46.8 0.0 copy-start.10
  46.8 0.0 copy-start.5
  46.8 0.0 copy-start.7
  46.8 7.1 %all-to-all-start = ((bf16[104,16,512]{2,0,1:T(8,128)(2,1)}), bf16[104,16,512]{2,0,1:T(8,128)(2,1)S(1)}, u32[]{:S(2)}, u32[]{:S(2)}) async-start(bf16[104,16,512]{2,0,1:T(8,128)(2,1)} %bitcast), calls=%async_computation | async-start | bytes 3407872 | tf_op jit(solution)/shard_map/all_to_all | solution.py:229
  53.9 1.9 collective-permute-start.1
  55.9 0.0 copy-done.9
  55.9 0.0 copy-done.10
  55.9 5.1 %collective-permute-done.1.rim_ref = bf16[8,256]{1,0:T(8,128)(2,1)S(1)} collective-permute-done((bf16[8,256]{1,0:T(8,128)(2,1)S(1)}, bf16[8,256]{1,0:T(8,128)(2,1)S(1)}, u32[]{:S(2)}, u32[]{:S(2)}) %collective-permute-start.1) | collective-permute-done | bytes 4128 | tf_op jit(solution)/shard_map/ppermute | solution.py:196
  61.0 0.0 copy-done.5
  61.0 0.0 copy-done.7
  61.0 3.3 %prep.1 = (bf16[1536,128]{1,0:T(8,128)(2,1)}, bf16[128,1536]{1,0:T(8,128)(2,1)}) custom-call(bf16[1536,256]{1,0:T(8,128)(2,1)S(1)} %all_gather.3.g_ref, bf16[8,256]{1,0:T(8,128)(2,1)S(1)} %collective-permute-done.1.rim_ref, f32[4,256]{1,0:T(4,128)S(1)} %copy-done.5, f32[1,256]{1,0:T(1,128)S(1)} %bitcast.19), custom_call_target="tpu_custom_call" | custom-call | tf_op jit(solution)/shard_map/prep/pallas_call | solution.py:246
  64.2 60.4 %all-to-all-done = bf16[104,16,512]{2,0,1:T(8,128)(2,1)S(1)} async-done(((bf16[104,16,512]{2,0,1:T(8,128)(2,1)}), bf16[104,16,512]{2,0,1:T(8,128)(2,1)S(1)}, u32[]{:S(2)}, u32[]{:S(2)}) %all-to-all-start) | async-done | bytes 1703968 | tf_op jit(solution)/shard_map/all_to_all | solution.py:229
  124.7 0.0 copy-start.4
  124.7 0.0 copy-start.6
  124.7 0.1 slice.20
  124.9 0.1 reshape.11.dt_ref
  125.0 0.1 broadcast_in_dim.20.par_ref
  125.1 0.3 copy-done.4
  125.4 0.0 copy-done.6
  125.4 0.0 copy-start.8
  125.4 7.2 %state.1 = (bf16[1536,512]{1,0:T(8,128)(2,1)}, f32[6,136,512]{2,1,0:T(8,128)}, f32[32,8,384]{2,1,0:T(8,128)S(1)}, f32[16,1536]{1,0:T(8,128)}) custom-call(bf16[1536,512]{1,0:T(8,128)(2,1)S(1)} %bitcast.16, bf16[8,512]{1,0:T(8,128)(2,1)S(1)} %slice_bitcast_fusion.1.spare_ref, f32[4,512]{1,0:T(4,128)S(1)} %copy-done.4, f32[1,512]{1,0:T(1,128)S(1)} %bitcast.18, ...), custom_call_target="tpu_custom_call" | custom-call | tf_op jit(solution)/shard_map/state/pallas_call | solution.py:262
  132.6 16.3 %all_to_all.20.part_ref = f32[32,8,384]{2,1,0:T(8,128)S(1)} all-to-all(f32[32,8,384]{2,1,0:T(8,128)S(1)} %get-tuple-element.20), channel_id=1, replica_groups=mesh['ctx'=32,'head'=16] {'ctx'}, dimensions={0} | all-to-all | bytes 786432 | tf_op jit(solution)/shard_map/all_to_all | solution.py:292
  149.0 0.8 scan.1
  149.8 5.1 %all-to-all-start.2 = ((f32[32,8,256]{2,1,0:T(8,128)}), f32[32,8,256]{2,1,0:T(8,128)S(1)}, u32[]{:S(2)}, u32[]{:S(2)}) async-start(f32[32,8,256]{2,1,0:T(8,128)} %scan.1), calls=%async_computation.2 | async-start | bytes 524288 | tf_op jit(solution)/shard_map/all_to_all | solution.py:299
  154.9 0.0 copy-done.8
  154.9 0.1 broadcast_in_dim.21
  155.0 0.1 broadcast_in_dim_reshape.3.skip_ref
  155.1 7.2 %diag.1.diag_ref = f32[1536,512]{1,0:T(8,128)} custom-call(bf16[1536,512]{1,0:T(8,128)(2,1)} %get-tuple-element.16.xc_ref, bf16[1536,128]{1,0:T(8,128)(2,1)} %get-tuple-element.17.c_ref, bf16[128,1536]{1,0:T(8,128)(2,1)} %get-tuple-element.15.bt_ref, f32[16,1536]{1,0:T(8,128)} %get-tuple-element.18.rows_ref, f32[1,512]{1,0:T(1,128)S(1)} %broadcast_in_dim_reshape.3.skip_ref), custom_call_target="tpu_custom_call" | custom-call | tf_op jit(solution)/shard_map/diag/pallas_call | solution.py:300
  162.2 0.4 all-to-all-done.2.in_ref
  162.6 6.8 %join.1 = bf16[1536,512]{1,0:T(8,128)(2,1)} custom-call(f32[1536,512]{1,0:T(8,128)} %diag.1.diag_ref, bf16[1536,128]{1,0:T(8,128)(2,1)} %get-tuple-element.17.c_ref, f32[16,1536]{1,0:T(8,128)} %get-tuple-element.18.rows_ref, f32[6,136,512]{2,1,0:T(8,128)} %get-tuple-element.19.local_ref, f32[32,8,256]{2,1,0:T(8,128)S(1)} %all-to-all-done.2.in_ref), custom_call_target="tpu_custom_call" | custom-call | tf_op jit(solution)/shard_map/join/pallas_call | solution.py:315
  169.4 9.4 %all-to-all-start.3 = ((bf16[96,16,512]{2,0,1:T(8,128)(2,1)}), bf16[96,16,512]{2,0,1:T(8,128)(2,1)}, u32[]{:S(2)}, u32[]{:S(2)}) async-start(bf16[96,16,512]{2,0,1:T(8,128)(2,1)} %bitcast.23), calls=%async_computation.3 | async-start | bytes 3145728 | tf_op jit(solution)/shard_map/all_to_all | solution.py:229
  178.9 0.0 copy-start.1
  178.9 1.4 copy-done.1
  180.3 0.0 copy-start.2
  180.3 0.6 gate.1.gate_ref
  180.8 72.7 %all-to-all-done.3 = bf16[96,16,512]{2,0,1:T(8,128)(2,1)} async-done(((bf16[96,16,512]{2,0,1:T(8,128)(2,1)}), bf16[96,16,512]{2,0,1:T(8,128)(2,1)}, u32[]{:S(2)}, u32[]{:S(2)}) %all-to-all-start.3) | async-done | bytes 1572896 | tf_op jit(solution)/shard_map/all_to_all | solution.py:229
  253.5 0.0 copy-done.2
  253.5 3.8 %norm.1 = bf16[96,8192]{1,0:T(8,128)(2,1)} custom-call(bf16[16,96,512]{2,1,0:T(8,128)(2,1)} %bitcast.11.y_ref, f32[96,8192]{1,0:T(8,128)S(1)} %gate.1.gate_ref, f32[1,8192]{1,0:T(1,128)S(1)} %bitcast.17), custom_call_target="tpu_custom_call" | custom-call | tf_op jit(solution)/shard_map/norm/pallas_call | solution.py:342
  (5 shorter events, 0.0 us)
Async XLA Ops:
  0.9 42.4 %collective-permute-start = (bf16[8,8192]{1,0:T(8,128)(2,1)S(1)}, bf16[8,8192]{1,0:T(8,128)(2,1)S(1)}, u32[]{:S(2)}, u32[]{:S(2)}) collective-permute-start(bf16[8,8192]{1,0:T(8,128)(2,1)S(1)} %slice.15), channel_id=1, source_target_pairs={{0,16},{16,32},{32,48},{48,64},{64,80},{80,96},{96,112},{112,128},... | collective-permute-start | bytes 393224 | tf_op jit(solution)/shard_map/ppermute | solution.py:196
  43.3 1.4 copy-start
  44.7 0.7 copy-start.3
  46.8 9.1 %copy-start.9 = (f32[8]{0:T(128)S(1)}, f32[8]{0:T(128)}, u32[]{:S(2)}) copy-start(f32[8]{0:T(128)} %param.21) | copy-start | bytes 100
  46.8 9.1 %copy-start.10 = (f32[8]{0:T(128)S(1)}, f32[8]{0:T(128)}, u32[]{:S(2)}) copy-start(f32[8]{0:T(128)} %param.20) | copy-start | bytes 100
  46.8 14.2 %copy-start.5 = (f32[4,256]{1,0:T(4,128)S(1)}, f32[4,256]{1,0:T(4,128)}, u32[]{:S(2)}) copy-start(f32[4,256]{1,0:T(4,128)} %taps_ref.2) | copy-start | bytes 12292
  46.8 14.2 %copy-start.7 = (f32[256]{0:T(256)S(1)}, f32[256]{0:T(256)}, u32[]{:S(2)}) copy-start(f32[256]{0:T(256)} %param.19) | copy-start | bytes 3076
  46.8 77.9 %all-to-all-start = ((bf16[104,16,512]{2,0,1:T(8,128)(2,1)}), bf16[104,16,512]{2,0,1:T(8,128)(2,1)S(1)}, u32[]{:S(2)}, u32[]{:S(2)}) async-start(bf16[104,16,512]{2,0,1:T(8,128)(2,1)} %bitcast), calls=%async_computation | async-start | bytes 3407872 | tf_op jit(solution)/shard_map/all_to_all | solution.py:229
  53.9 7.0 %collective-permute-start.1 = (bf16[8,256]{1,0:T(8,128)(2,1)S(1)}, bf16[8,256]{1,0:T(8,128)(2,1)S(1)}, u32[]{:S(2)}, u32[]{:S(2)}) collective-permute-start(bf16[8,256]{1,0:T(8,128)(2,1)S(1)} %slice.18), channel_id=1, source_target_pairs={{0,16},{16,32},{32,48},{48,64},{64,80},{80,96},{96,112},{112,128},... | collective-permute-start | bytes 12296 | tf_op jit(solution)/shard_map/ppermute | solution.py:196
  124.7 0.7 copy-start.4
  124.7 0.7 copy-start.6
  125.4 29.5 %copy-start.8 = (f32[8]{0:T(128)S(1)}, f32[8]{0:T(128)}, u32[]{:S(2)}) copy-start(f32[8]{0:T(128)} %param.22) | copy-start | bytes 100
  149.8 12.9 %all-to-all-start.2 = ((f32[32,8,256]{2,1,0:T(8,128)}), f32[32,8,256]{2,1,0:T(8,128)S(1)}, u32[]{:S(2)}, u32[]{:S(2)}) async-start(f32[32,8,256]{2,1,0:T(8,128)} %scan.1), calls=%async_computation.2 | async-start | bytes 524288 | tf_op jit(solution)/shard_map/all_to_all | solution.py:299
  169.4 84.1 %all-to-all-start.3 = ((bf16[96,16,512]{2,0,1:T(8,128)(2,1)}), bf16[96,16,512]{2,0,1:T(8,128)(2,1)}, u32[]{:S(2)}, u32[]{:S(2)}) async-start(bf16[96,16,512]{2,0,1:T(8,128)(2,1)} %bitcast.23), calls=%async_computation.3 | async-start | bytes 3145728 | tf_op jit(solution)/shard_map/all_to_all | solution.py:229
  178.9 1.4 copy-start.1
  180.3 73.3 %copy-start.2 = (f32[8192]{0:T(1024)S(1)}, f32[8192]{0:T(1024)}, u32[]{:S(2)}) copy-start(f32[8192]{0:T(1024)} %param.23) | copy-start | bytes 98308

commit v7 on v6

--- a/solution.py
+++ b/solution.py
@@ -12,6 +12,7 @@
 LANES = HEADS * WIDTH
 PART = 256
 RIM = 8
+TWO = 2
 F32 = jnp.float32
 BF16 = jnp.bfloat16
 
@@ -89,26 +90,29 @@
         run[...] = jnp.zeros_like(run)
         rows_ref[:HEADS], rows_ref[HEADS:] = step_tables(dt_ref[...], par_ref)
 
-    here = pl.ds(pl.multiple_of(BLOCK * pl.program_id(0), BLOCK), BLOCK)
-    cs = rows_ref[:HEADS, here]
-    weight = jnp.exp(cs[:, BLOCK - 1 :] - cs) * rows_ref[HEADS:, here]
     raw = x_ref[...]
-    xc = causal_conv(carry[...], raw, taps_ref[...], bias_ref[...])
-    carry[...] = raw[BLOCK - RIM :].astype(F32)
-    xc_ref[...] = xc
-    local_ref[0] = run[...]
-    bt = bt_ref[...].astype(F32)
-    for pair in range(HEADS // 2):
-        cols = slice(2 * WIDTH * pair, 2 * WIDTH * (pair + 1))
-        parts, tots = [], []
-        for h in (2 * pair, 2 * pair + 1):
-            bw = (bt * weight[h : h + 1]).astype(BF16)
-            parts.append(jnp.dot(bw, xc[:, cols], preferred_element_type=F32))
-            tots.append(cs[h : h + 1, BLOCK - 1 :])
-        tot = lane_pair(tots[0], tots[1], (1, 2 * WIDTH))
-        st = lane_pair(parts[0], parts[1], (STATE, 2 * WIDTH))
-        run[:STATE, cols] = run[:STATE, cols] * jnp.exp(tot) + st
-        run[STATE:, cols] = run[STATE:, cols] + tot
+    xc_all = causal_conv(carry[...], raw, taps_ref[...], bias_ref[...])
+    carry[...] = raw[TWO * BLOCK - RIM :].astype(F32)
+    xc_ref[...] = xc_all
+    for sub in range(TWO):
+        here = pl.ds(pl.multiple_of(BLOCK * (TWO * pl.program_id(0) + sub), BLOCK), BLOCK)
+        inside = slice(BLOCK * sub, BLOCK * (sub + 1))
+        cs = rows_ref[:HEADS, here]
+        weight = jnp.exp(cs[:, BLOCK - 1 :] - cs) * rows_ref[HEADS:, here]
+        xc = xc_all[inside]
+        local_ref[sub] = run[...]
+        bt = bt_ref[:, inside].astype(F32)
+        for pair in range(HEADS // 2):
+            cols = slice(2 * WIDTH * pair, 2 * WIDTH * (pair + 1))
+            parts, tots = [], []
+            for h in (2 * pair, 2 * pair + 1):
+                bw = (bt * weight[h : h + 1]).astype(BF16)
+                parts.append(jnp.dot(bw, xc[:, cols], preferred_element_type=F32))
+                tots.append(cs[h : h + 1, BLOCK - 1 :])
+            tot = lane_pair(tots[0], tots[1], (1, 2 * WIDTH))
+            st = lane_pair(parts[0], parts[1], (STATE, 2 * WIDTH))
+            run[:STATE, cols] = run[:STATE, cols] * jnp.exp(tot) + st
+            run[STATE:, cols] = run[STATE:, cols] + tot
 
     @pl.when(pl.program_id(0) == pl.num_programs(0) - 1)
     def _():
@@ -162,15 +166,16 @@
                 piece = in_ref[i * (LANES // PART) + j]
                 entry[8 * i : 8 * (i + 1), PART * j : PART * (j + 1)] = piece
 
-    hb = (entry[...] * jnp.exp(local_ref[0, STATE : STATE + 1]) + local_ref[0, :STATE]).astype(BF16)
-    off = jnp.dot(c_ref[...], hb, preferred_element_type=F32)
-    grow = jnp.exp(rows_ref[:HEADS]).T
-
-    for pair in range(HEADS // 2):
-        cols = slice(2 * WIDTH * pair, 2 * WIDTH * (pair + 1))
-        h = 2 * pair
-        scale = lane_pair(grow[:, h : h + 1], grow[:, h + 1 : h + 2], (BLOCK, 2 * WIDTH))
-        y_ref[:, cols] = (diag_ref[:, cols] + off[:, cols] * scale).astype(BF16)
+    for sub in range(TWO):
+        inside = slice(BLOCK * sub, BLOCK * (sub + 1))
+        hb = (entry[...] * jnp.exp(local_ref[sub, STATE : STATE + 1]) + local_ref[sub, :STATE]).astype(BF16)
+        off = jnp.dot(c_ref[inside], hb, preferred_element_type=F32)
+        grow = jnp.exp(rows_ref[:HEADS, inside]).T
+        for pair in range(HEADS // 2):
+            cols = slice(2 * WIDTH * pair, 2 * WIDTH * (pair + 1))
+            h = 2 * pair
+            scale = lane_pair(grow[:, h : h + 1], grow[:, h + 1 : h + 2], (BLOCK, 2 * WIDTH))
+            y_ref[inside, cols] = (diag_ref[inside, cols] + off[:, cols] * scale).astype(BF16)
 
 
 def gate_kernel(z_ref, out_ref):
@@ -204,12 +209,12 @@
     return pl.BlockSpec(shape, lambda k: tuple(0 for _ in shape))
 
 
-def rows_of(width):
-    return pl.BlockSpec((BLOCK, width), lambda k: (k, 0))
-
-
-def lanes_of(height):
-    return pl.BlockSpec((height, BLOCK), lambda k: (0, k))
+def rows_of(width, blocks=1):
+    return pl.BlockSpec((blocks * BLOCK, width), lambda k: (k, 0))
+
+
+def lanes_of(height, blocks=1):
+    return pl.BlockSpec((height, blocks * BLOCK), lambda k: (0, k))
 
 
 WHOLE = pltpu.CompilerParams(vmem_limit_bytes=16 << 20)
@@ -261,19 +266,19 @@
     pieces = (STATE // 8) * (LANES // PART)
     xc, local, parts, row_tab = pl.pallas_call(
         state_kernel,
-        grid=(nblk,),
-        in_specs=[
-            rows_of(LANES),
+        grid=(nblk // TWO,),
+        in_specs=[
+            rows_of(LANES, TWO),
             full((RIM, LANES)),
             full((4, LANES)),
             full((1, LANES)),
-            lanes_of(STATE),
+            lanes_of(STATE, TWO),
             full(dt_seg.shape),
             full(par.shape),
         ],
         out_specs=[
-            rows_of(LANES),
-            pl.BlockSpec((1, STATE + 8, LANES), lambda k: (k, 0, 0)),
+            rows_of(LANES, TWO),
+            pl.BlockSpec((TWO, STATE + 8, LANES), lambda k: (k, 0, 0)),
             full((pieces, 8, PART + 128)),
             full((2 * heads, seg)),
         ],
@@ -314,15 +319,15 @@
     )(held(xc), c_mat, b_t, row_tab, skip)
     y = pl.pallas_call(
         join_kernel,
-        grid=(nblk,),
-        in_specs=[
-            rows_of(LANES),
-            rows_of(STATE),
-            lanes_of(2 * heads),
-            pl.BlockSpec((1, STATE + 8, LANES), lambda k: (k, 0, 0)),
+        grid=(nblk // TWO,),
+        in_specs=[
+            rows_of(LANES, TWO),
+            rows_of(STATE, TWO),
+            lanes_of(2 * heads, TWO),
+            pl.BlockSpec((TWO, STATE + 8, LANES), lambda k: (k, 0, 0)),
             full((pieces, 8, PART)),
         ],
-        out_specs=rows_of(LANES),
+        out_specs=rows_of(LANES, TWO),
         out_shape=pltpu.HBM((seg, LANES), BF16),
         scratch_shapes=[pltpu.VMEM((STATE, LANES), F32)],
         compiler_params=PARAMS,

time: 259 us -> 256 us (0.988)
  no operation moved by 1% of the time
where the time goes in v7:
time: 256 us
  waiting for transfers between devices  139 us (54%)
  blocking collectives  56.8 us (22%)
  Pallas kernels  29.2 us (11%)
  starting transfers between devices  25.6 us (10%)
  local copies, waits for them, and re-layouts  5.31 us (2%)
    all_to_all x2, waiting for transfers between devices, exchange(): lax.all_to_all(value.transpose(1, 0, 2), 'head', 1, 1, tiled=True)  133 us
    all_gather x1, blocking collectives, per_device(): gathered = lax.all_gather(bc_in, 'head', axis=0, tiled=True)  40.4 us
    all_to_all x2, starting transfers between devices, exchange(): lax.all_to_all(value.transpose(1, 0, 2), 'head', 1, 1, tiled=True)  16.6 us
    all_to_all x1, blocking collectives, per_device(): got = lax.all_to_all(parts, 'ctx', 0, 0, tiled=True)  16.3 us
    pallas_call x1, Pallas kernels, per_device(): pl.pallas_call(diag_kernel, grid=(nblk,), in_specs=[rows_of(LANES), rows_...  7.15 us
    pallas_call x1, Pallas kernels, per_device(): pl.pallas_call(state_kernel, grid=(nblk // TWO,), in_specs=[rows_of(LANES...  6.68 us
    pallas_call x1, Pallas kernels, per_device(): pl.pallas_call(join_kernel, grid=(nblk // TWO,), in_specs=[rows_of(LANES,...  5.63 us
    all_to_all x1, starting transfers between devices, per_device(): incoming = lax.all_to_all(before, 'ctx', 0, 0, tiled=True)  5.12 us
  transfers between devices with their start and end apart: 5, of which 4 were waited for; matrix products, arithmetic and copies ran while one was open for 0% of the time, Pallas kernels for 4%

profile of v7, /device:TPU:2, one launch (start us, length us, event | category | flops | bytes accessed | tf_op | source)
XLA Modules:
  0.0 255.6 jit_solution(16620559799372627719)
XLA Ops:
  0.0 0.9 slice.15
  0.9 1.9 collective-permute-start
  2.8 40.4 %all_gather.3.g_ref = bf16[1536,256]{1,0:T(8,128)(2,1)S(1)} all-gather(bf16[96,256]{1,0:T(8,128)(2,1)} %param.14), channel_id=1, replica_groups=mesh['ctx'=32,'head'=16] {'head'}, dimensions={0}, use_global_device_ids=true | all-gather | bytes 835584 | tf_op jit(solution)/shard_map/all_gather | solution.py:237
  43.3 0.0 collective-permute-done.tail_ref
  43.3 0.0 copy-start
  43.3 1.4 copy-done
  44.7 0.0 copy-start.3
  44.7 0.7 copy-done.3
  45.4 1.3 pack.1
  46.8 0.0 copy-start.9
  46.8 0.0 copy-start.10
  46.8 0.0 copy-start.5
  46.8 0.0 copy-start.7
  46.8 7.1 %all-to-all-start = ((bf16[104,16,512]{2,0,1:T(8,128)(2,1)}), bf16[104,16,512]{2,0,1:T(8,128)(2,1)S(1)}, u32[]{:S(2)}, u32[]{:S(2)}) async-start(bf16[104,16,512]{2,0,1:T(8,128)(2,1)} %bitcast), calls=%async_computation | async-start | bytes 3407872 | tf_op jit(solution)/shard_map/all_to_all | solution.py:234
  53.9 1.9 collective-permute-start.1
  55.9 0.0 copy-done.9
  55.9 0.0 copy-done.10
  55.9 5.1 %collective-permute-done.1.rim_ref = bf16[8,256]{1,0:T(8,128)(2,1)S(1)} collective-permute-done((bf16[8,256]{1,0:T(8,128)(2,1)S(1)}, bf16[8,256]{1,0:T(8,128)(2,1)S(1)}, u32[]{:S(2)}, u32[]{:S(2)}) %collective-permute-start.1) | collective-permute-done | bytes 4128 | tf_op jit(solution)/shard_map/ppermute | solution.py:201
  61.0 0.0 copy-done.5
  61.0 0.0 copy-done.7
  61.0 3.3 %prep.1 = (bf16[1536,128]{1,0:T(8,128)(2,1)}, bf16[128,1536]{1,0:T(8,128)(2,1)}) custom-call(bf16[1536,256]{1,0:T(8,128)(2,1)S(1)} %all_gather.3.g_ref, bf16[8,256]{1,0:T(8,128)(2,1)S(1)} %collective-permute-done.1.rim_ref, f32[4,256]{1,0:T(4,128)S(1)} %copy-done.5, f32[1,256]{1,0:T(1,128)S(1)} %bitcast.19), custom_call_target="tpu_custom_call" | custom-call | tf_op jit(solution)/shard_map/prep/pallas_call | solution.py:251
  64.2 60.4 %all-to-all-done = bf16[104,16,512]{2,0,1:T(8,128)(2,1)S(1)} async-done(((bf16[104,16,512]{2,0,1:T(8,128)(2,1)}), bf16[104,16,512]{2,0,1:T(8,128)(2,1)S(1)}, u32[]{:S(2)}, u32[]{:S(2)}) %all-to-all-start) | async-done | bytes 1703968 | tf_op jit(solution)/shard_map/all_to_all | solution.py:234
  124.7 0.0 copy-start.4
  124.7 0.0 copy-start.6
  124.7 0.1 slice.20
  124.9 0.1 reshape.11.dt_ref
  125.0 0.1 broadcast_in_dim.20.par_ref
  125.1 0.3 copy-done.4
  125.4 0.0 copy-done.6
  125.4 0.0 copy-start.8
  125.4 6.7 %state.1 = (bf16[1536,512]{1,0:T(8,128)(2,1)}, f32[6,136,512]{2,1,0:T(8,128)}, f32[32,8,384]{2,1,0:T(8,128)S(1)}, f32[16,1536]{1,0:T(8,128)}) custom-call(bf16[1536,512]{1,0:T(8,128)(2,1)S(1)} %bitcast.16, bf16[8,512]{1,0:T(8,128)(2,1)S(1)} %slice_bitcast_fusion.1.spare_ref, f32[4,512]{1,0:T(4,128)S(1)} %copy-done.4, f32[1,512]{1,0:T(1,128)S(1)} %bitcast.18, ...), custom_call_target="tpu_custom_call" | custom-call | tf_op jit(solution)/shard_map/state/pallas_call | solution.py:267
  132.1 16.3 %all_to_all.20.part_ref = f32[32,8,384]{2,1,0:T(8,128)S(1)} all-to-all(f32[32,8,384]{2,1,0:T(8,128)S(1)} %get-tuple-element.20), channel_id=1, replica_groups=mesh['ctx'=32,'head'=16] {'ctx'}, dimensions={0} | all-to-all | bytes 786432 | tf_op jit(solution)/shard_map/all_to_all | solution.py:297
  148.4 0.8 scan.1
  149.2 5.1 %all-to-all-start.2 = ((f32[32,8,256]{2,1,0:T(8,128)}), f32[32,8,256]{2,1,0:T(8,128)S(1)}, u32[]{:S(2)}, u32[]{:S(2)}) async-start(f32[32,8,256]{2,1,0:T(8,128)} %scan.1), calls=%async_computation.2 | async-start | bytes 524288 | tf_op jit(solution)/shard_map/all_to_all | solution.py:304
  154.3 0.0 copy-done.8
  154.4 0.1 broadcast_in_dim.21
  154.4 0.1 broadcast_in_dim_reshape.3.skip_ref
  154.5 7.2 %diag.1.diag_ref = f32[1536,512]{1,0:T(8,128)} custom-call(bf16[1536,512]{1,0:T(8,128)(2,1)} %get-tuple-element.16.xc_ref, bf16[1536,128]{1,0:T(8,128)(2,1)} %get-tuple-element.17.c_ref, bf16[128,1536]{1,0:T(8,128)(2,1)} %get-tuple-element.15.bt_ref, f32[16,1536]{1,0:T(8,128)} %get-tuple-element.18.rows_ref, f32[1,512]{1,0:T(1,128)S(1)} %broadcast_in_dim_reshape.3.skip_ref), custom_call_target="tpu_custom_call" | custom-call | tf_op jit(solution)/shard_map/diag/pallas_call | solution.py:305
  161.7 0.4 all-to-all-done.2.in_ref
  162.1 5.6 %join.1 = bf16[1536,512]{1,0:T(8,128)(2,1)} custom-call(f32[1536,512]{1,0:T(8,128)} %diag.1.diag_ref, bf16[1536,128]{1,0:T(8,128)(2,1)} %get-tuple-element.17.c_ref, f32[16,1536]{1,0:T(8,128)} %get-tuple-element.18.rows_ref, f32[6,136,512]{2,1,0:T(8,128)} %get-tuple-element.19.local_ref, f32[32,8,256]{2,1,0:T(8,128)S(1)} %all-to-all-done.2.in_ref), custom_call_target="tpu_custom_call" | custom-call | tf_op jit(solution)/shard_map/join/pallas_call | solution.py:320
  167.7 9.4 %all-to-all-start.3 = ((bf16[96,16,512]{2,0,1:T(8,128)(2,1)}), bf16[96,16,512]{2,0,1:T(8,128)(2,1)}, u32[]{:S(2)}, u32[]{:S(2)}) async-start(bf16[96,16,512]{2,0,1:T(8,128)(2,1)} %bitcast.23), calls=%async_computation.3 | async-start | bytes 3145728 | tf_op jit(solution)/shard_map/all_to_all | solution.py:234
  177.1 0.0 copy-start.1
  177.2 1.4 copy-done.1
  178.6 0.0 copy-start.2
  178.6 0.6 gate.1.gate_ref
  179.1 72.7 %all-to-all-done.3 = bf16[96,16,512]{2,0,1:T(8,128)(2,1)} async-done(((bf16[96,16,512]{2,0,1:T(8,128)(2,1)}), bf16[96,16,512]{2,0,1:T(8,128)(2,1)}, u32[]{:S(2)}, u32[]{:S(2)}) %all-to-all-start.3) | async-done | bytes 1572896 | tf_op jit(solution)/shard_map/all_to_all | solution.py:234
  251.8 0.0 copy-done.2
  251.8 3.8 %norm.1 = bf16[96,8192]{1,0:T(8,128)(2,1)} custom-call(bf16[16,96,512]{2,1,0:T(8,128)(2,1)} %bitcast.11.y_ref, f32[96,8192]{1,0:T(8,128)S(1)} %gate.1.gate_ref, f32[1,8192]{1,0:T(1,128)S(1)} %bitcast.17), custom_call_target="tpu_custom_call" | custom-call | tf_op jit(solution)/shard_map/norm/pallas_call | solution.py:347
  (5 shorter events, 0.0 us)
Async XLA Ops:
  0.9 42.4 %collective-permute-start = (bf16[8,8192]{1,0:T(8,128)(2,1)S(1)}, bf16[8,8192]{1,0:T(8,128)(2,1)S(1)}, u32[]{:S(2)}, u32[]{:S(2)}) collective-permute-start(bf16[8,8192]{1,0:T(8,128)(2,1)S(1)} %slice.15), channel_id=1, source_target_pairs={{0,16},{16,32},{32,48},{48,64},{64,80},{80,96},{96,112},{112,128},... | collective-permute-start | bytes 393224 | tf_op jit(solution)/shard_map/ppermute | solution.py:201
  43.3 1.4 copy-start
  44.7 0.7 copy-start.3
  46.8 9.1 %copy-start.9 = (f32[8]{0:T(128)S(1)}, f32[8]{0:T(128)}, u32[]{:S(2)}) copy-start(f32[8]{0:T(128)} %param.21) | copy-start | bytes 100
  46.8 9.1 %copy-start.10 = (f32[8]{0:T(128)S(1)}, f32[8]{0:T(128)}, u32[]{:S(2)}) copy-start(f32[8]{0:T(128)} %param.20) | copy-start | bytes 100
  46.8 14.2 %copy-start.5 = (f32[4,256]{1,0:T(4,128)S(1)}, f32[4,256]{1,0:T(4,128)}, u32[]{:S(2)}) copy-start(f32[4,256]{1,0:T(4,128)} %taps_ref.2) | copy-start | bytes 12292
  46.8 14.2 %copy-start.7 = (f32[256]{0:T(256)S(1)}, f32[256]{0:T(256)}, u32[]{:S(2)}) copy-start(f32[256]{0:T(256)} %param.19) | copy-start | bytes 3076
  46.8 77.9 %all-to-all-start = ((bf16[104,16,512]{2,0,1:T(8,128)(2,1)}), bf16[104,16,512]{2,0,1:T(8,128)(2,1)S(1)}, u32[]{:S(2)}, u32[]{:S(2)}) async-start(bf16[104,16,512]{2,0,1:T(8,128)(2,1)} %bitcast), calls=%async_computation | async-start | bytes 3407872 | tf_op jit(solution)/shard_map/all_to_all | solution.py:234
  53.9 7.0 %collective-permute-start.1 = (bf16[8,256]{1,0:T(8,128)(2,1)S(1)}, bf16[8,256]{1,0:T(8,128)(2,1)S(1)}, u32[]{:S(2)}, u32[]{:S(2)}) collective-permute-start(bf16[8,256]{1,0:T(8,128)(2,1)S(1)} %slice.18), channel_id=1, source_target_pairs={{0,16},{16,32},{32,48},{48,64},{64,80},{80,96},{96,112},{112,128},... | collective-permute-start | bytes 12296 | tf_op jit(solution)/shard_map/ppermute | solution.py:201
  124.7 0.7 copy-start.4
  124.7 0.7 copy-start.6
  125.4 29.0 %copy-start.8 = (f32[8]{0:T(128)S(1)}, f32[8]{0:T(128)}, u32[]{:S(2)}) copy-start(f32[8]{0:T(128)} %param.22) | copy-start | bytes 100
  149.2 12.9 %all-to-all-start.2 = ((f32[32,8,256]{2,1,0:T(8,128)}), f32[32,8,256]{2,1,0:T(8,128)S(1)}, u32[]{:S(2)}, u32[]{:S(2)}) async-start(f32[32,8,256]{2,1,0:T(8,128)} %scan.1), calls=%async_computation.2 | async-start | bytes 524288 | tf_op jit(solution)/shard_map/all_to_all | solution.py:304
  167.7 84.1 %all-to-all-start.3 = ((bf16[96,16,512]{2,0,1:T(8,128)(2,1)}), bf16[96,16,512]{2,0,1:T(8,128)(2,1)}, u32[]{:S(2)}, u32[]{:S(2)}) async-start(bf16[96,16,512]{2,0,1:T(8,128)(2,1)} %bitcast.23), calls=%async_computation.3 | async-start | bytes 3145728 | tf_op jit(solution)/shard_map/all_to_all | solution.py:234
  177.1 1.4 copy-start.1
  178.6 73.3 %copy-start.2 = (f32[8192]{0:T(1024)S(1)}, f32[8192]{0:T(1024)}, u32[]{:S(2)}) copy-start(f32[8192]{0:T(1024)} %param.23) | copy-start | bytes 98308
